TPU v7x, 128 devices: a whole 4x4x4 slice. The times are simulated.
128 devices in a mesh: expert: 32 (over z, x, core), width: 4 (over y).
Axes of the slice: x: 4, y: 4, z: 4, core: 2. Of those that a mesh axis runs over, the one named last changes fastest.
Arguments:
- tokens: bfloat16 [4096, 4096], P('expert'), may hold values from -6 to 6
- expert_ids: int32 [4096, 8], P('expert'), may hold values from 0 to 63, all different within a row; in each aligned block of 128 rows (0 to 127, 128 to 255, ...) at most 32 rows name the same one
- combine_weights: float32 [4096, 8], P('expert'), may hold values from 0.05 to 0.3
- gate_weight: bfloat16 [64, 4096, 1536], P('expert', None, 'width'), may hold values from -0.09375 to 0.09375
- up_weight: bfloat16 [64, 4096, 1536], P('expert', None, 'width'), may hold values from -0.09375 to 0.09375
- down_weight: bfloat16 [64, 1536, 4096], P('expert', 'width'), may hold values from -0.15625 to 0.15625
Outputs:
- mixed: bfloat16 [4096, 4096], P('expert', 'width')
Inputs may be any that keep to these rules, and one draw needn't show every extreme that they name: `expert_ids`: each token names 8 different experts. Within the tokens of one index of expert (aligned blocks of 128 tokens) no expert is named by more than 32 tokens, a bound that some block reaches.
All inputs are finite; a program needn't handle non-finite values.
Results may differ from a plain program's by a relative error of at most 0.012.
Values may be sent and summed in bfloat16 or wider, within the bound.
No kernel may reach another device: no remote copies, remote signals or barrier semaphores. Data moves between devices by JAX's collectives and lax.ppermute only.
A program may use at most 128 MiB of HBM per device.

v0:
```python
import jax
import jax.numpy as jnp
from jax import lax
from jax.sharding import PartitionSpec as P


def local(tokens, expert_ids, combine_weights, gate_weight, up_weight, down_weight):
    tok_rows = tokens.shape[0]
    top_count = expert_ids.shape[1]
    exp_local = gate_weight.shape[0]
    n_expert = lax.axis_size("expert")
    n_width = lax.axis_size("width")
    experts_all = exp_local * n_expert
    slots = 2 * tok_rows * top_count // experts_all
    width_all = tokens.shape[1]
    cols = width_all // n_width
    flat_ids = expert_ids.reshape(-1)
    onehot = (flat_ids[:, None] == jnp.arange(experts_all, dtype=jnp.int32)[None, :]).astype(
        jnp.int32
    )
    rank = jnp.sum(jnp.cumsum(onehot, axis=0) * onehot, axis=1) - 1
    slot = flat_ids * slots + rank
    token_index = jnp.arange(tok_rows * top_count, dtype=jnp.int32) // top_count
    table = jnp.full((experts_all * slots,), tok_rows, jnp.int32).at[slot].set(token_index)
    padded = jnp.concatenate([tokens, jnp.zeros((1, width_all), jnp.bfloat16)], axis=0)
    outgoing = padded[table].reshape(n_expert, exp_local, slots, width_all)
    arrived = lax.all_to_all(outgoing, "expert", split_axis=0, concat_axis=0, tiled=True)
    gate = jnp.einsum("skmd,kdf->skmf", arrived, gate_weight, preferred_element_type=jnp.float32)
    up_part = jnp.einsum("skmd,kdf->skmf", arrived, up_weight, preferred_element_type=jnp.float32)
    hidden = (jax.nn.silu(gate) * up_part).astype(jnp.bfloat16)
    partial_value = jnp.einsum(
        "skmf,kfd->skmd", hidden, down_weight, preferred_element_type=jnp.float32
    )
    reduced = lax.psum_scatter(
        partial_value.astype(jnp.bfloat16), "width", scatter_dimension=3, tiled=True
    ).astype(jnp.float32)
    returned = lax.all_to_all(
        reduced.astype(jnp.bfloat16), "expert", split_axis=0, concat_axis=0, tiled=True
    ).astype(reduced.dtype)
    picked = returned.reshape(experts_all * slots, cols)[slot].reshape(tok_rows, top_count, cols)
    mixed = jnp.sum(combine_weights[:, :, None] * picked, axis=1)
    return mixed.astype(jnp.bfloat16)


def solution(mesh):
    placed = (
        P("expert", None),
        P("expert", None),
        P("expert", None),
        P("expert", None, "width"),
        P("expert", None, "width"),
        P("expert", "width", None),
    )
    return jax.shard_map(
        local, mesh=mesh, in_specs=placed, out_specs=P("expert", "width"), check_vma=False
    )
```

profile of v0, /device:TPU:0, one launch (start us, length us, event | category | flops | bytes accessed | tf_op | source)
XLA Modules:
  0.0 527.5 jit_solution(2398592450466023220)
XLA Ops:
  6.5 0.8 copy.18
  7.3 0.1 eq.29
  7.5 0.7 broadcast_multiply_fusion
  8.2 18.0 %reduce-window.6 = s32[64,8,128]{2,1,0:T(8,128)S(1)} reduce-window(s32[64,8,128]{2,1,0:T(8,128)S(1)} %fusion.23, s32[]{:T(128)} %constant.33.clone.1), window={size=1x1x128 pad=0_0x0_0x127_0}, to_apply=%region_0.0 | reduce-window | flops 8323072 | bytes 524292 | tf_op jit(solution)/shard_map/reduce-window
  26.2 0.1 slice.12
  26.4 0.1 copy.20
  26.6 0.1 broadcast_add_fusion
  26.9 0.1 copy.17
  27.0 0.1 mul.37
  27.1 4.3 scatter_custom_fusion
  31.4 1.3 concatenate.3
  32.8 14.3 %gather_fusion = bf16[2048,4096]{1,0:T(8,128)(2,1)} fusion(bf16[129,4096]{1,0:T(8,128)(2,1)S(1)} %concatenate.3, s32[2048]{0:T(1024)S(1)} %fusion.24), kind=kCustom, calls=%fused_computation | custom fusion | bytes 33562624 | tf_op jit(solution)/shard_map/gather | solution.py:26
  47.1 194.1 %all_to_all.10 = bf16[32,2,32,4096]{3,2,1,0:T(8,128)(2,1)S(1)} all-to-all(bf16[32,2,32,4096]{3,2,1,0:T(8,128)(2,1)} %bitcast.66), channel_id=1, replica_groups=mesh['expert'=32,'width'=4] {'expert'}, dimensions={0} | all-to-all | bytes 33554432 | tf_op jit(solution)/shard_map/all_to_all | solution.py:27
  241.2 5.7 %copy-done = bf16[32,2,32,4096]{3,2,1,0:T(8,128)(2,1)} copy-done((bf16[32,2,32,4096]{3,2,1,0:T(8,128)(2,1)}, bf16[32,2,32,4096]{3,2,1,0:T(8,128)(2,1)S(1)}, u32[]{:S(2)}) %copy-start) | copy-done | bytes 16777240
  246.9 12.0 %fusion.2 = f32[2,32,32,384]{3,2,1,0:T(8,128)} fusion(bf16[32,2,32,4096]{3,2,1,0:T(8,128)(2,1)S(1)} %all_to_all.10, bf16[2,4096,384]{2,1,0:T(8,128)(2,1)} %param.9), kind=kOutput, calls=%fused_computation.6 | convolution fusion | flops 6442450944 | bytes 26214400 | tf_op jit(solution)/shard_map/skmd,kdf->skmf/dot_general | solution.py:28
  258.9 26.2 %convert_bitcast_fusion = bf16[32,2,32,4096]{3,2,0,1:T(8,128)(2,1)} fusion(bf16[2,384,4096]{2,1,0:T(8,128)(2,1)} %param.11, f32[2,32,32,384]{3,2,1,0:T(8,128)} %fusion.2, bf16[2,4096,384]{2,1,0:T(8,128)(2,1)} %param.10, bf16[32,2,32,4096]{3,2,1,0:T(8,128)(2,1)} %copy-done), kind=kOutput, calls=%fused_computation.3 | convolution fusion | flops 12898009088 | bytes 49283072 | tf_op jit(solution)/shard_map/skmf,kfd->skmd/dot_general | solution.py:31
  285.1 149.1 %reduce-scatter.2.cloned.1.call-done = bf16[32,2,32,1024]{3,2,0,1:T(8,128)(2,1)} async-done(((bf16[32,2,32,4096]{3,2,0,1:T(8,128)(2,1)}), bf16[32,2,32,1024]{3,2,0,1:T(8,128)(2,1)}) %reduce-scatter.2.cloned.1.call-update) | async-done | bytes 4194320 | tf_op jit(solution)/shard_map/reduce_scatter | solution.py:34
  434.2 5.0 copy.24
  439.2 7.7 %all-to-all-start.1 = ((bf16[32,2,32,1024]{3,2,1,0:T(8,128)(2,1)}), bf16[32,2,32,1024]{3,2,1,0:T(8,128)(2,1)}, u32[]{:S(2)}, u32[]{:S(2)}) async-start(bf16[32,2,32,1024]{3,2,1,0:T(8,128)(2,1)} %copy.24), calls=%async_computation.2 | async-start | bytes 8388608 | tf_op jit(solution)/shard_map/all_to_all | solution.py:37
  446.9 0.1 copy.16
  447.0 53.2 %all-to-all-done.1 = bf16[32,2,32,1024]{3,2,1,0:T(8,128)(2,1)} async-done(((bf16[32,2,32,1024]{3,2,1,0:T(8,128)(2,1)}), bf16[32,2,32,1024]{3,2,1,0:T(8,128)(2,1)}, u32[]{:S(2)}, u32[]{:S(2)}) %all-to-all-start.1) | async-done | bytes 4194336 | tf_op jit(solution)/shard_map/all_to_all | solution.py:37
  500.2 6.5 %bitcast_convert_fusion = f32[2048,1024]{1,0:T(8,128)} fusion(bf16[32,2,32,1024]{3,2,1,0:T(8,128)(2,1)} %all-to-all-done.1), kind=kLoop, calls=%fused_computation.11 | loop fusion | flops 2097152 | bytes 12582912 | tf_op jit(solution)/shard_map/reshape | solution.py:40
  506.6 9.8 %gather_fusion.1 = f32[1024,1024]{1,0:T(8,128)} fusion(f32[2048,1024]{1,0:T(8,128)} %bitcast_convert_fusion, s32[1024]{0:T(1024)S(1)} %broadcast_clamp_fusion), kind=kCustom, calls=%fused_computation.1 | custom fusion | bytes 8392704 | tf_op jit(solution)/shard_map/gather | solution.py:40
  516.5 4.2 fusion.7
  (16 shorter events, 0.3 us)
Async XLA Ops:
  6.5 427.7 %reduce-scatter.2.cloned.1.call-start = ((), (), s32[]{:S(2)}) async-start(), calls=%async_computation.3 | async-start | bytes 20971520 | tf_op jit(solution)/shard_map/reduce_scatter | solution.py:34
  241.2 5.7 %copy-start = (bf16[32,2,32,4096]{3,2,1,0:T(8,128)(2,1)}, bf16[32,2,32,4096]{3,2,1,0:T(8,128)(2,1)S(1)}, u32[]{:S(2)}) copy-start(bf16[32,2,32,4096]{3,2,1,0:T(8,128)(2,1)S(1)} %all_to_all.10) | copy-start | bytes 50331652
  439.2 7.7 %copy-start.1 = (f32[128,8]{0,1:T(8,128)S(1)}, f32[128,8]{0,1:T(8,128)}, u32[]{:S(2)}) copy-start(f32[128,8]{0,1:T(8,128)} %param.8) | copy-start | bytes 12292
  439.2 61.0 %all-to-all-start.1 = ((bf16[32,2,32,1024]{3,2,1,0:T(8,128)(2,1)}), bf16[32,2,32,1024]{3,2,1,0:T(8,128)(2,1)}, u32[]{:S(2)}, u32[]{:S(2)}) async-start(bf16[32,2,32,1024]{3,2,1,0:T(8,128)(2,1)} %copy.24), calls=%async_computation.2 | async-start | bytes 8388608 | tf_op jit(solution)/shard_map/all_to_all | solution.py:37
Sparse Core Ops, SparseCore 0:
  285.3 148.9 reduce-scatter.1
where the time goes:
time: 528 us; the launch traced here: 527 us
  waiting for transfers between devices  202 us (38%)
  blocking collectives  194 us (37%)
  local copies, waits for them, and re-layouts  42.1 us (8%)
  matrix products  38.2 us (7%)
  other arithmetic  29.6 us (6%)
  between operations  13.5 us (3%)
  starting transfers between devices  7.68 us (1%)
    all_to_all x1, blocking collectives, local(): lax.all_to_all(outgoing, 'expert', split_axis=0, concat_axis=0, tiled=True)  194 us
    reduce_scatter x1, waiting for transfers between devices, local(): lax.psum_scatter(partial_value.astype(jnp.bfloat16), 'width', scatter_dim...  149 us
    all_to_all x1, waiting for transfers between devices, local(): lax.all_to_all(reduced.astype(jnp.bfloat16), 'expert', split_axis=0, conc...  53.2 us
    dot_general x1, matrix products, local(): jnp.einsum('skmf,kfd->skmd', hidden, down_weight, preferred_element_type=...  26.2 us
    another operation x3, other arithmetic  18.2 us
    gather x1, local copies, waits for them, and re-layouts, local(): outgoing = padded[table].reshape(n_expert, exp_local, slots, width_all)  14.3 us
    dot_general x1, matrix products, local(): jnp.einsum('skmd,kdf->skmf', arrived, gate_weight, preferred_element_type...  12 us
  transfers between devices with their start and end apart: 2, of which 2 were waited for; matrix products, arithmetic and copies ran while one was open for 0% of the time, Pallas kernels for 0%

commit v1 on v0

v1 whole, which is shorter than its diff:
```python
import jax
import jax.numpy as jnp
from jax import lax
from jax.experimental import pallas as pl
from jax.experimental.pallas import tpu as pltpu
from jax.sharding import PartitionSpec as P

MOST = 32
VMEM_BYTES = 60 * 1024 * 1024


def gate_up_body(group, slots, x_ref, q_ref, gate_ref, up_ref, out_ref, rows_ref):
    tok = x_ref.shape[0] // group
    exp_local, width_all, _ = gate_ref.shape
    place = lax.broadcasted_iota(jnp.int32, (slots, tok), 0)
    for b in range(group):
        pick = jnp.concatenate(
            [
                jnp.where(place == q_ref[b, j][None, :], 1.0, 0.0).astype(jnp.bfloat16)
                for j in range(exp_local)
            ],
            axis=0,
        )
        for c in range(0, width_all, 1024):
            rows = jnp.dot(
                pick,
                x_ref[b * tok : (b + 1) * tok, c : c + 1024],
                preferred_element_type=jnp.float32,
            ).astype(jnp.bfloat16)
            for j in range(exp_local):
                rows_ref[j, b * slots : (b + 1) * slots, c : c + 1024] = rows[
                    j * slots : (j + 1) * slots
                ]
    for j in range(exp_local):
        rows = rows_ref[j]
        gate = jnp.dot(rows, gate_ref[j], preferred_element_type=jnp.float32)
        up = jnp.dot(rows, up_ref[j], preferred_element_type=jnp.float32)
        hidden = (jax.nn.silu(gate) * up).astype(jnp.bfloat16)
        out_ref[:, j] = hidden.reshape(group, slots, hidden.shape[-1])


def gate_up(x_all, q_in, gate_weight, up_weight, slots, group=8):
    sources, exp_local, tok = q_in.shape
    _, width_all, hid = gate_weight.shape
    weight_spec = pl.BlockSpec(
        (exp_local, width_all, hid), lambda i: (0, 0, 0), pipeline_mode=pl.Buffered(1)
    )
    return pl.pallas_call(
        lambda *refs: gate_up_body(group, slots, *refs),
        out_shape=jax.ShapeDtypeStruct((sources, exp_local, slots, hid), jnp.bfloat16),
        grid=(sources // group,),
        in_specs=[
            pl.BlockSpec((group * tok, width_all), lambda i: (i, 0)),
            pl.BlockSpec((group, exp_local, tok), lambda i: (i, 0, 0)),
            weight_spec,
            weight_spec,
        ],
        out_specs=pl.BlockSpec((group, exp_local, slots, hid), lambda i: (i, 0, 0, 0)),
        scratch_shapes=[pltpu.VMEM((exp_local, group * slots, width_all), jnp.bfloat16)],
        compiler_params=pltpu.CompilerParams(vmem_limit_bytes=VMEM_BYTES),
        name="gate_up",
    )(x_all, q_in, gate_weight, up_weight)


def down_body(h_ref, w_ref, out_ref):
    n_width, group, exp_local, slots, hid = h_ref.shape
    cols = w_ref.shape[-1]
    for j in range(exp_local):
        total = jnp.zeros((group * slots, cols), jnp.float32)
        for y in range(n_width):
            total = total + jnp.dot(
                h_ref[y, :, j].reshape(group * slots, hid),
                w_ref[y, j],
                preferred_element_type=jnp.float32,
            )
        out_ref[:, j] = total.astype(jnp.bfloat16).reshape(group, slots, cols)


def down(h_all, weight, group=8):
    n_width, sources, exp_local, slots, hid = h_all.shape
    cols = weight.shape[-1]
    return pl.pallas_call(
        down_body,
        out_shape=jax.ShapeDtypeStruct((sources, exp_local, slots, cols), jnp.bfloat16),
        grid=(sources // group,),
        in_specs=[
            pl.BlockSpec((n_width, group, exp_local, slots, hid), lambda i: (0, i, 0, 0, 0)),
            pl.BlockSpec(
                (n_width, exp_local, hid, cols),
                lambda i: (0, 0, 0, 0),
                pipeline_mode=pl.Buffered(1),
            ),
        ],
        out_specs=pl.BlockSpec((group, exp_local, slots, cols), lambda i: (i, 0, 0, 0)),
        compiler_params=pltpu.CompilerParams(vmem_limit_bytes=VMEM_BYTES),
        name="down",
    )(h_all, weight)


def local(tokens, expert_ids, combine_weights, gate_weight, up_weight, down_weight):
    tok_rows = tokens.shape[0]
    exp_local = gate_weight.shape[0]
    n_expert = lax.axis_size("expert")
    experts_all = exp_local * n_expert
    slots = min(MOST, tok_rows)

    x_all = lax.all_gather(tokens, "expert", axis=0, tiled=True)

    experts = jnp.arange(experts_all, dtype=jnp.int32)
    hit = expert_ids.T[:, None, :] == experts[None, :, None]
    member = jnp.any(hit, axis=0)
    weight_of = jnp.sum(jnp.where(hit, combine_weights.T[:, None, :], 0.0), axis=0)
    order = jnp.arange(tok_rows, dtype=jnp.int32)
    earlier = (order[:, None] < order[None, :]).astype(jnp.bfloat16)
    rank = jnp.dot(member.astype(jnp.bfloat16), earlier, preferred_element_type=jnp.float32)
    place = jnp.where(member, rank.astype(jnp.int32), -1)
    q_in = lax.all_to_all(
        place.reshape(n_expert, exp_local, tok_rows), "expert", split_axis=0, concat_axis=0, tiled=True
    )
    seat = place[:, None, :] == jnp.arange(slots, dtype=jnp.int32)[None, :, None]
    spread = jnp.where(seat, weight_of[:, None, :], 0.0).reshape(experts_all * slots, tok_rows)
    high = spread.astype(jnp.bfloat16)
    low = (spread - high.astype(jnp.float32)).astype(jnp.bfloat16)

    n_width = lax.axis_size("width")
    hid, width_all = down_weight.shape[1:]
    cut = down_weight.reshape(exp_local, hid, n_width, width_all // n_width).transpose(2, 0, 1, 3)
    down_cols = lax.all_to_all(cut, "width", split_axis=0, concat_axis=0, tiled=True)
    x_all, q_in, down_cols = lax.optimization_barrier((x_all, q_in, down_cols))

    hidden = gate_up(x_all, q_in, gate_weight, up_weight, slots)
    h_all = lax.all_gather(hidden, "width", axis=0, tiled=False)
    rows = down(h_all, down_cols)
    returned = lax.all_to_all(rows, "expert", split_axis=0, concat_axis=0, tiled=True)
    returned = returned.reshape(experts_all * slots, rows.shape[-1])
    both = jnp.concatenate([high, low], axis=1)
    mixed = lax.dot_general(
        both, returned, (((0,), (0,)), ((), ())), preferred_element_type=jnp.float32
    )
    return (mixed[:tok_rows] + mixed[tok_rows:]).astype(jnp.bfloat16)


def solution(mesh):
    placed = (
        P("expert", None),
        P("expert", None),
        P("expert", None),
        P("expert", None, "width"),
        P("expert", None, "width"),
        P("expert", "width", None),
    )
    return jax.shard_map(
        local, mesh=mesh, in_specs=placed, out_specs=P("expert", "width"), check_vma=False
    )
```

time: 528 us -> 308 us (0.58)
  blocking collectives: 194 us -> 78.8 us
  waiting for transfers between devices: 202 us -> 130 us
  Pallas kernels: 0 us -> 44 us
  matrix products: 38.2 us -> 4.22 us
  other arithmetic: 29.6 us -> 3.71 us
  local copies, waits for them, and re-layouts: 42.1 us -> 17.5 us
  starting transfers between devices: 7.68 us -> 15.8 us
    reduce_scatter x1 -> x0, waiting for transfers between devices: 149 us -> none  [local(): lax.psum_scatter(partial_value.astype(jnp.bfloat16), 'width', scatter_dim...]
    all_to_all x1, blocking collectives: 194 us -> 78.8 us  [local(): lax.all_to_all(cut, 'width', split_axis=0, concat_axis=0, tiled=True)]
    all_gather x0 -> x2, waiting for transfers between devices: none -> 77.9 us  [the longest x1 65.1 us: local(): h_all = lax.all_gather(hidden, 'width', axis=0, tiled=False)]
    pallas_call x0 -> x2, Pallas kernels: none -> 44 us  [the longest x1 30.4 us: gate_up(): pl.pallas_call(lambda *refs: gate_up_body(group, slots, *refs), out_shape...]
    dot_general x2, matrix products: 38.2 us -> 4.22 us  [the longest x1 3.46 us: local(): lax.dot_general(both, returned, (((0,), (0,)), ((), ())), preferred_eleme...]
    gather x2 -> x0, local copies, waits for them, and re-layouts: 24.1 us -> none  [the longest x1 14.3 us: local(): outgoing = padded[table].reshape(n_expert, exp_local, slots, width_all)]
    another operation x3 -> x0, other arithmetic: 18.2 us -> none
    reshape x0 -> x1, local copies, waits for them, and re-layouts: none -> 8.65 us  [local(): down_weight.reshape(exp_local, hid, n_width, width_all // n_width)]
  transfers between devices with their start and end apart: 2 -> 4, of which waited for: 2 -> 3; matrix products, arithmetic and copies ran while one was open for 0% -> 7% of each run, Pallas kernels for 0% -> 0%
where the time goes in v1:
time: 308 us; the launch traced here: 307 us
  waiting for transfers between devices  130 us (42%)
  blocking collectives  78.8 us (26%)
  Pallas kernels  44 us (14%)
  local copies, waits for them, and re-layouts  17.5 us (6%)
  starting transfers between devices  15.8 us (5%)
  between operations  13.5 us (4%)
  matrix products  4.22 us (1%)
  other arithmetic  3.71 us (1%)
    all_to_all x1, blocking collectives, local(): lax.all_to_all(cut, 'width', split_axis=0, concat_axis=0, tiled=True)  78.8 us
    all_gather x1, waiting for transfers between devices, local(): h_all = lax.all_gather(hidden, 'width', axis=0, tiled=False)  65.1 us
    all_to_all x1, waiting for transfers between devices, local(): lax.all_to_all(rows, 'expert', split_axis=0, concat_axis=0, tiled=True)  51.1 us
    pallas_call x1, Pallas kernels, gate_up(): pl.pallas_call(lambda *refs: gate_up_body(group, slots, *refs), out_shape...  30.4 us
    pallas_call x1, Pallas kernels, down(): pl.pallas_call(down_body, out_shape=jax.ShapeDtypeStruct((sources, exp_lo...  13.6 us
    all_gather x1, waiting for transfers between devices, local(): x_all = lax.all_gather(tokens, 'expert', axis=0, tiled=True)  12.8 us
    unnamed x7, local copies, waits for them, and re-layouts  8.82 us
    reshape x1, local copies, waits for them, and re-layouts, local(): down_weight.reshape(exp_local, hid, n_width, width_all // n_width)  8.65 us
  transfers between devices with their start and end apart: 4, of which 3 were waited for; matrix products, arithmetic and copies ran while one was open for 7% of the time, Pallas kernels for 0%

profile of v1, /device:TPU:0, one launch (start us, length us, event | category | flops | bytes accessed | tf_op | source)
XLA Modules:
  0.0 307.3 jit_solution(12036628264760472868)
XLA Ops:
  6.5 0.0 all-gather.4.cloned.1.call-start
  6.5 0.7 all-gather.4.cloned.1.call-update
  7.3 0.7 fusion.9
  8.0 0.8 fusion
  8.7 8.2 %all-to-all-start = ((s32[32,2,128]{2,1,0:T(2,128)}), s32[32,2,128]{2,1,0:T(2,128)S(1)}, u32[]{:S(2)}, u32[]{:S(2)}) async-start(s32[32,2,128]{2,1,0:T(2,128)} %bitcast.4), calls=%async_computation | async-start | bytes 65536 | tf_op jit(solution)/shard_map/all_to_all | solution.py:117
  17.0 0.0 all-gather.6.cloned.1.call-start
  17.0 8.8 %copy.11 = bf16[2,384,4096]{1,2,0:T(8,128)(2,1)} copy(bf16[2,384,4096]{2,1,0:T(8,128)(2,1)} %param.11) | data formatting | bytes 12582912 | tf_op args[5]
  25.9 8.6 %copy.12 = bf16[2,384,4,1024]{3,1,0,2:T(8,128)(2,1)} copy(bf16[2,384,4,1024]{1,3,2,0:T(8,128)(2,1)} %bitcast.28) | data formatting | bytes 12582912 | tf_op jit(solution)/shard_map/reshape | solution.py:127
  34.5 0.0 all-to-all-done.refs_1_
  34.5 78.8 %all_to_all.15.w_ref = bf16[4,2,384,1024]{3,2,1,0:T(8,128)(2,1)} all-to-all(bf16[4,2,384,1024]{3,2,1,0:T(8,128)(2,1)} %bitcast.27), channel_id=1, replica_groups=mesh['expert'=32,'width'=4] {'width'}, dimensions={0} | all-to-all | bytes 12582912 | tf_op jit(solution)/shard_map/all_to_all | solution.py:128
  113.3 0.0 copy-done
  113.3 12.8 %all-gather.4.cloned.1.call-done.refs_0_ = bf16[4096,4096]{1,0:T(8,128)(2,1)} async-done(((bf16[128,4096]{1,0:T(8,128)(2,1)}), bf16[4096,4096]{1,0:T(8,128)(2,1)}) %all-gather.4.cloned.1.call-update) | async-done | bytes 33554448 | tf_op jit(solution)/shard_map/all_gather | solution.py:107
  126.1 30.4 %gate_up.1 = bf16[32,2,32,384]{3,2,1,0:T(8,128)(2,1)} custom-call(bf16[4096,4096]{1,0:T(8,128)(2,1)} %all-gather.4.cloned.1.call-done.refs_0_, s32[32,2,128]{2,1,0:T(2,128)} %copy-done, bf16[2,4096,384]{2,1,0:T(8,128)(2,1)} %refs_2_.1, bf16[2,4096,384]{2,1,0:T(8,128)(2,1)} %refs_3_.1), custom_call_target="tpu_custom_call" | custom-call | tf_op jit(solution)/shard_map/gate_up/pallas_call | solution.py:48
  156.5 0.0 all-gather.6.cloned.1.call-update
  156.5 65.1 %all-gather.6.cloned.1.call-done = bf16[128,2,32,384]{3,2,1,0:T(8,128)(2,1)} async-done(((bf16[32,2,32,384]{3,2,1,0:T(8,128)(2,1)}), bf16[128,2,32,384]{3,2,1,0:T(8,128)(2,1)}) %all-gather.6.cloned.1.call-update) | async-done | bytes 6291472 | tf_op jit(solution)/shard_map/all_gather | solution.py:132
  221.6 13.6 %down.1 = bf16[32,2,32,1024]{3,2,1,0:T(8,128)(2,1)} custom-call(bf16[4,32,2,32,384]{4,3,2,1,0:T(8,128)(2,1)} %bitcast.29, bf16[4,2,384,1024]{3,2,1,0:T(8,128)(2,1)} %all_to_all.15.w_ref), custom_call_target="tpu_custom_call" | custom-call | tf_op jit(solution)/shard_map/down/pallas_call | solution.py:82
  235.2 7.5 %all-to-all-start.2 = ((bf16[32,2,32,1024]{3,2,1,0:T(8,128)(2,1)}), bf16[32,2,32,1024]{3,2,1,0:T(8,128)(2,1)}, u32[]{:S(2)}, u32[]{:S(2)}) async-start(bf16[32,2,32,1024]{3,2,1,0:T(8,128)(2,1)} %down.1), calls=%async_computation.2 | async-start | bytes 8388608 | tf_op jit(solution)/shard_map/all_to_all | solution.py:134
  242.8 0.1 eq.39
  242.8 0.0 copy-done.2
  242.9 1.1 fusion.6
  244.0 1.1 fusion.7
  245.1 51.1 %all-to-all-done.2 = bf16[32,2,32,1024]{3,2,1,0:T(8,128)(2,1)} async-done(((bf16[32,2,32,1024]{3,2,1,0:T(8,128)(2,1)}), bf16[32,2,32,1024]{3,2,1,0:T(8,128)(2,1)}, u32[]{:S(2)}, u32[]{:S(2)}) %all-to-all-start.2) | async-done | bytes 4194336 | tf_op jit(solution)/shard_map/all_to_all | solution.py:134
  296.2 3.5 %fusion.1 = f32[256,1024]{1,0:T(8,128)S(1)} fusion(bf16[2048,1024]{1,0:T(8,128)(2,1)} %bitcast.8, bf16[2048,128]{1,0:T(8,128)(2,1)S(1)} %fusion.7, bf16[2048,128]{1,0:T(8,128)(2,1)S(1)} %fusion.6), kind=kOutput, calls=%fused_computation.2 | convolution fusion | flops 1075838976 | bytes 6291456 | tf_op jit(solution)/shard_map/dot_general | solution.py:137
  299.7 0.8 fusion.8
  (6 shorter events, 0.0 us)
Async XLA Ops:
  6.5 119.5 %all-gather.4.cloned.1.call-start = ((), (), s32[]{:S(2)}) async-start(), calls=%async_computation.3 | async-start | bytes 34603008 | tf_op jit(solution)/shard_map/all_gather | solution.py:107
  8.7 25.8 %all-to-all-start = ((s32[32,2,128]{2,1,0:T(2,128)}), s32[32,2,128]{2,1,0:T(2,128)S(1)}, u32[]{:S(2)}, u32[]{:S(2)}) async-start(s32[32,2,128]{2,1,0:T(2,128)} %bitcast.4), calls=%async_computation | async-start | bytes 65536 | tf_op jit(solution)/shard_map/all_to_all | solution.py:117
  17.0 204.6 %all-gather.6.cloned.1.call-start = ((), (), s32[]{:S(2)}) async-start(), calls=%async_computation.4 | async-start | bytes 7864320 | tf_op jit(solution)/shard_map/all_gather | solution.py:132
  34.5 78.8 %copy-start = (s32[32,2,128]{2,1,0:T(2,128)}, s32[32,2,128]{2,1,0:T(2,128)S(1)}, u32[]{:S(2)}) copy-start(s32[32,2,128]{2,1,0:T(2,128)S(1)} %all-to-all-done.refs_1_) | copy-start | bytes 98308
  235.2 7.6 %copy-start.1 = (s32[128,8]{0,1:T(8,128)S(1)}, s32[128,8]{0,1:T(8,128)}, u32[]{:S(2)}) copy-start(s32[128,8]{0,1:T(8,128)} %param.7) | copy-start | bytes 12292
  235.2 7.6 %copy-start.2 = (f32[128,8]{0,1:T(8,128)S(1)}, f32[128,8]{0,1:T(8,128)}, u32[]{:S(2)}) copy-start(f32[128,8]{0,1:T(8,128)} %param.8) | copy-start | bytes 12292
  235.2 61.0 %all-to-all-start.2 = ((bf16[32,2,32,1024]{3,2,1,0:T(8,128)(2,1)}), bf16[32,2,32,1024]{3,2,1,0:T(8,128)(2,1)}, u32[]{:S(2)}, u32[]{:S(2)}) async-start(bf16[32,2,32,1024]{3,2,1,0:T(8,128)(2,1)} %down.1), calls=%async_computation.2 | async-start | bytes 8388608 | tf_op jit(solution)/shard_map/all_to_all | solution.py:134
Sparse Core Ops, SparseCore 0:
  9.6 116.4 all-gather.3
  156.7 64.9 all-gather.5

commit v2 on v0

v2 whole, which is shorter than its diff:
```python
import jax
import jax.numpy as jnp
from jax import lax
from jax.experimental import pallas as pl
from jax.experimental.pallas import tpu as pltpu
from jax.sharding import PartitionSpec as P

MOST = 32
SIDE = 4
STEPS = 4
VMEM_BYTES = 56 * 1024 * 1024


def gate_up_body(slots, ids_ref, q_ref, *refs):
    parts = refs[:4]
    gate_ref, up_ref, out_ref, rows_ref, gate_acc, up_acc = refs[4:]
    step = pl.program_id(0)
    tok = q_ref.shape[-1]
    exp_local = gate_ref.shape[0]
    each = parts[0].shape[0] // tok
    place = lax.broadcasted_iota(jnp.int32, (slots, tok), 0)

    @pl.when(step == 0)
    def _():
        gate_acc[...] = jnp.zeros_like(gate_acc)
        up_acc[...] = jnp.zeros_like(up_acc)

    for b in range(4 * each):
        seats = q_ref[ids_ref[b]]
        pick = jnp.concatenate(
            [
                jnp.where(place == seats[j][None, :], 1.0, 0.0).astype(jnp.bfloat16)
                for j in range(exp_local)
            ],
            axis=0,
        )
        at = (b % each) * tok
        rows = jnp.dot(
            pick, parts[b // each][at : at + tok, :], preferred_element_type=jnp.float32
        ).astype(jnp.bfloat16)
        for j in range(exp_local):
            rows_ref[j, b * slots : (b + 1) * slots, :] = rows[j * slots : (j + 1) * slots]
    for j in range(exp_local):
        rows = rows_ref[j]
        gate_acc[j] += jnp.dot(rows, gate_ref[j], preferred_element_type=jnp.float32)
        up_acc[j] += jnp.dot(rows, up_ref[j], preferred_element_type=jnp.float32)

    @pl.when(step == pl.num_programs(0) - 1)
    def _():
        for j in range(exp_local):
            hidden = (jax.nn.silu(gate_acc[j]) * up_acc[j]).astype(jnp.bfloat16)
            out_ref[:, j] = hidden.reshape(4 * each, slots, hidden.shape[-1])


def gate_up(ids, q_in, parts, gate_weight, up_weight, slots):
    _, exp_local, tok = q_in.shape
    _, width_all, hid = gate_weight.shape
    count = 4 * parts[0].shape[0] // tok
    wide = width_all // STEPS
    weight_spec = pl.BlockSpec((exp_local, wide, hid), lambda k, ids: (0, k, 0))
    part_spec = pl.BlockSpec((parts[0].shape[0], wide), lambda k, ids: (0, k))
    flops = 2 * exp_local * count * slots * width_all * 2 * hid
    return pl.pallas_call(
        lambda *refs: gate_up_body(slots, *refs),
        out_shape=jax.ShapeDtypeStruct((count, exp_local, slots, hid), jnp.bfloat16),
        grid_spec=pltpu.PrefetchScalarGridSpec(
            num_scalar_prefetch=1,
            grid=(STEPS,),
            in_specs=[
                pl.BlockSpec(q_in.shape, lambda k, ids: (0, 0, 0)),
                *[part_spec] * 4,
                weight_spec,
                weight_spec,
            ],
            out_specs=pl.BlockSpec((count, exp_local, slots, hid), lambda k, ids: (0, 0, 0, 0)),
            scratch_shapes=[
                pltpu.VMEM((exp_local, count * slots, wide), jnp.bfloat16),
                pltpu.VMEM((exp_local, count * slots, hid), jnp.float32),
                pltpu.VMEM((exp_local, count * slots, hid), jnp.float32),
            ],
        ),
        compiler_params=pltpu.CompilerParams(vmem_limit_bytes=VMEM_BYTES),
        cost_estimate=pl.CostEstimate(
            flops=flops,
            transcendentals=0,
            bytes_accessed=2 * (2 * exp_local * width_all * hid + count * tok * width_all),
        ),
        name="gate_up",
    )(ids, q_in, *parts, gate_weight, up_weight)


def down_body(chunks, ids_ref, *refs):
    hs = refs[: 4 * chunks]
    ws = refs[4 * chunks : 4 * chunks + 4]
    out_ref, rows_ref, sem = refs[-3:]
    count, exp_local, slots, hid = hs[0].shape
    cols = ws[0].shape[-1]
    copies = []
    for n in range(chunks):
        for j in range(exp_local):
            total = jnp.zeros((count * slots, cols), jnp.float32)
            for y in range(4):
                total = total + jnp.dot(
                    hs[4 * n + y][:, j].reshape(count * slots, hid),
                    ws[y][j],
                    preferred_element_type=jnp.float32,
                )
            rows_ref[n, :, j] = total.astype(jnp.bfloat16).reshape(count, slots, cols)
        for b in range(count):
            copy = pltpu.make_async_copy(
                rows_ref.at[n, b], out_ref.at[ids_ref[n * count + b]], sem.at[n * count + b]
            )
            copy.start()
            copies.append(copy)
    for copy in copies:
        copy.wait()


def down(ids, hidden, weights, sources, before=None):
    chunks = len(hidden)
    count, exp_local, slots, hid = hidden[0][0].shape
    cols = weights[0].shape[-1]
    flat = [h for four in hidden for h in four]
    operands = [ids, *flat, *weights]
    specs = [pl.BlockSpec(memory_space=pltpu.VMEM)] * (len(flat) + 4)
    aliases = {}
    if before is not None:
        aliases = {len(operands): 0}
        operands.append(before)
        specs = specs + [pl.BlockSpec(memory_space=pl.ANY)]
    return pl.pallas_call(
        lambda *refs: down_body(chunks, *refs),
        out_shape=jax.ShapeDtypeStruct((sources, exp_local, slots, cols), jnp.bfloat16),
        grid_spec=pltpu.PrefetchScalarGridSpec(
            num_scalar_prefetch=1,
            grid=(),
            in_specs=specs,
            out_specs=pl.BlockSpec(memory_space=pl.ANY),
            scratch_shapes=[
                pltpu.VMEM((chunks, count, exp_local, slots, cols), jnp.bfloat16),
                pltpu.SemaphoreType.DMA((chunks * count,)),
            ],
        ),
        input_output_aliases=aliases,
        compiler_params=pltpu.CompilerParams(vmem_limit_bytes=VMEM_BYTES),
        cost_estimate=pl.CostEstimate(
            flops=2 * chunks * exp_local * count * slots * cols * 4 * hid,
            transcendentals=0,
            bytes_accessed=2 * (exp_local * 4 * hid * cols + chunks * exp_local * count * slots * cols),
        ),
        name="down",
    )(*operands)


def place_of(z, x, c):
    return (z % SIDE) * SIDE * 2 + (x % SIDE) * 2 + c


def move(axis, by):
    pairs = []
    for z in range(SIDE):
        for x in range(SIDE):
            for c in range(2):
                along_z = (axis == 0) == (c == 0)
                to = place_of(z + by, x, c) if along_z else place_of(z, x + by, c)
                pairs.append((place_of(z, x, c), to))
    return pairs


def other_core():
    spots = [(z, x, c) for z in range(SIDE) for x in range(SIDE) for c in range(2)]
    return [(place_of(z, x, c), place_of(z, x, 1 - c)) for z, x, c in spots]


def gather_chunks(tokens):
    half = tokens.shape[0] // 2
    send = lambda v, axis, by: lax.ppermute(v, "expert", move(axis, by))
    swap = lambda v: lax.ppermute(v, "expert", other_core())
    fore, back = send(tokens, 0, 1), send(tokens, 0, -1)
    far = [send(fore[:half], 0, 1), send(back[half:], 0, -1)]
    near_a = jnp.concatenate([tokens, fore], axis=0)
    near_b = jnp.concatenate([back, *far], axis=0)
    fore_a, back_b = send(near_a, 1, 1), send(near_b, 1, -1)
    fore_b, back_a = send(near_b, 1, 1), send(near_a, 1, -1)
    far_a, far_b = send(fore_a, 1, 1), send(back_b, 1, -1)
    pairs = [(near_a, near_b), (fore_a, back_b), (fore_b, back_a), (far_a, far_b)]
    return [[a, swap(a), b, swap(b)] for a, b in pairs]


def chunk_ids():
    me = lax.axis_index("expert")
    z, x, c = me // (2 * SIDE), me // 2 % SIDE, me % 2
    near, wide = (0, -1), (1, 2)
    chunks = [
        ((near, 0), (wide, 0)),
        ((near, -1), (wide, 1)),
        ((wide, -1), (near, 1)),
        ((near, -2), (wide, 2)),
    ]
    first, second, kinds = [], [], []
    for halves in chunks:
        for along, across in halves:
            for kind in (0, 1):
                for step in along:
                    first.append(step)
                    second.append(across)
                    kinds.append(kind)
    first, second, kinds = (jnp.array(v, jnp.int32) for v in (first, second, kinds))
    core = jnp.where(kinds == 0, c, 1 - c)
    dz = jnp.where(core == 0, first, second)
    dx = jnp.where(core == 0, second, first)
    ids = (z + dz + SIDE) % SIDE * (2 * SIDE) + (x + dx + SIDE) % SIDE * 2 + core
    return ids.astype(jnp.int32).reshape(4, -1)


def around(v, by):
    n = lax.axis_size("width")
    return lax.ppermute(v, "width", [(i, (i + by) % n) for i in range(n)])


def local(tokens, expert_ids, combine_weights, gate_weight, up_weight, down_weight):
    tok_rows = tokens.shape[0]
    exp_local = gate_weight.shape[0]
    n_expert = lax.axis_size("expert")
    n_width = lax.axis_size("width")
    experts_all = exp_local * n_expert
    slots = min(MOST, tok_rows)

    experts = jnp.arange(experts_all, dtype=jnp.int32)
    hit = expert_ids.T[:, None, :] == experts[None, :, None]
    member = jnp.any(hit, axis=0)
    weight_of = jnp.sum(jnp.where(hit, combine_weights.T[:, None, :], 0.0), axis=0)
    order = jnp.arange(tok_rows, dtype=jnp.int32)
    earlier = (order[:, None] < order[None, :]).astype(jnp.bfloat16)
    rank = jnp.dot(member.astype(jnp.bfloat16), earlier, preferred_element_type=jnp.float32)
    place = jnp.where(member, rank.astype(jnp.int32), -1)
    q_in = lax.all_to_all(
        place.reshape(n_expert, exp_local, tok_rows), "expert", split_axis=0, concat_axis=0, tiled=True
    )
    seat = place[:, None, :] == jnp.arange(slots, dtype=jnp.int32)[None, :, None]
    spread = jnp.where(seat, weight_of[:, None, :], 0.0).reshape(experts_all * slots, tok_rows)
    high = spread.astype(jnp.bfloat16)
    low = (spread - high.astype(jnp.float32)).astype(jnp.bfloat16)

    cols = down_weight.shape[2] // n_width
    mine = lax.axis_index("width")
    cut = lambda by: lax.dynamic_slice_in_dim(down_weight, (mine + by) % n_width * cols, cols, 2)
    weights = [cut(0), around(cut(1), 1), around(cut(3), -1), around(cut(2), 2)]

    ids = chunk_ids()
    hidden = []
    for n, parts in enumerate(gather_chunks(tokens)):
        h = gate_up(ids[n], q_in, parts, gate_weight, up_weight, slots)
        half = h.shape[0] // 2
        fore, back = around(h, 1), around(h, -1)
        far = jnp.concatenate([around(fore[:half], 1), around(back[half:], -1)], axis=0)
        hidden.append([h, fore, back, far])
    rows = down(ids[:3].reshape(-1), hidden[:3], weights, n_expert)
    rows = down(ids[3], hidden[3:], weights, n_expert, rows)

    returned = lax.all_to_all(rows, "expert", split_axis=0, concat_axis=0, tiled=True)
    returned = returned.reshape(experts_all * slots, cols)
    both = jnp.concatenate([high, low], axis=1)
    mixed = lax.dot_general(
        both, returned, (((0,), (0,)), ((), ())), preferred_element_type=jnp.float32
    )
    return (mixed[:tok_rows] + mixed[tok_rows:]).astype(jnp.bfloat16)


def solution(mesh):
    placed = (
        P("expert", None),
        P("expert", None),
        P("expert", None),
        P("expert", None, "width"),
        P("expert", None, "width"),
        P("expert", "width", None),
    )
    return jax.shard_map(
        local, mesh=mesh, in_specs=placed, out_specs=P("expert", "width"), check_vma=False
    )
```

time: 528 us -> 344 us (0.65)
  blocking collectives: 194 us -> 0 us
  Pallas kernels: 0 us -> 67 us
  starting transfers between devices: 7.68 us -> 58.8 us
  matrix products: 38.2 us -> 4.22 us
  local copies, waits for them, and re-layouts: 42.1 us -> 16.2 us
  other arithmetic: 29.6 us -> 6.3 us
  between operations: 13.5 us -> 0.49 us
  waiting for transfers between devices: 202 us -> 190 us
    all_to_all x1 -> x0, blocking collectives: 194 us -> none  [local(): lax.all_to_all(outgoing, 'expert', split_axis=0, concat_axis=0, tiled=True)]
    reduce_scatter x1 -> x0, waiting for transfers between devices: 149 us -> none  [local(): lax.psum_scatter(partial_value.astype(jnp.bfloat16), 'width', scatter_dim...]
    ppermute x0 -> x37, waiting for transfers between devices: none -> 122 us  [the longest x19 70.8 us: around(): return lax.ppermute(v, 'width', [(i, (i + by) % n) for i in range(n)])]
    pallas_call x0 -> x6, Pallas kernels: none -> 67 us  [the longest x4 47.1 us: gate_up(): pl.pallas_call(lambda *refs: gate_up_body(slots, *refs), out_shape=jax.Sh...]
    ppermute x0 -> x37, starting transfers between devices: none -> 48.2 us  [the longest x19 26.4 us: around(): return lax.ppermute(v, 'width', [(i, (i + by) % n) for i in range(n)])]
    dot_general x2, matrix products: 38.2 us -> 4.22 us  [the longest x1 3.46 us: local(): lax.dot_general(both, returned, (((0,), (0,)), ((), ())), preferred_eleme...]
    gather x2 -> x0, local copies, waits for them, and re-layouts: 24.1 us -> none  [the longest x1 14.3 us: local(): outgoing = padded[table].reshape(n_expert, exp_local, slots, width_all)]
    another operation x3 -> x0, other arithmetic: 18.2 us -> none
  transfers between devices with their start and end apart: 2 -> 39, of which waited for: 2 -> 12; matrix products, arithmetic and copies ran while one was open for 0% -> 5% of each run, Pallas kernels for 0% -> 17%
where the time goes in v2:
time: 344 us; the launch traced here: 343 us
  waiting for transfers between devices  190 us (55%)
  Pallas kernels  67 us (19%)
  starting transfers between devices  58.8 us (17%)
  local copies, waits for them, and re-layouts  16.2 us (5%)
  other arithmetic  6.3 us (2%)
  matrix products  4.22 us (1%)
    ppermute x19, waiting for transfers between devices, around(): return lax.ppermute(v, 'width', [(i, (i + by) % n) for i in range(n)])  70.8 us
    ppermute x10, waiting for transfers between devices, gather_chunks(): send = lambda v, axis, by: lax.ppermute(v, 'expert', move(axis, by))  51.4 us
    all_to_all x1, waiting for transfers between devices, local(): lax.all_to_all(rows, 'expert', split_axis=0, concat_axis=0, tiled=True)  51.1 us
    pallas_call x4, Pallas kernels, gate_up(): pl.pallas_call(lambda *refs: gate_up_body(slots, *refs), out_shape=jax.Sh...  47.1 us
    ppermute x19, starting transfers between devices, around(): return lax.ppermute(v, 'width', [(i, (i + by) % n) for i in range(n)])  26.4 us
    ppermute x10, starting transfers between devices, gather_chunks(): send = lambda v, axis, by: lax.ppermute(v, 'expert', move(axis, by))  21.1 us
    pallas_call x2, Pallas kernels, down(): pl.pallas_call(lambda *refs: down_body(chunks, *refs), out_shape=jax.Shap...  20 us
    all_to_all x1, waiting for transfers between devices, local(): lax.all_to_all(place.reshape(n_expert, exp_local, tok_rows), 'expert', sp...  16.9 us
  transfers between devices with their start and end apart: 39, of which 12 were waited for; matrix products, arithmetic and copies ran while one was open for 5% of the time, Pallas kernels for 17%

profile of v2, /device:TPU:0, one launch (start us, length us, event | category | flops | bytes accessed | tf_op | source)
XLA Modules:
  0.0 343.3 jit_solution(8398599334072565318)
XLA Ops:
  6.5 10.7 %collective-permute-done = bf16[128,4096]{1,0:T(8,128)(2,1)S(1)} collective-permute-done((bf16[128,4096]{1,0:T(8,128)(2,1)}, bf16[128,4096]{1,0:T(8,128)(2,1)S(1)}, u32[]{:S(2)}, u32[]{:S(2)}) %collective-permute-start) | collective-permute-done | bytes 1048608 | tf_op jit(solution)/shard_map/ppermute | solution.py:177
  24.5 12.6 %collective-permute-done.5 = bf16[64,4096]{1,0:T(8,128)(2,1)S(1)} collective-permute-done((bf16[64,4096]{1,0:T(8,128)(2,1)S(1)}, bf16[64,4096]{1,0:T(8,128)(2,1)S(1)}, u32[]{:S(2)}, u32[]{:S(2)}) %collective-permute-start.5) | collective-permute-done | bytes 524320 | tf_op jit(solution)/shard_map/ppermute | solution.py:177
  37.8 12.6 %collective-permute-done.31.refs_4_ = bf16[256,4096]{1,0:T(8,128)(2,1)} collective-permute-done((bf16[256,4096]{1,0:T(8,128)(2,1)}, bf16[256,4096]{1,0:T(8,128)(2,1)}, u32[]{:S(2)}, u32[]{:S(2)}) %collective-permute-start.31) | collective-permute-done | bytes 2097184 | tf_op jit(solution)/shard_map/ppermute | solution.py:177
  50.4 3.7 %collective-permute-start.7 = (bf16[256,4096]{1,0:T(8,128)(2,1)S(1)}, bf16[256,4096]{1,0:T(8,128)(2,1)}, u32[]{:S(2)}, u32[]{:S(2)}) collective-permute-start(bf16[256,4096]{1,0:T(8,128)(2,1)S(1)} %constant_dynamic-update-slice_fusion.2.refs_4_), channel_id=1, source_target_pairs={{0,24},{4,100},{8,0},{12,108},{16,8},{20,116},{24,16},{28,124},{32... | collective-permute-start | bytes 6291464 | tf_op jit(solution)/shard_map/ppermute | solution.py:177
  54.9 3.9 %all-to-all-start = ((s32[32,2,128]{2,1,0:T(2,128)}), s32[32,2,128]{2,1,0:T(2,128)S(1)}, u32[]{:S(2)}, u32[]{:S(2)}) async-start(s32[32,2,128]{2,1,0:T(2,128)} %bitcast.4), calls=%async_computation | async-start | bytes 65536 | tf_op jit(solution)/shard_map/all_to_all | solution.py:237
  61.3 16.9 %all-to-all-done.refs_1_ = s32[32,2,128]{2,1,0:T(2,128)S(1)} async-done(((s32[32,2,128]{2,1,0:T(2,128)}), s32[32,2,128]{2,1,0:T(2,128)S(1)}, u32[]{:S(2)}, u32[]{:S(2)}) %all-to-all-start) | async-done | bytes 32800 | tf_op jit(solution)/shard_map/all_to_all | solution.py:237
  78.8 11.8 %gate_up.5.refs_1_ = bf16[8,2,32,384]{3,2,1,0:T(8,128)(2,1)} custom-call(s32[8]{0:T(128)} %get-tuple-element.11.refs_0_, s32[32,2,128]{2,1,0:T(2,128)} %copy-done.10, bf16[256,4096]{1,0:T(8,128)(2,1)} %constant_dynamic-update-slice_fusion.refs_2_, bf16[256,4096]{1,0:T(8,128)(2,1)} %collective-permute-done.17.refs_3_, bf16[256,4096]{1,0:T(8,128)(2,1)} %copy-done, ...), custom_call_target="tpu_custom_call" | custom-call | flops 3221225472 | bytes 20971520 | tf_op jit(solution)/shard_map/gate_up/pallas_call | solution.py:63
  92.1 5.1 %collective-permute-start.8 = (bf16[256,4096]{1,0:T(8,128)(2,1)}, bf16[256,4096]{1,0:T(8,128)(2,1)S(1)}, u32[]{:S(2)}, u32[]{:S(2)}) collective-permute-start(bf16[256,4096]{1,0:T(8,128)(2,1)} %collective-permute-done.7.refs_4_), channel_id=1, source_target_pairs={{0,24},{4,100},{8,0},{12,108},{16,8},{20,116},{24,16},{28,124},{32... | collective-permute-start | bytes 6291464 | tf_op jit(solution)/shard_map/ppermute | solution.py:177
  97.2 5.9 %collective-permute-done.19.refs_2_ = bf16[8,2,32,384]{3,2,1,0:T(8,128)(2,1)S(1)} collective-permute-done((bf16[8,2,32,384]{3,2,1,0:T(8,128)(2,1)}, bf16[8,2,32,384]{3,2,1,0:T(8,128)(2,1)S(1)}, u32[]{:S(2)}, u32[]{:S(2)}) %collective-permute-start.19) | collective-permute-done | bytes 393248 | tf_op jit(solution)/shard_map/ppermute | solution.py:218
  105.5 15.6 %collective-permute-done.8.refs_4_ = bf16[256,4096]{1,0:T(8,128)(2,1)S(1)} collective-permute-done((bf16[256,4096]{1,0:T(8,128)(2,1)}, bf16[256,4096]{1,0:T(8,128)(2,1)S(1)}, u32[]{:S(2)}, u32[]{:S(2)}) %collective-permute-start.8) | collective-permute-done | bytes 2097184 | tf_op jit(solution)/shard_map/ppermute | solution.py:177
  121.1 11.8 %gate_up.7.refs_9_ = bf16[8,2,32,384]{3,2,1,0:T(8,128)(2,1)} custom-call(s32[8]{0:T(128)} %get-tuple-element.9.refs_0_, s32[32,2,128]{2,1,0:T(2,128)} %copy-done.10, bf16[256,4096]{1,0:T(8,128)(2,1)} %collective-permute-done.29.refs_2_, bf16[256,4096]{1,0:T(8,128)(2,1)} %copy-done.4, bf16[256,4096]{1,0:T(8,128)(2,1)} %collective-permute-done.31.refs_4_, ...), custom_call_target="tpu_custom_call" | custom-call | flops 3221225472 | bytes 20971520 | tf_op jit(solution)/shard_map/gate_up/pallas_call | solution.py:63
  137.9 11.8 %gate_up.6.refs_5_ = bf16[8,2,32,384]{3,2,1,0:T(8,128)(2,1)} custom-call(s32[8]{0:T(128)} %get-tuple-element.10.refs_0_, s32[32,2,128]{2,1,0:T(2,128)} %copy-done.10, bf16[256,4096]{1,0:T(8,128)(2,1)} %collective-permute-done.1.refs_2_, bf16[256,4096]{1,0:T(8,128)(2,1)} %copy-done.2, bf16[256,4096]{1,0:T(8,128)(2,1)} %collective-permute-done.7.refs_4_, ...), custom_call_target="tpu_custom_call" | custom-call | flops 3221225472 | bytes 20971520 | tf_op jit(solution)/shard_map/gate_up/pallas_call | solution.py:63
  154.2 4.3 %collective-permute-done.22 = bf16[4,2,32,384]{3,2,1,0:T(8,128)(2,1)S(1)} collective-permute-done((bf16[4,2,32,384]{3,2,1,0:T(8,128)(2,1)S(1)}, bf16[4,2,32,384]{3,2,1,0:T(8,128)(2,1)S(1)}, u32[]{:S(2)}, u32[]{:S(2)}) %collective-permute-start.22) | collective-permute-done | bytes 196640 | tf_op jit(solution)/shard_map/ppermute | solution.py:218
  158.8 4.5 %collective-permute-done.25.refs_6_ = bf16[8,2,32,384]{3,2,1,0:T(8,128)(2,1)} collective-permute-done((bf16[8,2,32,384]{3,2,1,0:T(8,128)(2,1)}, bf16[8,2,32,384]{3,2,1,0:T(8,128)(2,1)}, u32[]{:S(2)}, u32[]{:S(2)}) %collective-permute-start.25) | collective-permute-done | bytes 393248 | tf_op jit(solution)/shard_map/ppermute | solution.py:218
  163.3 6.0 %constant_dynamic-slice_fusion = (bf16[2,384,1024]{2,1,0:T(8,128)(2,1)}, bf16[2,384,1024]{2,1,0:T(8,128)(2,1)}, bf16[2,384,1024]{2,1,0:T(8,128)(2,1)}, bf16[2,384,1024]{2,1,0:T(8,128)(2,1)}) fusion(bf16[2,384,4096]{2,1,0:T(8,128)(2,1)} %param.14, s32[]{:T(128)S(6)} %select_n.99, s32[]{:T(128)S(6)} %select_n.95, s32[]{:T(128)S(6)} %select_n.93, s32[]{:T(128)S(6)} %select_n.97), kind=kLoop, calls=%fused_computation.34 | loop fusion | bytes 12582928 | tf_op jit(solution)/shard_map/dynamic_slice | solution.py:247
  178.8 11.8 %gate_up.4.refs_1_ = bf16[8,2,32,384]{3,2,1,0:T(8,128)(2,1)} custom-call(s32[8]{0:T(128)} %get-tuple-element.12.refs_0_, s32[32,2,128]{2,1,0:T(2,128)} %copy-done.10, bf16[256,4096]{1,0:T(8,128)(2,1)} %collective-permute-done.2.refs_2_, bf16[256,4096]{1,0:T(8,128)(2,1)} %collective-permute-done.3.refs_3_, bf16[256,4096]{1,0:T(8,128)(2,1)} %copy-done.1, ...), custom_call_target="tpu_custom_call" | custom-call | flops 3221225472 | bytes 20971520 | tf_op jit(solution)/shard_map/gate_up/pallas_call | solution.py:63
  190.5 52.3 %collective-permute-done.27 = bf16[4,2,32,384]{3,2,1,0:T(8,128)(2,1)S(1)} collective-permute-done((bf16[4,2,32,384]{3,2,1,0:T(8,128)(2,1)S(1)}, bf16[4,2,32,384]{3,2,1,0:T(8,128)(2,1)S(1)}, u32[]{:S(2)}, u32[]{:S(2)}) %collective-permute-start.27) | collective-permute-done | bytes 196640 | tf_op jit(solution)/shard_map/ppermute | solution.py:218
  248.5 3.7 %collective-permute-done.10.refs_2_ = bf16[8,2,32,384]{3,2,1,0:T(8,128)(2,1)S(1)} collective-permute-done((bf16[8,2,32,384]{3,2,1,0:T(8,128)(2,1)}, bf16[8,2,32,384]{3,2,1,0:T(8,128)(2,1)S(1)}, u32[]{:S(2)}, u32[]{:S(2)}) %collective-permute-start.10) | collective-permute-done | bytes 393248 | tf_op jit(solution)/shard_map/ppermute | solution.py:218
  252.3 3.5 %collective-permute-start.13 = (bf16[4,2,32,384]{3,2,1,0:T(8,128)(2,1)S(1)}, bf16[4,2,32,384]{3,2,1,0:T(8,128)(2,1)S(1)}, u32[]{:S(2)}, u32[]{:S(2)}) collective-permute-start(bf16[4,2,32,384]{3,2,1,0:T(8,128)(2,1)S(1)} %slice.77), channel_id=1, source_target_pairs={{0,3},{1,0},{2,1},{3,2},{4,7},{5,4},{6,5},{7,6},{8,11},{9,8},{10,9... | collective-permute-start | bytes 589832 | tf_op jit(solution)/shard_map/ppermute | solution.py:218
  258.1 12.6 %down.2.refs_9_ = bf16[32,2,32,1024]{3,2,1,0:T(8,128)(2,1)} custom-call(s32[24]{0:T(128)} %bitcast.27, bf16[8,2,32,384]{3,2,1,0:T(8,128)(2,1)} %gate_up.5.refs_1_, bf16[8,2,32,384]{3,2,1,0:T(8,128)(2,1)} %copy-done.11, bf16[8,2,32,384]{3,2,1,0:T(8,128)(2,1)} %copy-done.12, bf16[8,2,32,384]{3,2,1,0:T(8,128)(2,1)} %pad_maximum_fusion.1.refs_4_, ...), custom_call_target="tpu_custom_call" | custom-call | flops 4831838208 | bytes 9437184 | tf_op jit(solution)/shard_map/down/pallas_call | solution.py:131
  271.5 7.4 %down.3 = bf16[32,2,32,1024]{3,2,1,0:T(8,128)(2,1)} custom-call(s32[8]{0:T(128)} %get-tuple-element.12.refs_0_, bf16[8,2,32,384]{3,2,1,0:T(8,128)(2,1)} %gate_up.4.refs_1_, bf16[8,2,32,384]{3,2,1,0:T(8,128)(2,1)} %copy-done.8, bf16[8,2,32,384]{3,2,1,0:T(8,128)(2,1)} %copy-done.9, ...), custom_call_target="tpu_custom_call", output_to_operand_aliasing={{}: (9, {})} | custom-call | flops 1610612736 | bytes 7340032 | tf_op jit(solution)/shard_map/down/pallas_call | solution.py:131
  278.9 6.7 %all-to-all-start.1 = ((bf16[32,2,32,1024]{3,2,1,0:T(8,128)(2,1)}), bf16[32,2,32,1024]{3,2,1,0:T(8,128)(2,1)}, u32[]{:S(2)}, u32[]{:S(2)}) async-start(bf16[32,2,32,1024]{3,2,1,0:T(8,128)(2,1)} %down.3), calls=%async_computation.1 | async-start | bytes 8388608 | tf_op jit(solution)/shard_map/all_to_all | solution.py:261
  288.0 51.1 %all-to-all-done.1 = bf16[32,2,32,1024]{3,2,1,0:T(8,128)(2,1)} async-done(((bf16[32,2,32,1024]{3,2,1,0:T(8,128)(2,1)}), bf16[32,2,32,1024]{3,2,1,0:T(8,128)(2,1)}, u32[]{:S(2)}, u32[]{:S(2)}) %all-to-all-start.1) | async-done | bytes 4194336 | tf_op jit(solution)/shard_map/all_to_all | solution.py:261
  339.1 3.5 %fusion.1 = f32[256,1024]{1,0:T(8,128)S(1)} fusion(bf16[2048,1024]{1,0:T(8,128)(2,1)} %bitcast.5, bf16[2048,128]{1,0:T(8,128)(2,1)S(1)} %fusion.7, bf16[2048,128]{1,0:T(8,128)(2,1)S(1)} %fusion.6), kind=kOutput, calls=%fused_computation.2 | convolution fusion | flops 1075838976 | bytes 6291456 | tf_op jit(solution)/shard_map/dot_general | solution.py:264
  (131 shorter events, 53.4 us)
Async XLA Ops:
  2.0 19.2 %collective-permute-start.4 = (bf16[128,4096]{1,0:T(8,128)(2,1)}, bf16[128,4096]{1,0:T(8,128)(2,1)S(1)}, u32[]{:S(2)}, u32[]{:S(2)}) collective-permute-start(bf16[128,4096]{1,0:T(8,128)(2,1)} %param.9), channel_id=1, source_target_pairs={{0,96},{4,28},{8,104},{12,4},{16,112},{20,12},{24,120},{28,20},{32... | collective-permute-start | bytes 3145736 | tf_op jit(solution)/shard_map/ppermute | solution.py:177
  18.1 32.2 %collective-permute-start.31 = (bf16[256,4096]{1,0:T(8,128)(2,1)}, bf16[256,4096]{1,0:T(8,128)(2,1)}, u32[]{:S(2)}, u32[]{:S(2)}) collective-permute-start(bf16[256,4096]{1,0:T(8,128)(2,1)} %constant_dynamic-update-slice_fusion.refs_2_), channel_id=1, source_target_pairs={{0,24},{4,100},{8,0},{12,108},{16,8},{20,116},{24,16},{28,124},{32... | collective-permute-start | bytes 6291464 | tf_op jit(solution)/shard_map/ppermute | solution.py:177
  21.0 33.1 %collective-permute-start.1 = (bf16[256,4096]{1,0:T(8,128)(2,1)}, bf16[256,4096]{1,0:T(8,128)(2,1)}, u32[]{:S(2)}, u32[]{:S(2)}) collective-permute-start(bf16[256,4096]{1,0:T(8,128)(2,1)} %constant_dynamic-update-slice_fusion.refs_2_), channel_id=1, source_target_pairs={{0,8},{4,36},{8,16},{12,44},{16,24},{20,52},{24,0},{28,60},{32,40}... | collective-permute-start | bytes 6291464 | tf_op jit(solution)/shard_map/ppermute | solution.py:177
  21.1 38.4 %collective-permute-start.17 = (bf16[256,4096]{1,0:T(8,128)(2,1)}, bf16[256,4096]{1,0:T(8,128)(2,1)}, u32[]{:S(2)}, u32[]{:S(2)}) collective-permute-start(bf16[256,4096]{1,0:T(8,128)(2,1)} %constant_dynamic-update-slice_fusion.refs_2_), channel_id=1, source_target_pairs={{0,4},{4,0},{8,12},{12,8},{16,20},{20,16},{24,28},{28,24},{32,36},... | collective-permute-start | bytes 6291464 | tf_op jit(solution)/shard_map/ppermute | solution.py:178
  37.2 41.0 %collective-permute-start.18 = (bf16[256,4096]{1,0:T(8,128)(2,1)S(1)}, bf16[256,4096]{1,0:T(8,128)(2,1)}, u32[]{:S(2)}, u32[]{:S(2)}) collective-permute-start(bf16[256,4096]{1,0:T(8,128)(2,1)S(1)} %constant_dynamic-update-slice_fusion.2.refs_4_), channel_id=1, source_target_pairs={{0,4},{4,0},{8,12},{12,8},{16,20},{20,16},{24,28},{28,24},{32,36},... | collective-permute-start | bytes 6291464 | tf_op jit(solution)/shard_map/ppermute | solution.py:178
  37.3 54.8 %collective-permute-start.29 = (bf16[256,4096]{1,0:T(8,128)(2,1)S(1)}, bf16[256,4096]{1,0:T(8,128)(2,1)}, u32[]{:S(2)}, u32[]{:S(2)}) collective-permute-start(bf16[256,4096]{1,0:T(8,128)(2,1)S(1)} %constant_dynamic-update-slice_fusion.2.refs_4_), channel_id=1, source_target_pairs={{0,8},{4,36},{8,16},{12,44},{16,24},{20,52},{24,0},{28,60},{32,40}... | collective-permute-start | bytes 6291464 | tf_op jit(solution)/shard_map/ppermute | solution.py:177
  50.4 41.7 %collective-permute-start.7 = (bf16[256,4096]{1,0:T(8,128)(2,1)S(1)}, bf16[256,4096]{1,0:T(8,128)(2,1)}, u32[]{:S(2)}, u32[]{:S(2)}) collective-permute-start(bf16[256,4096]{1,0:T(8,128)(2,1)S(1)} %constant_dynamic-update-slice_fusion.2.refs_4_), channel_id=1, source_target_pairs={{0,24},{4,100},{8,0},{12,108},{16,8},{20,116},{24,16},{28,124},{32... | collective-permute-start | bytes 6291464 | tf_op jit(solution)/shard_map/ppermute | solution.py:177
  54.1 49.0 %collective-permute-start.32 = (bf16[256,4096]{1,0:T(8,128)(2,1)}, bf16[256,4096]{1,0:T(8,128)(2,1)}, u32[]{:S(2)}, u32[]{:S(2)}) collective-permute-start(bf16[256,4096]{1,0:T(8,128)(2,1)} %collective-permute-done.31.refs_4_), channel_id=1, source_target_pairs={{0,4},{4,0},{8,12},{12,8},{16,20},{20,16},{24,28},{28,24},{32,36},... | collective-permute-start | bytes 6291464 | tf_op jit(solution)/shard_map/ppermute | solution.py:178
  54.9 23.3 %all-to-all-start = ((s32[32,2,128]{2,1,0:T(2,128)}), s32[32,2,128]{2,1,0:T(2,128)S(1)}, u32[]{:S(2)}, u32[]{:S(2)}) async-start(s32[32,2,128]{2,1,0:T(2,128)} %bitcast.4), calls=%async_computation | async-start | bytes 65536 | tf_op jit(solution)/shard_map/all_to_all | solution.py:237
  59.5 44.0 %collective-permute-start.2 = (bf16[256,4096]{1,0:T(8,128)(2,1)}, bf16[256,4096]{1,0:T(8,128)(2,1)}, u32[]{:S(2)}, u32[]{:S(2)}) collective-permute-start(bf16[256,4096]{1,0:T(8,128)(2,1)} %collective-permute-done.1.refs_2_), channel_id=1, source_target_pairs={{0,8},{4,36},{8,16},{12,44},{16,24},{20,52},{24,0},{28,60},{32,40}... | collective-permute-start | bytes 6291464 | tf_op jit(solution)/shard_map/ppermute | solution.py:177
  92.1 28.9 %collective-permute-start.8 = (bf16[256,4096]{1,0:T(8,128)(2,1)}, bf16[256,4096]{1,0:T(8,128)(2,1)S(1)}, u32[]{:S(2)}, u32[]{:S(2)}) collective-permute-start(bf16[256,4096]{1,0:T(8,128)(2,1)} %collective-permute-done.7.refs_4_), channel_id=1, source_target_pairs={{0,24},{4,100},{8,0},{12,108},{16,8},{20,116},{24,16},{28,124},{32... | collective-permute-start | bytes 6291464 | tf_op jit(solution)/shard_map/ppermute | solution.py:177
  103.1 31.6 %collective-permute-start.23 = (bf16[256,4096]{1,0:T(8,128)(2,1)}, bf16[256,4096]{1,0:T(8,128)(2,1)S(1)}, u32[]{:S(2)}, u32[]{:S(2)}) collective-permute-start(bf16[256,4096]{1,0:T(8,128)(2,1)} %collective-permute-done.1.refs_2_), channel_id=1, source_target_pairs={{0,4},{4,0},{8,12},{12,8},{16,20},{20,16},{24,28},{28,24},{32,36},... | collective-permute-start | bytes 6291464 | tf_op jit(solution)/shard_map/ppermute | solution.py:178
  103.1 32.9 %collective-permute-start.24 = (bf16[256,4096]{1,0:T(8,128)(2,1)}, bf16[256,4096]{1,0:T(8,128)(2,1)S(1)}, u32[]{:S(2)}, u32[]{:S(2)}) collective-permute-start(bf16[256,4096]{1,0:T(8,128)(2,1)} %collective-permute-done.7.refs_4_), channel_id=1, source_target_pairs={{0,4},{4,0},{8,12},{12,8},{16,20},{20,16},{24,28},{28,24},{32,36},... | collective-permute-start | bytes 6291464 | tf_op jit(solution)/shard_map/ppermute | solution.py:178
  103.6 29.3 %collective-permute-start.20 = (bf16[8,2,32,384]{3,2,1,0:T(8,128)(2,1)}, bf16[8,2,32,384]{3,2,1,0:T(8,128)(2,1)S(1)}, u32[]{:S(2)}, u32[]{:S(2)}) collective-permute-start(bf16[8,2,32,384]{3,2,1,0:T(8,128)(2,1)} %gate_up.5.refs_1_), channel_id=1, source_target_pairs={{0,3},{1,0},{2,1},{3,2},{4,7},{5,4},{6,5},{7,6},{8,11},{9,8},{10,9... | collective-permute-start | bytes 1179656 | tf_op jit(solution)/shard_map/ppermute | solution.py:218
  105.4 70.1 %collective-permute-start.3 = (bf16[256,4096]{1,0:T(8,128)(2,1)}, bf16[256,4096]{1,0:T(8,128)(2,1)}, u32[]{:S(2)}, u32[]{:S(2)}) collective-permute-start(bf16[256,4096]{1,0:T(8,128)(2,1)} %collective-permute-done.2.refs_2_), channel_id=1, source_target_pairs={{0,4},{4,0},{8,12},{12,8},{16,20},{20,16},{24,28},{28,24},{32,36},... | collective-permute-start | bytes 6291464 | tf_op jit(solution)/shard_map/ppermute | solution.py:178
  121.0 55.0 %collective-permute-start.9 = (bf16[256,4096]{1,0:T(8,128)(2,1)S(1)}, bf16[256,4096]{1,0:T(8,128)(2,1)}, u32[]{:S(2)}, u32[]{:S(2)}) collective-permute-start(bf16[256,4096]{1,0:T(8,128)(2,1)S(1)} %collective-permute-done.8.refs_4_), channel_id=1, source_target_pairs={{0,4},{4,0},{8,12},{12,8},{16,20},{20,16},{24,28},{28,24},{32,36},... | collective-permute-start | bytes 6291464 | tf_op jit(solution)/shard_map/ppermute | solution.py:178
  169.4 86.5 %collective-permute-start.14 = (bf16[2,384,1024]{2,1,0:T(8,128)(2,1)}, bf16[2,384,1024]{2,1,0:T(8,128)(2,1)S(1)}, u32[]{:S(2)}, u32[]{:S(2)}) collective-permute-start(bf16[2,384,1024]{2,1,0:T(8,128)(2,1)} %get-tuple-element.6), channel_id=1, source_target_pairs={{0,1},{1,2},{2,3},{3,0},{4,5},{5,6},{6,7},{7,4},{8,9},{9,10},{10,1... | collective-permute-start | bytes 4718600 | tf_op jit(solution)/shard_map/ppermute | solution.py:218
  171.4 84.5 %collective-permute-start.15 = (bf16[2,384,1024]{2,1,0:T(8,128)(2,1)}, bf16[2,384,1024]{2,1,0:T(8,128)(2,1)S(1)}, u32[]{:S(2)}, u32[]{:S(2)}) collective-permute-start(bf16[2,384,1024]{2,1,0:T(8,128)(2,1)} %get-tuple-element.8), channel_id=1, source_target_pairs={{0,3},{1,0},{2,1},{3,2},{4,7},{5,4},{6,5},{7,6},{8,11},{9,8},{10,9... | collective-permute-start | bytes 4718600 | tf_op jit(solution)/shard_map/ppermute | solution.py:218
  172.6 83.3 %collective-permute-start.16 = (bf16[2,384,1024]{2,1,0:T(8,128)(2,1)}, bf16[2,384,1024]{2,1,0:T(8,128)(2,1)S(1)}, u32[]{:S(2)}, u32[]{:S(2)}) collective-permute-start(bf16[2,384,1024]{2,1,0:T(8,128)(2,1)} %get-tuple-element.5), channel_id=1, source_target_pairs={{0,2},{1,3},{2,0},{3,1},{4,6},{5,7},{6,4},{7,5},{8,10},{9,11},{10,... | collective-permute-start | bytes 4718600 | tf_op jit(solution)/shard_map/ppermute | solution.py:218
  175.4 67.3 %collective-permute-start.27 = (bf16[4,2,32,384]{3,2,1,0:T(8,128)(2,1)S(1)}, bf16[4,2,32,384]{3,2,1,0:T(8,128)(2,1)S(1)}, u32[]{:S(2)}, u32[]{:S(2)}) collective-permute-start(bf16[4,2,32,384]{3,2,1,0:T(8,128)(2,1)S(1)} %slice.80), channel_id=1, source_target_pairs={{0,1},{1,2},{2,3},{3,0},{4,5},{5,6},{6,7},{7,4},{8,9},{9,10},{10,1... | collective-permute-start | bytes 589832 | tf_op jit(solution)/shard_map/ppermute | solution.py:218
  176.0 67.1 %collective-permute-start.28 = (bf16[4,2,32,384]{3,2,1,0:T(8,128)(2,1)S(1)}, bf16[4,2,32,384]{3,2,1,0:T(8,128)(2,1)S(1)}, u32[]{:S(2)}, u32[]{:S(2)}) collective-permute-start(bf16[4,2,32,384]{3,2,1,0:T(8,128)(2,1)S(1)} %slice.81), channel_id=1, source_target_pairs={{0,3},{1,0},{2,1},{3,2},{4,7},{5,4},{6,5},{7,6},{8,11},{9,8},{10,9... | collective-permute-start | bytes 589832 | tf_op jit(solution)/shard_map/ppermute | solution.py:218
  252.2 18.5 %collective-permute-start.12 = (bf16[4,2,32,384]{3,2,1,0:T(8,128)(2,1)S(1)}, bf16[4,2,32,384]{3,2,1,0:T(8,128)(2,1)S(1)}, u32[]{:S(2)}, u32[]{:S(2)}) collective-permute-start(bf16[4,2,32,384]{3,2,1,0:T(8,128)(2,1)S(1)} %slice.76), channel_id=1, source_target_pairs={{0,1},{1,2},{2,3},{3,0},{4,5},{5,6},{6,7},{7,4},{8,9},{9,10},{10,1... | collective-permute-start | bytes 589832 | tf_op jit(solution)/shard_map/ppermute | solution.py:218
  252.3 18.4 %collective-permute-start.13 = (bf16[4,2,32,384]{3,2,1,0:T(8,128)(2,1)S(1)}, bf16[4,2,32,384]{3,2,1,0:T(8,128)(2,1)S(1)}, u32[]{:S(2)}, u32[]{:S(2)}) collective-permute-start(bf16[4,2,32,384]{3,2,1,0:T(8,128)(2,1)S(1)} %slice.77), channel_id=1, source_target_pairs={{0,3},{1,0},{2,1},{3,2},{4,7},{5,4},{6,5},{7,6},{8,11},{9,8},{10,9... | collective-permute-start | bytes 589832 | tf_op jit(solution)/shard_map/ppermute | solution.py:218
  278.9 60.2 %all-to-all-start.1 = ((bf16[32,2,32,1024]{3,2,1,0:T(8,128)(2,1)}), bf16[32,2,32,1024]{3,2,1,0:T(8,128)(2,1)}, u32[]{:S(2)}, u32[]{:S(2)}) async-start(bf16[32,2,32,1024]{3,2,1,0:T(8,128)(2,1)} %down.3), calls=%async_computation.1 | async-start | bytes 8388608 | tf_op jit(solution)/shard_map/all_to_all | solution.py:261
  (35 other events, 547.2 us)

commit v3 on v1

v3 whole, which is shorter than its diff:
```python
import jax
import jax.numpy as jnp
from jax import lax
from jax.experimental import pallas as pl
from jax.experimental.pallas import tpu as pltpu
from jax.sharding import PartitionSpec as P

MOST = 32
VMEM_BYTES = 60 * 1024 * 1024


def gate_up_body(group, slots, j, x_ref, q_ref, gate_ref, up_ref, out_ref, rows_ref):
    tok = x_ref.shape[0] // group
    width_all = x_ref.shape[1]
    place = lax.broadcasted_iota(jnp.int32, (slots, tok), 0)
    for b in range(group):
        pick = jnp.where(place == q_ref[b, j][None, :], 1.0, 0.0).astype(jnp.bfloat16)
        for c in range(0, width_all, 1024):
            rows_ref[b * slots : (b + 1) * slots, c : c + 1024] = jnp.dot(
                pick,
                x_ref[b * tok : (b + 1) * tok, c : c + 1024],
                preferred_element_type=jnp.float32,
            ).astype(jnp.bfloat16)
    hid = gate_ref.shape[-1]
    joined = jnp.concatenate([gate_ref[0], up_ref[0]], axis=1)
    both = jnp.dot(rows_ref[...], joined, preferred_element_type=jnp.float32)
    hidden = (jax.nn.silu(both[:, :hid]) * both[:, hid:]).astype(jnp.bfloat16)
    out_ref[...] = hidden.reshape(group, slots, hid)


def gate_up(x_all, q_in, gate_weight, up_weight, slots, j, group=8):
    sources, exp_local, tok = q_in.shape
    _, width_all, hid = gate_weight.shape
    weight_spec = pl.BlockSpec(
        (1, width_all, hid), lambda i: (j, 0, 0), pipeline_mode=pl.Buffered(1)
    )
    return pl.pallas_call(
        lambda *refs: gate_up_body(group, slots, j, *refs),
        out_shape=jax.ShapeDtypeStruct((sources, slots, hid), jnp.bfloat16),
        grid=(sources // group,),
        in_specs=[
            pl.BlockSpec((group * tok, width_all), lambda i: (i, 0)),
            pl.BlockSpec((group, exp_local, tok), lambda i: (i, 0, 0)),
            weight_spec,
            weight_spec,
        ],
        out_specs=pl.BlockSpec((group, slots, hid), lambda i: (i, 0, 0)),
        scratch_shapes=[pltpu.VMEM((group * slots, width_all), jnp.bfloat16)],
        compiler_params=pltpu.CompilerParams(vmem_limit_bytes=VMEM_BYTES),
        cost_estimate=pl.CostEstimate(
            flops=4 * sources * slots * width_all * hid,
            transcendentals=0,
            bytes_accessed=2 * (sources * tok * width_all + 2 * width_all * hid),
        ),
        name="gate_up",
    )(x_all, q_in, gate_weight, up_weight)


def down_body(*refs):
    hs, ws, out_ref = refs[:4], refs[4:8], refs[8]
    group, slots, hid = hs[0].shape
    rows = jnp.concatenate([h[...].reshape(group * slots, hid) for h in hs], axis=1)
    weight = jnp.concatenate([w[0] for w in ws], axis=0)
    total = jnp.dot(rows, weight, preferred_element_type=jnp.float32)
    out_ref[...] = total.astype(jnp.bfloat16).reshape(out_ref.shape)


def down(hidden, weights, j, group=8):
    sources, slots, hid = hidden[0].shape
    cols = weights[0].shape[-1]
    return pl.pallas_call(
        down_body,
        out_shape=jax.ShapeDtypeStruct((sources, slots, cols), jnp.bfloat16),
        grid=(sources // group,),
        in_specs=[pl.BlockSpec((group, slots, hid), lambda i: (i, 0, 0))] * 4
        + [pl.BlockSpec((1, hid, cols), lambda i: (j, 0, 0), pipeline_mode=pl.Buffered(1))] * 4,
        out_specs=pl.BlockSpec((group, slots, cols), lambda i: (i, 0, 0)),
        compiler_params=pltpu.CompilerParams(vmem_limit_bytes=VMEM_BYTES),
        cost_estimate=pl.CostEstimate(
            flops=8 * sources * slots * hid * cols,
            transcendentals=0,
            bytes_accessed=2 * (4 * sources * slots * hid + 4 * hid * cols + sources * slots * cols),
        ),
        name="down",
    )(*hidden, *weights)


def around(v, by):
    n = lax.axis_size("width")
    return lax.ppermute(v, "width", [(i, (i + by) % n) for i in range(n)])


def local(tokens, expert_ids, combine_weights, gate_weight, up_weight, down_weight):
    tok_rows = tokens.shape[0]
    exp_local = gate_weight.shape[0]
    n_expert = lax.axis_size("expert")
    experts_all = exp_local * n_expert
    slots = min(MOST, tok_rows)

    x_all = lax.all_gather(tokens, "expert", axis=0, tiled=True)

    experts = jnp.arange(experts_all, dtype=jnp.int32)
    hit = expert_ids.T[:, None, :] == experts[None, :, None]
    member = jnp.any(hit, axis=0)
    weight_of = jnp.sum(jnp.where(hit, combine_weights.T[:, None, :], 0.0), axis=0)
    order = jnp.arange(tok_rows, dtype=jnp.int32)
    earlier = (order[:, None] < order[None, :]).astype(jnp.bfloat16)
    rank = jnp.dot(member.astype(jnp.bfloat16), earlier, preferred_element_type=jnp.float32)
    place = jnp.where(member, rank.astype(jnp.int32), -1)
    q_in = lax.all_to_all(
        place.reshape(n_expert, exp_local, tok_rows), "expert", split_axis=0, concat_axis=0, tiled=True
    )
    seat = place[:, None, :] == jnp.arange(slots, dtype=jnp.int32)[None, :, None]
    spread = jnp.where(seat, weight_of[:, None, :], 0.0)
    spread = spread.reshape(n_expert, exp_local, slots, tok_rows)
    high = spread.astype(jnp.bfloat16)
    low = (spread - high.astype(jnp.float32)).astype(jnp.bfloat16)
    seats = jnp.concatenate([high, low], axis=3)

    n_width = lax.axis_size("width")
    cols = down_weight.shape[2] // n_width
    mine = lax.axis_index("width")
    cut = lambda by: lax.dynamic_slice_in_dim(down_weight, (mine + by) % n_width * cols, cols, 2)
    weights = [cut(0), around(cut(1), 1), around(cut(3), -1), around(cut(2), 2)]
    x_all, q_in, seats, *weights = lax.optimization_barrier((x_all, q_in, seats, *weights))

    mixed = jnp.zeros((2 * tok_rows, cols), jnp.float32)
    hidden = [gate_up(x_all, q_in, gate_weight, up_weight, slots, j) for j in range(exp_local)]
    rings = [[h, around(h, 1), around(h, -1), around(h, 2)] for h in hidden]
    rings[0], hidden[-1] = lax.optimization_barrier((rings[0], hidden[-1]))
    rings[-1][0] = hidden[-1]
    for j, ring in enumerate(rings):
        rows = down(ring, weights, j)
        returned = lax.all_to_all(rows, "expert", split_axis=0, concat_axis=0, tiled=True)
        mixed = mixed + lax.dot_general(
            seats[:, j].reshape(n_expert * slots, 2 * tok_rows),
            returned.reshape(n_expert * slots, cols),
            (((0,), (0,)), ((), ())),
            preferred_element_type=jnp.float32,
        )
    return (mixed[:tok_rows] + mixed[tok_rows:]).astype(jnp.bfloat16)


def solution(mesh):
    placed = (
        P("expert", None),
        P("expert", None),
        P("expert", None),
        P("expert", None, "width"),
        P("expert", None, "width"),
        P("expert", "width", None),
    )
    return jax.shard_map(
        local, mesh=mesh, in_specs=placed, out_specs=P("expert", "width"), check_vma=False
    )
```

time: 308 us -> 292 us (0.948)
  blocking collectives: 78.8 us -> 0 us
  waiting for transfers between devices: 130 us -> 175 us
  starting transfers between devices: 15.8 us -> 36.4 us
  local copies, waits for them, and re-layouts: 17.5 us -> 7.99 us
  Pallas kernels: 44 us -> 51.4 us
    ppermute x0 -> x9, waiting for transfers between devices: none -> 98.6 us  [around(): return lax.ppermute(v, 'width', [(i, (i + by) % n) for i in range(n)])]
    all_to_all x1 -> x0, blocking collectives: 78.8 us -> none  [local(): lax.all_to_all(cut, 'width', split_axis=0, concat_axis=0, tiled=True)]
    all_gather x1 -> x0, waiting for transfers between devices: 65.1 us -> none  [local(): h_all = lax.all_gather(hidden, 'width', axis=0, tiled=False)]
    all_gather x1, waiting for transfers between devices: 12.8 us -> 41.6 us  [local(): x_all = lax.all_gather(tokens, 'expert', axis=0, tiled=True)]
    all_to_all x1 -> x2, waiting for transfers between devices: 51.1 us -> 28.4 us  [local(): lax.all_to_all(rows, 'expert', split_axis=0, concat_axis=0, tiled=True)]
    ppermute x0 -> x9, starting transfers between devices: none -> 15.7 us  [around(): return lax.ppermute(v, 'width', [(i, (i + by) % n) for i in range(n)])]
    reshape x1 -> x0, local copies, waits for them, and re-layouts: 8.65 us -> none  [local(): down_weight.reshape(exp_local, hid, n_width, width_all // n_width)]
    pallas_call x2 -> x4, Pallas kernels: 44 us -> 51.4 us  [the longest x2 36.5 us: gate_up(): pl.pallas_call(lambda *refs: gate_up_body(group, slots, j, *refs), out_sh...]
  transfers between devices with their start and end apart: 4 -> 13, of which waited for: 3 -> 9; matrix products, arithmetic and copies ran while one was open for 7% -> 3% of each run, Pallas kernels for 0% -> 9%
where the time goes in v3:
time: 292 us; the launch traced here: 291 us
  waiting for transfers between devices  175 us (60%)
  Pallas kernels  51.4 us (18%)
  starting transfers between devices  36.4 us (12%)
  between operations  13.6 us (5%)
  local copies, waits for them, and re-layouts  7.99 us (3%)
  matrix products  3.98 us (1%)
    ppermute x9, waiting for transfers between devices, around(): return lax.ppermute(v, 'width', [(i, (i + by) % n) for i in range(n)])  98.6 us
    all_gather x1, waiting for transfers between devices, local(): x_all = lax.all_gather(tokens, 'expert', axis=0, tiled=True)  41.6 us
    pallas_call x2, Pallas kernels, gate_up(): pl.pallas_call(lambda *refs: gate_up_body(group, slots, j, *refs), out_sh...  36.5 us
    all_to_all x2, waiting for transfers between devices, local(): lax.all_to_all(rows, 'expert', split_axis=0, concat_axis=0, tiled=True)  28.4 us
    ppermute x9, starting transfers between devices, around(): return lax.ppermute(v, 'width', [(i, (i + by) % n) for i in range(n)])  15.7 us
    pallas_call x2, Pallas kernels, down(): pl.pallas_call(down_body, out_shape=jax.ShapeDtypeStruct((sources, slots,...  15 us
    all_to_all x2, starting transfers between devices, local(): lax.all_to_all(rows, 'expert', split_axis=0, concat_axis=0, tiled=True)  12.6 us
    all_to_all x1, starting transfers between devices, local(): lax.all_to_all(place.reshape(n_expert, exp_local, tok_rows), 'expert', sp...  8.16 us
  transfers between devices with their start and end apart: 13, of which 9 were waited for; matrix products, arithmetic and copies ran while one was open for 3% of the time, Pallas kernels for 9%

profile of v3, /device:TPU:0, one launch (start us, length us, event | category | flops | bytes accessed | tf_op | source)
XLA Modules:
  0.0 290.9 jit_solution(9770864492824400290)
XLA Ops:
  7.3 5.3 %constant_dynamic-slice_fusion = (bf16[2,384,1024]{2,1,0:T(8,128)(2,1)}, bf16[2,384,1024]{2,1,0:T(8,128)(2,1)}, bf16[2,384,1024]{2,1,0:T(8,128)(2,1)}, bf16[2,384,1024]{2,1,0:T(8,128)(2,1)S(1)}) fusion(bf16[2,384,4096]{2,1,0:T(8,128)(2,1)} %param.11, s32[]{:T(128)S(6)} %select_n.54, s32[]{:T(128)S(6)} %select_n.50, s32[]{:T(128)S(6)} %select_n.48, ...), kind=kLoop, calls=%fused_computation.14 | loop fusion | bytes 12582928 | tf_op jit(solution)/shard_map/dynamic_slice | solution.py:123
  12.7 3.3 %collective-permute-start.2 = (bf16[2,384,1024]{2,1,0:T(8,128)(2,1)}, bf16[2,384,1024]{2,1,0:T(8,128)(2,1)}, u32[]{:S(2)}, u32[]{:S(2)}) collective-permute-start(bf16[2,384,1024]{2,1,0:T(8,128)(2,1)} %get-tuple-element.29), channel_id=1, source_target_pairs={{0,2},{1,3},{2,0},{3,1},{4,6},{5,7},{6,4},{7,5},{8,10},{9,11},{10,... | collective-permute-start | bytes 4718600 | tf_op jit(solution)/shard_map/ppermute | solution.py:90
  16.6 2.6 collective-permute-start.1
  20.0 8.2 %all-to-all-start = ((s32[32,2,128]{2,1,0:T(2,128)}), s32[32,2,128]{2,1,0:T(2,128)S(1)}, u32[]{:S(2)}, u32[]{:S(2)}) async-start(s32[32,2,128]{2,1,0:T(2,128)} %bitcast.1), calls=%async_computation | async-start | bytes 65536 | tf_op jit(solution)/shard_map/all_to_all | solution.py:110
  28.2 1.0 fusion.1
  30.3 5.4 %all-to-all-done.refs_1_ = s32[32,2,128]{2,1,0:T(2,128)S(1)} async-done(((s32[32,2,128]{2,1,0:T(2,128)}), s32[32,2,128]{2,1,0:T(2,128)S(1)}, u32[]{:S(2)}, u32[]{:S(2)}) %all-to-all-start) | async-done | bytes 32800 | tf_op jit(solution)/shard_map/all_to_all | solution.py:110
  35.7 16.1 %collective-permute-done.2.refs_7_ = bf16[2,384,1024]{2,1,0:T(8,128)(2,1)} collective-permute-done((bf16[2,384,1024]{2,1,0:T(8,128)(2,1)}, bf16[2,384,1024]{2,1,0:T(8,128)(2,1)}, u32[]{:S(2)}, u32[]{:S(2)}) %collective-permute-start.2) | collective-permute-done | bytes 1572896 | tf_op jit(solution)/shard_map/ppermute | solution.py:90
  51.8 32.5 %collective-permute-done.refs_5_ = bf16[2,384,1024]{2,1,0:T(8,128)(2,1)} collective-permute-done((bf16[2,384,1024]{2,1,0:T(8,128)(2,1)}, bf16[2,384,1024]{2,1,0:T(8,128)(2,1)}, u32[]{:S(2)}, u32[]{:S(2)}) %collective-permute-start) | collective-permute-done | bytes 1572896 | tf_op jit(solution)/shard_map/ppermute | solution.py:90
  84.8 41.6 %all-gather.2.cloned.1.call-done.refs_0_ = bf16[4096,4096]{1,0:T(8,128)(2,1)} async-done(((bf16[128,4096]{1,0:T(8,128)(2,1)}), bf16[4096,4096]{1,0:T(8,128)(2,1)}) %all-gather.2.cloned.1.call-update) | async-done | bytes 33554448 | tf_op jit(solution)/shard_map/all_gather | solution.py:100
  126.4 18.2 %gate_up.2.refs_0_ = bf16[32,32,384]{2,1,0:T(8,128)(2,1)} custom-call(bf16[4096,4096]{1,0:T(8,128)(2,1)} %all-gather.2.cloned.1.call-done.refs_0_, s32[32,2,128]{2,1,0:T(2,128)} %copy-done, bf16[2,4096,384]{2,1,0:T(8,128)(2,1)} %refs_2_.3, bf16[2,4096,384]{2,1,0:T(8,128)(2,1)} %refs_3_.3), custom_call_target="tpu_custom_call" | custom-call | flops 6442450944 | bytes 39845888 | tf_op jit(solution)/shard_map/gate_up/pallas_call | solution.py:37
  144.6 3.0 %collective-permute-start.5 = (bf16[32,32,384]{2,1,0:T(8,128)(2,1)}, bf16[32,32,384]{2,1,0:T(8,128)(2,1)S(1)}, u32[]{:S(2)}, u32[]{:S(2)}) collective-permute-start(bf16[32,32,384]{2,1,0:T(8,128)(2,1)} %gate_up.2.refs_0_), channel_id=1, source_target_pairs={{0,2},{1,3},{2,0},{3,1},{4,6},{5,7},{6,4},{7,5},{8,10},{9,11},{10,... | collective-permute-start | bytes 2359304 | tf_op jit(solution)/shard_map/ppermute | solution.py:90
  147.6 1.1 collective-permute-start.4
  149.7 18.2 %gate_up.3.refs_0_ = bf16[32,32,384]{2,1,0:T(8,128)(2,1)} custom-call(bf16[4096,4096]{1,0:T(8,128)(2,1)} %all-gather.2.cloned.1.call-done.refs_0_, s32[32,2,128]{2,1,0:T(2,128)} %copy-done, bf16[2,4096,384]{2,1,0:T(8,128)(2,1)} %refs_2_.3, bf16[2,4096,384]{2,1,0:T(8,128)(2,1)} %refs_3_.3), custom_call_target="tpu_custom_call" | custom-call | flops 6442450944 | bytes 39845888 | tf_op jit(solution)/shard_map/gate_up/pallas_call | solution.py:37
  167.9 15.1 %collective-permute-done.4.refs_2_ = bf16[32,32,384]{2,1,0:T(8,128)(2,1)S(1)} collective-permute-done((bf16[32,32,384]{2,1,0:T(8,128)(2,1)}, bf16[32,32,384]{2,1,0:T(8,128)(2,1)S(1)}, u32[]{:S(2)}, u32[]{:S(2)}) %collective-permute-start.4) | collective-permute-done | bytes 786464 | tf_op jit(solution)/shard_map/ppermute | solution.py:90
  184.8 7.5 %down.2 = bf16[32,32,1024]{2,1,0:T(8,128)(2,1)} custom-call(bf16[32,32,384]{2,1,0:T(8,128)(2,1)} %gate_up.2.refs_0_, bf16[32,32,384]{2,1,0:T(8,128)(2,1)} %copy-done.5, bf16[32,32,384]{2,1,0:T(8,128)(2,1)} %copy-done.4, bf16[32,32,384]{2,1,0:T(8,128)(2,1)} %copy-done.3, bf16[2,384,1024]{2,1,0:T(8,128)(2,1)} %get-tuple-element.24.refs_4_, ...), custom_call_target="tpu_custom_call" | custom-call | flops 3221225472 | bytes 8388608 | tf_op jit(solution)/shard_map/down/pallas_call | solution.py:71
  192.3 5.2 %all-to-all-start.1 = ((bf16[32,32,1024]{2,1,0:T(8,128)(2,1)}), bf16[32,32,1024]{2,1,0:T(8,128)(2,1)S(1)}, u32[]{:S(2)}, u32[]{:S(2)}) async-start(bf16[32,32,1024]{2,1,0:T(8,128)(2,1)} %down.2), calls=%async_computation.1 | async-start | bytes 4194304 | tf_op jit(solution)/shard_map/all_to_all | solution.py:134
  197.5 2.1 collective-permute-start.8
  199.6 2.0 collective-permute-start.7
  201.6 18.2 %collective-permute-done.8.refs_3_ = bf16[32,32,384]{2,1,0:T(8,128)(2,1)} collective-permute-done((bf16[32,32,384]{2,1,0:T(8,128)(2,1)}, bf16[32,32,384]{2,1,0:T(8,128)(2,1)}, u32[]{:S(2)}, u32[]{:S(2)}) %collective-permute-start.8) | collective-permute-done | bytes 786464 | tf_op jit(solution)/shard_map/ppermute | solution.py:90
  219.8 16.2 %collective-permute-done.7.refs_2_ = bf16[32,32,384]{2,1,0:T(8,128)(2,1)} collective-permute-done((bf16[32,32,384]{2,1,0:T(8,128)(2,1)}, bf16[32,32,384]{2,1,0:T(8,128)(2,1)}, u32[]{:S(2)}, u32[]{:S(2)}) %collective-permute-start.7) | collective-permute-done | bytes 786464 | tf_op jit(solution)/shard_map/ppermute | solution.py:90
  235.9 7.5 %down.3 = bf16[32,32,1024]{2,1,0:T(8,128)(2,1)} custom-call(bf16[32,32,384]{2,1,0:T(8,128)(2,1)} %gate_up.3.refs_0_, bf16[32,32,384]{2,1,0:T(8,128)(2,1)} %collective-permute-done.6.refs_1_, bf16[32,32,384]{2,1,0:T(8,128)(2,1)} %collective-permute-done.7.refs_2_, bf16[32,32,384]{2,1,0:T(8,128)(2,1)} %collective-permute-done.8.refs_3_, ...), custom_call_target="tpu_custom_call" | custom-call | flops 3221225472 | bytes 8388608 | tf_op jit(solution)/shard_map/down/pallas_call | solution.py:71
  243.4 7.4 %all-to-all-start.2 = ((bf16[32,32,1024]{2,1,0:T(8,128)(2,1)}), bf16[32,32,1024]{2,1,0:T(8,128)(2,1)}, u32[]{:S(2)}, u32[]{:S(2)}) async-start(bf16[32,32,1024]{2,1,0:T(8,128)(2,1)} %down.3), calls=%async_computation.2 | async-start | bytes 4194304 | tf_op jit(solution)/shard_map/all_to_all | solution.py:134
  252.4 28.4 %all-to-all-done.2 = bf16[32,32,1024]{2,1,0:T(8,128)(2,1)} async-done(((bf16[32,32,1024]{2,1,0:T(8,128)(2,1)}), bf16[32,32,1024]{2,1,0:T(8,128)(2,1)}, u32[]{:S(2)}, u32[]{:S(2)}) %all-to-all-start.2) | async-done | bytes 2097184 | tf_op jit(solution)/shard_map/all_to_all | solution.py:134
  280.8 2.5 convolution_add_fusion
  (30 shorter events, 8.8 us)
Async XLA Ops:
  6.5 119.9 %all-gather.2.cloned.1.call-start = ((), (), s32[]{:S(2)}) async-start(), calls=%async_computation.3 | async-start | bytes 34603008 | tf_op jit(solution)/shard_map/all_gather | solution.py:100
  7.3 11.9 %copy-start.1 = (s32[128,8]{0,1:T(8,128)S(1)}, s32[128,8]{0,1:T(8,128)}, u32[]{:S(2)}) copy-start(s32[128,8]{0,1:T(8,128)} %param.7) | copy-start | bytes 12292
  7.3 20.8 %copy-start.2 = (f32[128,8]{0,1:T(8,128)S(1)}, f32[128,8]{0,1:T(8,128)}, u32[]{:S(2)}) copy-start(f32[128,8]{0,1:T(8,128)} %param.8) | copy-start | bytes 12292
  12.7 39.1 %collective-permute-start.2 = (bf16[2,384,1024]{2,1,0:T(8,128)(2,1)}, bf16[2,384,1024]{2,1,0:T(8,128)(2,1)}, u32[]{:S(2)}, u32[]{:S(2)}) collective-permute-start(bf16[2,384,1024]{2,1,0:T(8,128)(2,1)} %get-tuple-element.29), channel_id=1, source_target_pairs={{0,2},{1,3},{2,0},{3,1},{4,6},{5,7},{6,4},{7,5},{8,10},{9,11},{10,... | collective-permute-start | bytes 4718600 | tf_op jit(solution)/shard_map/ppermute | solution.py:90
  16.0 68.4 %collective-permute-start = (bf16[2,384,1024]{2,1,0:T(8,128)(2,1)}, bf16[2,384,1024]{2,1,0:T(8,128)(2,1)}, u32[]{:S(2)}, u32[]{:S(2)}) collective-permute-start(bf16[2,384,1024]{2,1,0:T(8,128)(2,1)} %get-tuple-element.30), channel_id=1, source_target_pairs={{0,1},{1,2},{2,3},{3,0},{4,5},{5,6},{6,7},{7,4},{8,9},{9,10},{10,1... | collective-permute-start | bytes 4718600 | tf_op jit(solution)/shard_map/ppermute | solution.py:90
  16.6 68.2 %collective-permute-start.1 = (bf16[2,384,1024]{2,1,0:T(8,128)(2,1)S(1)}, bf16[2,384,1024]{2,1,0:T(8,128)(2,1)}, u32[]{:S(2)}, u32[]{:S(2)}) collective-permute-start(bf16[2,384,1024]{2,1,0:T(8,128)(2,1)S(1)} %get-tuple-element.32), channel_id=1, source_target_pairs={{0,3},{1,0},{2,1},{3,2},{4,7},{5,4},{6,5},{7,6},{8,11},{9,8},{10,9... | collective-permute-start | bytes 4718600 | tf_op jit(solution)/shard_map/ppermute | solution.py:90
  20.0 15.7 %all-to-all-start = ((s32[32,2,128]{2,1,0:T(2,128)}), s32[32,2,128]{2,1,0:T(2,128)S(1)}, u32[]{:S(2)}, u32[]{:S(2)}) async-start(s32[32,2,128]{2,1,0:T(2,128)} %bitcast.1), calls=%async_computation | async-start | bytes 65536 | tf_op jit(solution)/shard_map/all_to_all | solution.py:110
  35.7 90.8 %copy-start = (s32[32,2,128]{2,1,0:T(2,128)}, s32[32,2,128]{2,1,0:T(2,128)S(1)}, u32[]{:S(2)}) copy-start(s32[32,2,128]{2,1,0:T(2,128)S(1)} %all-to-all-done.refs_1_) | copy-start | bytes 98308
  144.6 23.3 %collective-permute-start.5 = (bf16[32,32,384]{2,1,0:T(8,128)(2,1)}, bf16[32,32,384]{2,1,0:T(8,128)(2,1)S(1)}, u32[]{:S(2)}, u32[]{:S(2)}) collective-permute-start(bf16[32,32,384]{2,1,0:T(8,128)(2,1)} %gate_up.2.refs_0_), channel_id=1, source_target_pairs={{0,2},{1,3},{2,0},{3,1},{4,6},{5,7},{6,4},{7,5},{8,10},{9,11},{10,... | collective-permute-start | bytes 2359304 | tf_op jit(solution)/shard_map/ppermute | solution.py:90
  147.6 35.4 %collective-permute-start.4 = (bf16[32,32,384]{2,1,0:T(8,128)(2,1)}, bf16[32,32,384]{2,1,0:T(8,128)(2,1)S(1)}, u32[]{:S(2)}, u32[]{:S(2)}) collective-permute-start(bf16[32,32,384]{2,1,0:T(8,128)(2,1)} %gate_up.2.refs_0_), channel_id=1, source_target_pairs={{0,3},{1,0},{2,1},{3,2},{4,7},{5,4},{6,5},{7,6},{8,11},{9,8},{10,9... | collective-permute-start | bytes 2359304 | tf_op jit(solution)/shard_map/ppermute | solution.py:90
  148.8 34.2 %collective-permute-start.3 = (bf16[32,32,384]{2,1,0:T(8,128)(2,1)}, bf16[32,32,384]{2,1,0:T(8,128)(2,1)S(1)}, u32[]{:S(2)}, u32[]{:S(2)}) collective-permute-start(bf16[32,32,384]{2,1,0:T(8,128)(2,1)} %gate_up.2.refs_0_), channel_id=1, source_target_pairs={{0,1},{1,2},{2,3},{3,0},{4,5},{5,6},{6,7},{7,4},{8,9},{9,10},{10,1... | collective-permute-start | bytes 2359304 | tf_op jit(solution)/shard_map/ppermute | solution.py:90
  167.9 15.1 %copy-start.3 = (bf16[32,32,384]{2,1,0:T(8,128)(2,1)}, bf16[32,32,384]{2,1,0:T(8,128)(2,1)S(1)}, u32[]{:S(2)}) copy-start(bf16[32,32,384]{2,1,0:T(8,128)(2,1)S(1)} %collective-permute-done.5.refs_3_) | copy-start | bytes 2359300
  183.0 0.9 copy-start.4
  183.9 0.9 copy-start.5
  192.3 51.1 %all-to-all-start.1 = ((bf16[32,32,1024]{2,1,0:T(8,128)(2,1)}), bf16[32,32,1024]{2,1,0:T(8,128)(2,1)S(1)}, u32[]{:S(2)}, u32[]{:S(2)}) async-start(bf16[32,32,1024]{2,1,0:T(8,128)(2,1)} %down.2), calls=%async_computation.1 | async-start | bytes 4194304 | tf_op jit(solution)/shard_map/all_to_all | solution.py:134
  197.5 22.3 %collective-permute-start.8 = (bf16[32,32,384]{2,1,0:T(8,128)(2,1)}, bf16[32,32,384]{2,1,0:T(8,128)(2,1)}, u32[]{:S(2)}, u32[]{:S(2)}) collective-permute-start(bf16[32,32,384]{2,1,0:T(8,128)(2,1)} %gate_up.3.refs_0_), channel_id=1, source_target_pairs={{0,2},{1,3},{2,0},{3,1},{4,6},{5,7},{6,4},{7,5},{8,10},{9,11},{10,... | collective-permute-start | bytes 2359304 | tf_op jit(solution)/shard_map/ppermute | solution.py:90
  199.6 36.4 %collective-permute-start.7 = (bf16[32,32,384]{2,1,0:T(8,128)(2,1)}, bf16[32,32,384]{2,1,0:T(8,128)(2,1)}, u32[]{:S(2)}, u32[]{:S(2)}) collective-permute-start(bf16[32,32,384]{2,1,0:T(8,128)(2,1)} %gate_up.3.refs_0_), channel_id=1, source_target_pairs={{0,3},{1,0},{2,1},{3,2},{4,7},{5,4},{6,5},{7,6},{8,11},{9,8},{10,9... | collective-permute-start | bytes 2359304 | tf_op jit(solution)/shard_map/ppermute | solution.py:90
  201.6 34.4 %collective-permute-start.6 = (bf16[32,32,384]{2,1,0:T(8,128)(2,1)}, bf16[32,32,384]{2,1,0:T(8,128)(2,1)}, u32[]{:S(2)}, u32[]{:S(2)}) collective-permute-start(bf16[32,32,384]{2,1,0:T(8,128)(2,1)} %gate_up.3.refs_0_), channel_id=1, source_target_pairs={{0,1},{1,2},{2,3},{3,0},{4,5},{5,6},{6,7},{7,4},{8,9},{9,10},{10,1... | collective-permute-start | bytes 2359304 | tf_op jit(solution)/shard_map/ppermute | solution.py:90
  243.4 37.4 %all-to-all-start.2 = ((bf16[32,32,1024]{2,1,0:T(8,128)(2,1)}), bf16[32,32,1024]{2,1,0:T(8,128)(2,1)}, u32[]{:S(2)}, u32[]{:S(2)}) async-start(bf16[32,32,1024]{2,1,0:T(8,128)(2,1)} %down.3), calls=%async_computation.2 | async-start | bytes 4194304 | tf_op jit(solution)/shard_map/all_to_all | solution.py:134
Sparse Core Ops, SparseCore 0:
  9.6 116.7 all-gather.1

commit v4 on v3

--- a/solution.py
+++ b/solution.py
@@ -56,25 +56,50 @@
     )(x_all, q_in, gate_weight, up_weight)
 
 
-def down_body(*refs):
-    hs, ws, out_ref = refs[:4], refs[4:8], refs[8]
+def down_body(half_steps, *refs):
+    hs, far, ws, out_ref, far_ref = refs[:3], refs[3:5], refs[5:9], refs[9], refs[10]
     group, slots, hid = hs[0].shape
-    rows = jnp.concatenate([h[...].reshape(group * slots, hid) for h in hs], axis=1)
+
+    @pl.when(pl.program_id(0) < half_steps)
+    def _():
+        far_ref[...] = far[0][...]
+
+    @pl.when(pl.program_id(0) >= half_steps)
+    def _():
+        far_ref[...] = far[1][...]
+
+    rows = jnp.concatenate(
+        [h[...].reshape(group * slots, hid) for h in (*hs, far_ref)], axis=1
+    )
     weight = jnp.concatenate([w[0] for w in ws], axis=0)
     total = jnp.dot(rows, weight, preferred_element_type=jnp.float32)
     out_ref[...] = total.astype(jnp.bfloat16).reshape(out_ref.shape)
 
 
-def down(hidden, weights, j, group=8):
-    sources, slots, hid = hidden[0].shape
+def down(ring, weights, j, group=8):
+    own, fore, back, (far_low, far_high) = ring
+    sources, slots, hid = own.shape
     cols = weights[0].shape[-1]
+    steps = sources // group
+    half = steps // 2
+    low_at = far_low.shape[0] // group - half
+    high_at = far_high.shape[0] // group - half
+    spec = pl.BlockSpec((group, slots, hid), lambda i: (i, 0, 0))
+    low_spec = pl.BlockSpec(
+        (group, slots, hid), lambda i: (low_at + jnp.minimum(i, half - 1), 0, 0)
+    )
+    high_spec = pl.BlockSpec(
+        (group, slots, hid), lambda i: (high_at + jnp.maximum(i - half, 0), 0, 0)
+    )
     return pl.pallas_call(
-        down_body,
+        lambda *refs: down_body(half, *refs),
         out_shape=jax.ShapeDtypeStruct((sources, slots, cols), jnp.bfloat16),
-        grid=(sources // group,),
-        in_specs=[pl.BlockSpec((group, slots, hid), lambda i: (i, 0, 0))] * 4
+        grid=(steps,),
+        in_specs=[spec] * 3
+        + [low_spec, high_spec]
         + [pl.BlockSpec((1, hid, cols), lambda i: (j, 0, 0), pipeline_mode=pl.Buffered(1))] * 4,
         out_specs=pl.BlockSpec((group, slots, cols), lambda i: (i, 0, 0)),
+        scratch_shapes=[pltpu.VMEM((group, slots, hid), jnp.bfloat16)],
         compiler_params=pltpu.CompilerParams(vmem_limit_bytes=VMEM_BYTES),
         cost_estimate=pl.CostEstimate(
             flops=8 * sources * slots * hid * cols,
@@ -82,7 +107,7 @@
             bytes_accessed=2 * (4 * sources * slots * hid + 4 * hid * cols + sources * slots * cols),
         ),
         name="down",
-    )(*hidden, *weights)
+    )(own, fore, back, far_low, far_high, *weights)
 
 
 def around(v, by):
@@ -126,9 +151,14 @@
 
     mixed = jnp.zeros((2 * tok_rows, cols), jnp.float32)
     hidden = [gate_up(x_all, q_in, gate_weight, up_weight, slots, j) for j in range(exp_local)]
-    rings = [[h, around(h, 1), around(h, -1), around(h, 2)] for h in hidden]
-    rings[0], hidden[-1] = lax.optimization_barrier((rings[0], hidden[-1]))
-    rings[-1][0] = hidden[-1]
+    half = n_expert // 2
+    first, last = hidden
+    fore, back = around(first, 1), around(first, -1)
+    fore, back, last = lax.optimization_barrier((fore, back, last))
+    ahead = around(jnp.concatenate([last, fore[:half]], axis=0), 1)
+    behind = around(jnp.concatenate([last, back[half:]], axis=0), -1)
+    rings = [[first, fore, back, (ahead, behind)]]
+    rings.append([last, ahead, behind, (around(ahead[:half], 1), around(behind[half:n_expert], -1))])
     for j, ring in enumerate(rings):
         rows = down(ring, weights, j)
         returned = lax.all_to_all(rows, "expert", split_axis=0, concat_axis=0, tiled=True)

time: 292 us -> 298 us (1.021)
  waiting for transfers between devices: 175 us -> 180 us
    all_to_all x2, waiting for transfers between devices: 28.4 us -> 50.5 us  [local(): lax.all_to_all(rows, 'expert', split_axis=0, concat_axis=0, tiled=True)]
    ppermute x9, waiting for transfers between devices: 98.6 us -> 84.1 us  [around(): return lax.ppermute(v, 'width', [(i, (i + by) % n) for i in range(n)])]
  transfers between devices with their start and end apart: 13 -> 13, of which waited for: 9 -> 9; matrix products, arithmetic and copies ran while one was open for 3% -> 4% of each run, Pallas kernels for 9% -> 9%
where the time goes in v4:
time: 298 us; the launch traced here: 297 us
  waiting for transfers between devices  180 us (60%)
  Pallas kernels  51.7 us (17%)
  starting transfers between devices  33.5 us (11%)
  between operations  13.6 us (5%)
  local copies, waits for them, and re-layouts  9.99 us (3%)
  other arithmetic  4.07 us (1%)
  matrix products  3.97 us (1%)
    ppermute x9, waiting for transfers between devices, around(): return lax.ppermute(v, 'width', [(i, (i + by) % n) for i in range(n)])  84.1 us
    all_to_all x2, waiting for transfers between devices, local(): lax.all_to_all(rows, 'expert', split_axis=0, concat_axis=0, tiled=True)  50.5 us
    all_gather x1, waiting for transfers between devices, local(): x_all = lax.all_gather(tokens, 'expert', axis=0, tiled=True)  40.4 us
    pallas_call x2, Pallas kernels, gate_up(): pl.pallas_call(lambda *refs: gate_up_body(group, slots, j, *refs), out_sh...  36.4 us
    ppermute x9, starting transfers between devices, around(): return lax.ppermute(v, 'width', [(i, (i + by) % n) for i in range(n)])  15.3 us
    pallas_call x2, Pallas kernels, down(): pl.pallas_call(lambda *refs: down_body(half, *refs), out_shape=jax.ShapeD...  15.2 us
    all_to_all x2, starting transfers between devices, local(): lax.all_to_all(rows, 'expert', split_axis=0, concat_axis=0, tiled=True)  10.1 us
    all_to_all x1, starting transfers between devices, local(): lax.all_to_all(place.reshape(n_expert, exp_local, tok_rows), 'expert', sp...  8.16 us
  transfers between devices with their start and end apart: 13, of which 9 were waited for; matrix products, arithmetic and copies ran while one was open for 4% of the time, Pallas kernels for 9%

profile of v4, /device:TPU:0, one launch (start us, length us, event | category | flops | bytes accessed | tf_op | source)
XLA Modules:
  0.0 297.1 jit_solution(17590669743650638388)
XLA Ops:
  7.3 6.0 %constant_dynamic-slice_fusion = (bf16[2,384,1024]{2,1,0:T(8,128)(2,1)}, bf16[2,384,1024]{2,1,0:T(8,128)(2,1)}, bf16[2,384,1024]{2,1,0:T(8,128)(2,1)}, bf16[2,384,1024]{2,1,0:T(8,128)(2,1)}) fusion(bf16[2,384,4096]{2,1,0:T(8,128)(2,1)} %param.11, s32[]{:T(128)S(6)} %select_n.54, s32[]{:T(128)S(6)} %select_n.50, s32[]{:T(128)S(6)} %select_n.48, s32[]{:T(128)S(6)} %select_n.52), kind=kLoop, calls=%fused_computation.16 | loop fusion | bytes 12582928 | tf_op jit(solution)/shard_map/dynamic_slice | solution.py:148
  13.4 1.7 collective-permute-start
  15.0 1.6 collective-permute-start.1
  16.6 2.1 collective-permute-start.2
  19.5 8.2 %all-to-all-start = ((s32[32,2,128]{2,1,0:T(2,128)}), s32[32,2,128]{2,1,0:T(2,128)S(1)}, u32[]{:S(2)}, u32[]{:S(2)}) async-start(s32[32,2,128]{2,1,0:T(2,128)} %bitcast.1), calls=%async_computation | async-start | bytes 65536 | tf_op jit(solution)/shard_map/all_to_all | solution.py:135
  30.7 4.4 %all-to-all-done.refs_1_ = s32[32,2,128]{2,1,0:T(2,128)S(1)} async-done(((s32[32,2,128]{2,1,0:T(2,128)}), s32[32,2,128]{2,1,0:T(2,128)S(1)}, u32[]{:S(2)}, u32[]{:S(2)}) %all-to-all-start) | async-done | bytes 32800 | tf_op jit(solution)/shard_map/all_to_all | solution.py:135
  35.2 15.9 %collective-permute-done.refs_6_ = bf16[2,384,1024]{2,1,0:T(8,128)(2,1)S(1)} collective-permute-done((bf16[2,384,1024]{2,1,0:T(8,128)(2,1)}, bf16[2,384,1024]{2,1,0:T(8,128)(2,1)S(1)}, u32[]{:S(2)}, u32[]{:S(2)}) %collective-permute-start) | collective-permute-done | bytes 1572896 | tf_op jit(solution)/shard_map/ppermute | solution.py:115
  52.5 33.5 %collective-permute-done.2.refs_8_ = bf16[2,384,1024]{2,1,0:T(8,128)(2,1)} collective-permute-done((bf16[2,384,1024]{2,1,0:T(8,128)(2,1)}, bf16[2,384,1024]{2,1,0:T(8,128)(2,1)}, u32[]{:S(2)}, u32[]{:S(2)}) %collective-permute-start.2) | collective-permute-done | bytes 1572896 | tf_op jit(solution)/shard_map/ppermute | solution.py:115
  86.0 40.4 %all-gather.2.cloned.1.call-done.refs_0_ = bf16[4096,4096]{1,0:T(8,128)(2,1)} async-done(((bf16[128,4096]{1,0:T(8,128)(2,1)}), bf16[4096,4096]{1,0:T(8,128)(2,1)}) %all-gather.2.cloned.1.call-update) | async-done | bytes 33554448 | tf_op jit(solution)/shard_map/all_gather | solution.py:125
  126.4 18.2 %gate_up.2.refs_0_ = bf16[32,32,384]{2,1,0:T(8,128)(2,1)} custom-call(bf16[4096,4096]{1,0:T(8,128)(2,1)} %all-gather.2.cloned.1.call-done.refs_0_, s32[32,2,128]{2,1,0:T(2,128)} %copy-done.9, bf16[2,4096,384]{2,1,0:T(8,128)(2,1)} %refs_2_.3, bf16[2,4096,384]{2,1,0:T(8,128)(2,1)} %refs_3_.3), custom_call_target="tpu_custom_call" | custom-call | flops 6442450944 | bytes 39845888 | tf_op jit(solution)/shard_map/gate_up/pallas_call | solution.py:37
  144.6 1.6 collective-permute-start.3
  146.2 1.8 collective-permute-start.4
  148.0 18.2 %gate_up.3.refs_0_ = bf16[32,32,384]{2,1,0:T(8,128)(2,1)} custom-call(bf16[4096,4096]{1,0:T(8,128)(2,1)} %all-gather.2.cloned.1.call-done.refs_0_, s32[32,2,128]{2,1,0:T(2,128)} %copy-done.9, bf16[2,4096,384]{2,1,0:T(8,128)(2,1)} %refs_2_.3, bf16[2,4096,384]{2,1,0:T(8,128)(2,1)} %refs_3_.3), custom_call_target="tpu_custom_call" | custom-call | flops 6442450944 | bytes 39845888 | tf_op jit(solution)/shard_map/gate_up/pallas_call | solution.py:37
  169.0 2.3 collective-permute-start.6
  171.2 25.5 %collective-permute-done.5.refs_3_.refs_1_ = bf16[48,32,384]{2,1,0:T(8,128)(2,1)S(1)} collective-permute-done((bf16[48,32,384]{2,1,0:T(8,128)(2,1)S(1)}, bf16[48,32,384]{2,1,0:T(8,128)(2,1)S(1)}, u32[]{:S(2)}, u32[]{:S(2)}) %collective-permute-start.5) | collective-permute-done | bytes 1179680 | tf_op jit(solution)/shard_map/ppermute | solution.py:115
  197.0 3.3 %collective-permute-start.8 = (bf16[16,32,384]{2,1,0:T(8,128)(2,1)S(1)}, bf16[16,32,384]{2,1,0:T(8,128)(2,1)S(1)}, u32[]{:S(2)}, u32[]{:S(2)}) collective-permute-start(bf16[16,32,384]{2,1,0:T(8,128)(2,1)S(1)} %slice.33), channel_id=1, source_target_pairs={{0,3},{1,0},{2,1},{3,2},{4,7},{5,4},{6,5},{7,6},{8,11},{9,8},{10,9... | collective-permute-start | bytes 1179656 | tf_op jit(solution)/shard_map/ppermute | solution.py:115
  200.3 7.7 %collective-permute-done.7.refs_3_ = bf16[16,32,384]{2,1,0:T(8,128)(2,1)S(1)} collective-permute-done((bf16[16,32,384]{2,1,0:T(8,128)(2,1)S(1)}, bf16[16,32,384]{2,1,0:T(8,128)(2,1)S(1)}, u32[]{:S(2)}, u32[]{:S(2)}) %collective-permute-start.7) | collective-permute-done | bytes 393248 | tf_op jit(solution)/shard_map/ppermute | solution.py:115
  209.4 7.6 %down.3 = bf16[32,32,1024]{2,1,0:T(8,128)(2,1)} custom-call(bf16[32,32,384]{2,1,0:T(8,128)(2,1)} %gate_up.3.refs_0_, bf16[48,32,384]{2,1,0:T(8,128)(2,1)} %copy-done.1, bf16[48,32,384]{2,1,0:T(8,128)(2,1)} %copy-done.2, bf16[16,32,384]{2,1,0:T(8,128)(2,1)} %copy-done.7, bf16[16,32,384]{2,1,0:T(8,128)(2,1)} %copy-done.8, ...), custom_call_target="tpu_custom_call" | custom-call | flops 3221225472 | bytes 8388608 | tf_op jit(solution)/shard_map/down/pallas_call | solution.py:94
  217.1 5.4 %all-to-all-start.2 = ((bf16[32,32,1024]{2,1,0:T(8,128)(2,1)}), bf16[32,32,1024]{2,1,0:T(8,128)(2,1)S(1)}, u32[]{:S(2)}, u32[]{:S(2)}) async-start(bf16[32,32,1024]{2,1,0:T(8,128)(2,1)} %down.3), calls=%async_computation.2 | async-start | bytes 4194304 | tf_op jit(solution)/shard_map/all_to_all | solution.py:164
  222.4 7.6 %down.2 = bf16[32,32,1024]{2,1,0:T(8,128)(2,1)} custom-call(bf16[32,32,384]{2,1,0:T(8,128)(2,1)} %gate_up.2.refs_0_, bf16[32,32,384]{2,1,0:T(8,128)(2,1)} %collective-permute-done.3.refs_1_, bf16[32,32,384]{2,1,0:T(8,128)(2,1)} %copy-done.6, bf16[48,32,384]{2,1,0:T(8,128)(2,1)} %copy-done.1, bf16[48,32,384]{2,1,0:T(8,128)(2,1)} %copy-done.2, ...), custom_call_target="tpu_custom_call" | custom-call | flops 3221225472 | bytes 8388608 | tf_op jit(solution)/shard_map/down/pallas_call | solution.py:94
  230.0 22.2 %all-to-all-done.2 = bf16[32,32,1024]{2,1,0:T(8,128)(2,1)S(1)} async-done(((bf16[32,32,1024]{2,1,0:T(8,128)(2,1)}), bf16[32,32,1024]{2,1,0:T(8,128)(2,1)S(1)}, u32[]{:S(2)}, u32[]{:S(2)}) %all-to-all-start.2) | async-done | bytes 2097184 | tf_op jit(solution)/shard_map/all_to_all | solution.py:164
  252.2 4.8 %all-to-all-start.1 = ((bf16[32,32,1024]{2,1,0:T(8,128)(2,1)}), bf16[32,32,1024]{2,1,0:T(8,128)(2,1)}, u32[]{:S(2)}, u32[]{:S(2)}) async-start(bf16[32,32,1024]{2,1,0:T(8,128)(2,1)} %down.2), calls=%async_computation.1 | async-start | bytes 4194304 | tf_op jit(solution)/shard_map/all_to_all | solution.py:164
  258.6 28.3 %all-to-all-done.1 = bf16[32,32,1024]{2,1,0:T(8,128)(2,1)} async-done(((bf16[32,32,1024]{2,1,0:T(8,128)(2,1)}), bf16[32,32,1024]{2,1,0:T(8,128)(2,1)}, u32[]{:S(2)}, u32[]{:S(2)}) %all-to-all-start.1) | async-done | bytes 2097184 | tf_op jit(solution)/shard_map/all_to_all | solution.py:164
  286.9 2.5 convolution_add_fusion
  (47 shorter events, 12.9 us)
Async XLA Ops:
  6.5 119.9 %all-gather.2.cloned.1.call-start = ((), (), s32[]{:S(2)}) async-start(), calls=%async_computation.3 | async-start | bytes 34603008 | tf_op jit(solution)/shard_map/all_gather | solution.py:125
  7.3 11.3 %copy-start.10 = (s32[128,8]{0,1:T(8,128)S(1)}, s32[128,8]{0,1:T(8,128)}, u32[]{:S(2)}) copy-start(s32[128,8]{0,1:T(8,128)} %param.7) | copy-start | bytes 12292
  7.3 20.3 %copy-start.11 = (f32[128,8]{0,1:T(8,128)S(1)}, f32[128,8]{0,1:T(8,128)}, u32[]{:S(2)}) copy-start(f32[128,8]{0,1:T(8,128)} %param.8) | copy-start | bytes 12292
  13.4 37.7 %collective-permute-start = (bf16[2,384,1024]{2,1,0:T(8,128)(2,1)}, bf16[2,384,1024]{2,1,0:T(8,128)(2,1)S(1)}, u32[]{:S(2)}, u32[]{:S(2)}) collective-permute-start(bf16[2,384,1024]{2,1,0:T(8,128)(2,1)} %get-tuple-element.26), channel_id=1, source_target_pairs={{0,1},{1,2},{2,3},{3,0},{4,5},{5,6},{6,7},{7,4},{8,9},{9,10},{10,1... | collective-permute-start | bytes 4718600 | tf_op jit(solution)/shard_map/ppermute | solution.py:115
  15.0 37.5 %collective-permute-start.1 = (bf16[2,384,1024]{2,1,0:T(8,128)(2,1)}, bf16[2,384,1024]{2,1,0:T(8,128)(2,1)S(1)}, u32[]{:S(2)}, u32[]{:S(2)}) collective-permute-start(bf16[2,384,1024]{2,1,0:T(8,128)(2,1)} %get-tuple-element.28), channel_id=1, source_target_pairs={{0,3},{1,0},{2,1},{3,2},{4,7},{5,4},{6,5},{7,6},{8,11},{9,8},{10,9... | collective-permute-start | bytes 4718600 | tf_op jit(solution)/shard_map/ppermute | solution.py:115
  16.6 69.5 %collective-permute-start.2 = (bf16[2,384,1024]{2,1,0:T(8,128)(2,1)}, bf16[2,384,1024]{2,1,0:T(8,128)(2,1)}, u32[]{:S(2)}, u32[]{:S(2)}) collective-permute-start(bf16[2,384,1024]{2,1,0:T(8,128)(2,1)} %get-tuple-element.25), channel_id=1, source_target_pairs={{0,2},{1,3},{2,0},{3,1},{4,6},{5,7},{6,4},{7,5},{8,10},{9,11},{10,... | collective-permute-start | bytes 4718600 | tf_op jit(solution)/shard_map/ppermute | solution.py:115
  19.5 15.7 %all-to-all-start = ((s32[32,2,128]{2,1,0:T(2,128)}), s32[32,2,128]{2,1,0:T(2,128)S(1)}, u32[]{:S(2)}, u32[]{:S(2)}) async-start(s32[32,2,128]{2,1,0:T(2,128)} %bitcast.1), calls=%async_computation | async-start | bytes 65536 | tf_op jit(solution)/shard_map/all_to_all | solution.py:135
  35.2 91.3 %copy-start.9 = (s32[32,2,128]{2,1,0:T(2,128)}, s32[32,2,128]{2,1,0:T(2,128)S(1)}, u32[]{:S(2)}) copy-start(s32[32,2,128]{2,1,0:T(2,128)S(1)} %all-to-all-done.refs_1_) | copy-start | bytes 98308
  51.1 93.6 %copy-start.3 = (bf16[2,384,1024]{2,1,0:T(8,128)(2,1)}, bf16[2,384,1024]{2,1,0:T(8,128)(2,1)S(1)}, u32[]{:S(2)}) copy-start(bf16[2,384,1024]{2,1,0:T(8,128)(2,1)S(1)} %collective-permute-done.refs_6_) | copy-start | bytes 4718596
  52.5 92.1 %copy-start.4 = (bf16[2,384,1024]{2,1,0:T(8,128)(2,1)}, bf16[2,384,1024]{2,1,0:T(8,128)(2,1)S(1)}, u32[]{:S(2)}) copy-start(bf16[2,384,1024]{2,1,0:T(8,128)(2,1)S(1)} %collective-permute-done.1.refs_7_) | copy-start | bytes 4718596
  144.6 21.5 %collective-permute-start.3 = (bf16[32,32,384]{2,1,0:T(8,128)(2,1)}, bf16[32,32,384]{2,1,0:T(8,128)(2,1)}, u32[]{:S(2)}, u32[]{:S(2)}) collective-permute-start(bf16[32,32,384]{2,1,0:T(8,128)(2,1)} %gate_up.2.refs_0_), channel_id=1, source_target_pairs={{0,1},{1,2},{2,3},{3,0},{4,5},{5,6},{6,7},{7,4},{8,9},{9,10},{10,1... | collective-permute-start | bytes 2359304 | tf_op jit(solution)/shard_map/ppermute | solution.py:115
  146.2 20.0 %collective-permute-start.4 = (bf16[32,32,384]{2,1,0:T(8,128)(2,1)}, bf16[32,32,384]{2,1,0:T(8,128)(2,1)S(1)}, u32[]{:S(2)}, u32[]{:S(2)}) collective-permute-start(bf16[32,32,384]{2,1,0:T(8,128)(2,1)} %gate_up.2.refs_0_), channel_id=1, source_target_pairs={{0,3},{1,0},{2,1},{3,2},{4,7},{5,4},{6,5},{7,6},{8,11},{9,8},{10,9... | collective-permute-start | bytes 2359304 | tf_op jit(solution)/shard_map/ppermute | solution.py:115
  166.2 1.5 copy-start
  166.2 1.7 copy-start.6
  167.9 28.9 %collective-permute-start.5 = (bf16[48,32,384]{2,1,0:T(8,128)(2,1)S(1)}, bf16[48,32,384]{2,1,0:T(8,128)(2,1)S(1)}, u32[]{:S(2)}, u32[]{:S(2)}) collective-permute-start(bf16[48,32,384]{2,1,0:T(8,128)(2,1)S(1)} %get-tuple-element.32), channel_id=1, source_target_pairs={{0,1},{1,2},{2,3},{3,0},{4,5},{5,6},{6,7},{7,4},{8,9},{9,10},{10,1... | collective-permute-start | bytes 3538952 | tf_op jit(solution)/shard_map/ppermute | solution.py:115
  169.0 27.9 %collective-permute-start.6 = (bf16[48,32,384]{2,1,0:T(8,128)(2,1)S(1)}, bf16[48,32,384]{2,1,0:T(8,128)(2,1)S(1)}, u32[]{:S(2)}, u32[]{:S(2)}) collective-permute-start(bf16[48,32,384]{2,1,0:T(8,128)(2,1)S(1)} %get-tuple-element.31), channel_id=1, source_target_pairs={{0,3},{1,0},{2,1},{3,2},{4,7},{5,4},{6,5},{7,6},{8,11},{9,8},{10,9... | collective-permute-start | bytes 3538952 | tf_op jit(solution)/shard_map/ppermute | solution.py:115
  196.8 11.2 %copy-start.1 = (bf16[48,32,384]{2,1,0:T(8,128)(2,1)}, bf16[48,32,384]{2,1,0:T(8,128)(2,1)S(1)}, u32[]{:S(2)}) copy-start(bf16[48,32,384]{2,1,0:T(8,128)(2,1)S(1)} %collective-permute-done.5.refs_3_.refs_1_) | copy-start | bytes 3538948
  196.8 11.1 %collective-permute-start.7 = (bf16[16,32,384]{2,1,0:T(8,128)(2,1)S(1)}, bf16[16,32,384]{2,1,0:T(8,128)(2,1)S(1)}, u32[]{:S(2)}, u32[]{:S(2)}) collective-permute-start(bf16[16,32,384]{2,1,0:T(8,128)(2,1)S(1)} %slice.32), channel_id=1, source_target_pairs={{0,1},{1,2},{2,3},{3,0},{4,5},{5,6},{6,7},{7,4},{8,9},{9,10},{10,1... | collective-permute-start | bytes 1179656 | tf_op jit(solution)/shard_map/ppermute | solution.py:115
  196.9 11.0 %copy-start.2 = (bf16[48,32,384]{2,1,0:T(8,128)(2,1)}, bf16[48,32,384]{2,1,0:T(8,128)(2,1)S(1)}, u32[]{:S(2)}) copy-start(bf16[48,32,384]{2,1,0:T(8,128)(2,1)S(1)} %collective-permute-done.6.refs_4_.refs_2_) | copy-start | bytes 3538948
  197.0 11.0 %collective-permute-start.8 = (bf16[16,32,384]{2,1,0:T(8,128)(2,1)S(1)}, bf16[16,32,384]{2,1,0:T(8,128)(2,1)S(1)}, u32[]{:S(2)}, u32[]{:S(2)}) collective-permute-start(bf16[16,32,384]{2,1,0:T(8,128)(2,1)S(1)} %slice.33), channel_id=1, source_target_pairs={{0,3},{1,0},{2,1},{3,2},{4,7},{5,4},{6,5},{7,6},{8,11},{9,8},{10,9... | collective-permute-start | bytes 1179656 | tf_op jit(solution)/shard_map/ppermute | solution.py:115
  208.7 0.8 copy-start.8
  217.1 35.2 %all-to-all-start.2 = ((bf16[32,32,1024]{2,1,0:T(8,128)(2,1)}), bf16[32,32,1024]{2,1,0:T(8,128)(2,1)S(1)}, u32[]{:S(2)}, u32[]{:S(2)}) async-start(bf16[32,32,1024]{2,1,0:T(8,128)(2,1)} %down.3), calls=%async_computation.2 | async-start | bytes 4194304 | tf_op jit(solution)/shard_map/all_to_all | solution.py:164
  230.0 26.9 %copy-start.5 = (bf16[32,2,32,256]{3,2,1,0:T(8,128)(2,1)S(1)}, bf16[32,2,32,256]{3,2,1,0:T(8,128)(2,1)}, u32[]{:S(2)}) copy-start(bf16[32,2,32,256]{3,2,1,0:T(8,128)(2,1)} %pad_maximum_fusion.2) | copy-start | bytes 3145732
  252.2 34.7 %all-to-all-start.1 = ((bf16[32,32,1024]{2,1,0:T(8,128)(2,1)}), bf16[32,32,1024]{2,1,0:T(8,128)(2,1)}, u32[]{:S(2)}, u32[]{:S(2)}) async-start(bf16[32,32,1024]{2,1,0:T(8,128)(2,1)} %down.2), calls=%async_computation.1 | async-start | bytes 4194304 | tf_op jit(solution)/shard_map/all_to_all | solution.py:164
  (1 other events, 0.7 us)
Sparse Core Ops, SparseCore 0:
  9.6 116.7 all-gather.1

commit v5 on v2

--- a/solution.py
+++ b/solution.py
@@ -13,7 +13,7 @@
 
 def gate_up_body(slots, ids_ref, q_ref, *refs):
     parts = refs[:4]
-    gate_ref, up_ref, out_ref, rows_ref, gate_acc, up_acc = refs[4:]
+    gate_ref, up_ref, out_ref, rows_ref, acc_ref = refs[4:]
     step = pl.program_id(0)
     tok = q_ref.shape[-1]
     exp_local = gate_ref.shape[0]
@@ -22,8 +22,7 @@
 
     @pl.when(step == 0)
     def _():
-        gate_acc[...] = jnp.zeros_like(gate_acc)
-        up_acc[...] = jnp.zeros_like(up_acc)
+        acc_ref[...] = jnp.zeros_like(acc_ref)
 
     for b in range(4 * each):
         seats = q_ref[ids_ref[b]]
@@ -41,15 +40,15 @@
         for j in range(exp_local):
             rows_ref[j, b * slots : (b + 1) * slots, :] = rows[j * slots : (j + 1) * slots]
     for j in range(exp_local):
-        rows = rows_ref[j]
-        gate_acc[j] += jnp.dot(rows, gate_ref[j], preferred_element_type=jnp.float32)
-        up_acc[j] += jnp.dot(rows, up_ref[j], preferred_element_type=jnp.float32)
+        joined = jnp.concatenate([gate_ref[j], up_ref[j]], axis=1)
+        acc_ref[j] += jnp.dot(rows_ref[j], joined, preferred_element_type=jnp.float32)
 
     @pl.when(step == pl.num_programs(0) - 1)
     def _():
         for j in range(exp_local):
-            hidden = (jax.nn.silu(gate_acc[j]) * up_acc[j]).astype(jnp.bfloat16)
-            out_ref[:, j] = hidden.reshape(4 * each, slots, hidden.shape[-1])
+            hid = gate_ref.shape[-1]
+            hidden = (jax.nn.silu(acc_ref[j, :, :hid]) * acc_ref[j, :, hid:]).astype(jnp.bfloat16)
+            out_ref[:, j] = hidden.reshape(4 * each, slots, hid)
 
 
 def gate_up(ids, q_in, parts, gate_weight, up_weight, slots):
@@ -59,7 +58,6 @@
     wide = width_all // STEPS
     weight_spec = pl.BlockSpec((exp_local, wide, hid), lambda k, ids: (0, k, 0))
     part_spec = pl.BlockSpec((parts[0].shape[0], wide), lambda k, ids: (0, k))
-    flops = 2 * exp_local * count * slots * width_all * 2 * hid
     return pl.pallas_call(
         lambda *refs: gate_up_body(slots, *refs),
         out_shape=jax.ShapeDtypeStruct((count, exp_local, slots, hid), jnp.bfloat16),
@@ -75,36 +73,30 @@
             out_specs=pl.BlockSpec((count, exp_local, slots, hid), lambda k, ids: (0, 0, 0, 0)),
             scratch_shapes=[
                 pltpu.VMEM((exp_local, count * slots, wide), jnp.bfloat16),
-                pltpu.VMEM((exp_local, count * slots, hid), jnp.float32),
-                pltpu.VMEM((exp_local, count * slots, hid), jnp.float32),
+                pltpu.VMEM((exp_local, count * slots, 2 * hid), jnp.float32),
             ],
         ),
         compiler_params=pltpu.CompilerParams(vmem_limit_bytes=VMEM_BYTES),
-        cost_estimate=pl.CostEstimate(
-            flops=flops,
-            transcendentals=0,
-            bytes_accessed=2 * (2 * exp_local * width_all * hid + count * tok * width_all),
-        ),
+        cost_estimate=pl.CostEstimate(flops=1, transcendentals=0, bytes_accessed=1),
         name="gate_up",
     )(ids, q_in, *parts, gate_weight, up_weight)
 
 
 def down_body(chunks, ids_ref, *refs):
-    hs = refs[: 4 * chunks]
-    ws = refs[4 * chunks : 4 * chunks + 4]
+    hs, w_ref = refs[:chunks], refs[chunks]
     out_ref, rows_ref, sem = refs[-3:]
-    count, exp_local, slots, hid = hs[0].shape
-    cols = ws[0].shape[-1]
+    n_width, count, exp_local, slots, hid = hs[0].shape
+    cols = w_ref.shape[-1]
     copies = []
     for n in range(chunks):
         for j in range(exp_local):
-            total = jnp.zeros((count * slots, cols), jnp.float32)
-            for y in range(4):
-                total = total + jnp.dot(
-                    hs[4 * n + y][:, j].reshape(count * slots, hid),
-                    ws[y][j],
-                    preferred_element_type=jnp.float32,
-                )
+            rows = [hs[n][y, :, j].reshape(count * slots, hid) for y in range(n_width)]
+            weight = [w_ref[y, j] for y in range(n_width)]
+            total = jnp.dot(
+                jnp.concatenate(rows, axis=1),
+                jnp.concatenate(weight, axis=0),
+                preferred_element_type=jnp.float32,
+            )
             rows_ref[n, :, j] = total.astype(jnp.bfloat16).reshape(count, slots, cols)
         for b in range(count):
             copy = pltpu.make_async_copy(
@@ -118,11 +110,10 @@
 
 def down(ids, hidden, weights, sources, before=None):
     chunks = len(hidden)
-    count, exp_local, slots, hid = hidden[0][0].shape
-    cols = weights[0].shape[-1]
-    flat = [h for four in hidden for h in four]
-    operands = [ids, *flat, *weights]
-    specs = [pl.BlockSpec(memory_space=pltpu.VMEM)] * (len(flat) + 4)
+    _, count, exp_local, slots, hid = hidden[0].shape
+    cols = weights.shape[-1]
+    operands = [ids, *hidden, weights]
+    specs = [pl.BlockSpec(memory_space=pltpu.VMEM)] * (chunks + 1)
     aliases = {}
     if before is not None:
         aliases = {len(operands): 0}
@@ -143,11 +134,7 @@
         ),
         input_output_aliases=aliases,
         compiler_params=pltpu.CompilerParams(vmem_limit_bytes=VMEM_BYTES),
-        cost_estimate=pl.CostEstimate(
-            flops=2 * chunks * exp_local * count * slots * cols * 4 * hid,
-            transcendentals=0,
-            bytes_accessed=2 * (exp_local * 4 * hid * cols + chunks * exp_local * count * slots * cols),
-        ),
+        cost_estimate=pl.CostEstimate(flops=1, transcendentals=0, bytes_accessed=1),
         name="down",
     )(*operands)
 
@@ -172,19 +159,21 @@
     return [(place_of(z, x, c), place_of(z, x, 1 - c)) for z, x, c in spots]
 
 
-def gather_chunks(tokens):
+def gather_chunks(tokens, q_in, weights):
     half = tokens.shape[0] // 2
     send = lambda v, axis, by: lax.ppermute(v, "expert", move(axis, by))
     swap = lambda v: lax.ppermute(v, "expert", other_core())
     fore, back = send(tokens, 0, 1), send(tokens, 0, -1)
+    fore, back = lax.optimization_barrier((fore, back))
     far = [send(fore[:half], 0, 1), send(back[half:], 0, -1)]
     near_a = jnp.concatenate([tokens, fore], axis=0)
     near_b = jnp.concatenate([back, *far], axis=0)
-    fore_a, back_b = send(near_a, 1, 1), send(near_b, 1, -1)
-    fore_b, back_a = send(near_b, 1, 1), send(near_a, 1, -1)
+    fore_a, back_a = send(near_a, 1, 1), send(near_a, 1, -1)
+    fore_b, back_b = send(near_b, 1, 1), send(near_b, 1, -1)
+    back_b, weights = lax.optimization_barrier((back_b, weights))
     far_a, far_b = send(fore_a, 1, 1), send(back_b, 1, -1)
-    pairs = [(near_a, near_b), (fore_a, back_b), (fore_b, back_a), (far_a, far_b)]
-    return [[a, swap(a), b, swap(b)] for a, b in pairs]
+    pairs = [(near_a, near_b), (fore_a, back_a), (fore_b, back_b), (far_a, far_b)]
+    return [[a, swap(a), b, swap(b)] for a, b in pairs], q_in, weights
 
 
 def chunk_ids():
@@ -193,8 +182,8 @@
     near, wide = (0, -1), (1, 2)
     chunks = [
         ((near, 0), (wide, 0)),
-        ((near, -1), (wide, 1)),
-        ((wide, -1), (near, 1)),
+        ((near, -1), (near, 1)),
+        ((wide, -1), (wide, 1)),
         ((near, -2), (wide, 2)),
     ]
     first, second, kinds = [], [], []
@@ -213,11 +202,6 @@
     return ids.astype(jnp.int32).reshape(4, -1)
 
 
-def around(v, by):
-    n = lax.axis_size("width")
-    return lax.ppermute(v, "width", [(i, (i + by) % n) for i in range(n)])
-
-
 def local(tokens, expert_ids, combine_weights, gate_weight, up_weight, down_weight):
     tok_rows = tokens.shape[0]
     exp_local = gate_weight.shape[0]
@@ -234,27 +218,23 @@
     earlier = (order[:, None] < order[None, :]).astype(jnp.bfloat16)
     rank = jnp.dot(member.astype(jnp.bfloat16), earlier, preferred_element_type=jnp.float32)
     place = jnp.where(member, rank.astype(jnp.int32), -1)
-    q_in = lax.all_to_all(
-        place.reshape(n_expert, exp_local, tok_rows), "expert", split_axis=0, concat_axis=0, tiled=True
-    )
+    q_all = lax.all_gather(place, "expert", axis=0, tiled=False)
+    q_in = lax.dynamic_slice_in_dim(q_all, lax.axis_index("expert") * exp_local, exp_local, 1)
     seat = place[:, None, :] == jnp.arange(slots, dtype=jnp.int32)[None, :, None]
     spread = jnp.where(seat, weight_of[:, None, :], 0.0).reshape(experts_all * slots, tok_rows)
     high = spread.astype(jnp.bfloat16)
     low = (spread - high.astype(jnp.float32)).astype(jnp.bfloat16)
 
     cols = down_weight.shape[2] // n_width
-    mine = lax.axis_index("width")
-    cut = lambda by: lax.dynamic_slice_in_dim(down_weight, (mine + by) % n_width * cols, cols, 2)
-    weights = [cut(0), around(cut(1), 1), around(cut(3), -1), around(cut(2), 2)]
+    cut = jnp.stack([down_weight[:, :, n * cols : (n + 1) * cols] for n in range(n_width)])
+    weights = lax.all_to_all(cut, "width", split_axis=0, concat_axis=0, tiled=True)
 
     ids = chunk_ids()
     hidden = []
-    for n, parts in enumerate(gather_chunks(tokens)):
+    chunks, q_in, weights = gather_chunks(tokens, q_in, weights)
+    for n, parts in enumerate(chunks):
         h = gate_up(ids[n], q_in, parts, gate_weight, up_weight, slots)
-        half = h.shape[0] // 2
-        fore, back = around(h, 1), around(h, -1)
-        far = jnp.concatenate([around(fore[:half], 1), around(back[half:], -1)], axis=0)
-        hidden.append([h, fore, back, far])
+        hidden.append(lax.all_gather(h, "width", axis=0, tiled=False))
     rows = down(ids[:3].reshape(-1), hidden[:3], weights, n_expert)
     rows = down(ids[3], hidden[3:], weights, n_expert, rows)
 

time: 344 us -> 272 us (0.79)
  waiting for transfers between devices: 190 us -> 138 us
  starting transfers between devices: 58.8 us -> 32 us
  between operations: 0.49 us -> 13.4 us
  Pallas kernels: 67 us -> 62.8 us
    ppermute x19 -> x0, waiting for transfers between devices: 70.8 us -> none  [around(): return lax.ppermute(v, 'width', [(i, (i + by) % n) for i in range(n)])]
    all_gather x0 -> x5, waiting for transfers between devices: none -> 49.4 us  [the longest x1 26.4 us: local(): q_all = lax.all_gather(place, 'expert', axis=0, tiled=False)]
    ppermute x10, waiting for transfers between devices: 51.4 us -> 22.1 us  [gather_chunks(): send = lambda v, axis, by: lax.ppermute(v, 'expert', move(axis, by))]
    ppermute x19 -> x0, starting transfers between devices: 26.4 us -> none  [around(): return lax.ppermute(v, 'width', [(i, (i + by) % n) for i in range(n)])]
    all_to_all x1, waiting for transfers between devices: 16.9 us -> 0.01 us  [local(): lax.all_to_all(cut, 'width', split_axis=0, concat_axis=0, tiled=True)]
    ppermute x8, waiting for transfers between devices: 0.02 us -> 13.8 us  [gather_chunks(): swap = lambda v: lax.ppermute(v, 'expert', other_core())]
    dynamic_slice x1, local copies, waits for them, and re-layouts: 6.02 us -> 1.52 us  [local(): lax.dynamic_slice_in_dim(q_all, lax.axis_index('expert') * exp_local, exp...]
    ppermute x10, starting transfers between devices: 21.1 us -> 17.2 us  [gather_chunks(): send = lambda v, axis, by: lax.ppermute(v, 'expert', move(axis, by))]
  transfers between devices with their start and end apart: 39 -> 25, of which waited for: 12 -> 14; matrix products, arithmetic and copies ran while one was open for 5% -> 6% of each run, Pallas kernels for 17% -> 21%
where the time goes in v5:
time: 272 us
  waiting for transfers between devices  138 us (51%)
  Pallas kernels  62.8 us (23%)
  starting transfers between devices  32 us (12%)
  local copies, waits for them, and re-layouts  16.5 us (6%)
  between operations  13.4 us (5%)
  other arithmetic  4.76 us (2%)
  matrix products  4.22 us (2%)
    all_to_all x1, waiting for transfers between devices, local(): lax.all_to_all(rows, 'expert', split_axis=0, concat_axis=0, tiled=True)  52.7 us
    pallas_call x4, Pallas kernels, gate_up(): pl.pallas_call(lambda *refs: gate_up_body(slots, *refs), out_shape=jax.Sh...  45 us
    all_gather x1, waiting for transfers between devices, local(): q_all = lax.all_gather(place, 'expert', axis=0, tiled=False)  26.4 us
    all_gather x4, waiting for transfers between devices, local(): hidden.append(lax.all_gather(h, 'width', axis=0, tiled=False))  23 us
    ppermute x10, waiting for transfers between devices, gather_chunks(): send = lambda v, axis, by: lax.ppermute(v, 'expert', move(axis, by))  22.1 us
    pallas_call x2, Pallas kernels, down(): pl.pallas_call(lambda *refs: down_body(chunks, *refs), out_shape=jax.Shap...  17.9 us
    ppermute x10, starting transfers between devices, gather_chunks(): send = lambda v, axis, by: lax.ppermute(v, 'expert', move(axis, by))  17.2 us
    ppermute x8, waiting for transfers between devices, gather_chunks(): swap = lambda v: lax.ppermute(v, 'expert', other_core())  13.8 us
  transfers between devices with their start and end apart: 25, of which 14 were waited for; matrix products, arithmetic and copies ran while one was open for 6% of the time, Pallas kernels for 21%

profile of v5, /device:TPU:0, one launch (start us, length us, event | category | flops | bytes accessed | tf_op | source)
XLA Modules:
  0.0 271.8 jit_solution(17847389439567591856)
XLA Ops:
  10.7 3.6 %slice_bitcast_fusion.3 = (bf16[1,2,384,1024]{3,2,1,0:T(8,128)(2,1)S(1)}, bf16[1,2,384,1024]{3,2,1,0:T(8,128)(2,1)S(1)}, bf16[1,2,384,1024]{3,2,1,0:T(8,128)(2,1)S(1)}, bf16[1,2,384,1024]{3,2,1,0:T(8,128)(2,1)S(1)}) fusion(bf16[2,384,4096]{2,1,0:T(8,128)(2,1)} %param.14), kind=kLoop, calls=%fused_computation.4 | loop fusion | bytes 12582912 | tf_op jit(solution)/shard_map/stack | solution.py:229
  14.3 3.2 %pad_maximum_fusion = bf16[4,2,384,1024]{3,2,1,0:T(8,128)(2,1)} fusion(bf16[1,2,384,1024]{3,2,1,0:T(8,128)(2,1)S(1)} %get-tuple-element.15, bf16[1,2,384,1024]{3,2,1,0:T(8,128)(2,1)S(1)} %get-tuple-element.16, bf16[1,2,384,1024]{3,2,1,0:T(8,128)(2,1)S(1)} %get-tuple-element.14, bf16[1,2,384,1024]{3,2,1,0:T(8,128)(2,1)S(1)} %get-tuple-element.13), kind=kLoop, calls=%fused_computation | loop fusion | flops 9437184 | bytes 12582912 | tf_op jit(solution)/shard_map/stack | solution.py:229
  17.5 5.4 %all-to-all-start = ((bf16[4,2,384,1024]{3,2,1,0:T(8,128)(2,1)}), bf16[4,2,384,1024]{3,2,1,0:T(8,128)(2,1)}, u32[]{:S(2)}, u32[]{:S(2)}) async-start(bf16[4,2,384,1024]{3,2,1,0:T(8,128)(2,1)} %pad_maximum_fusion), calls=%async_computation | async-start | bytes 12582912 | tf_op jit(solution)/shard_map/all_to_all | solution.py:230
  29.1 2.9 %collective-permute-start.6 = (bf16[64,4096]{1,0:T(8,128)(2,1)S(1)}, bf16[64,4096]{1,0:T(8,128)(2,1)S(1)}, u32[]{:S(2)}, u32[]{:S(2)}) collective-permute-start(bf16[64,4096]{1,0:T(8,128)(2,1)S(1)} %slice.47), channel_id=1, source_target_pairs={{0,96},{4,28},{8,104},{12,4},{16,112},{20,12},{24,120},{28,20},{32... | collective-permute-start | bytes 1572872 | tf_op jit(solution)/shard_map/ppermute | solution.py:164
  32.2 3.5 %collective-permute-done.5 = bf16[64,4096]{1,0:T(8,128)(2,1)S(1)} collective-permute-done((bf16[64,4096]{1,0:T(8,128)(2,1)S(1)}, bf16[64,4096]{1,0:T(8,128)(2,1)S(1)}, u32[]{:S(2)}, u32[]{:S(2)}) %collective-permute-start.5) | collective-permute-done | bytes 524320 | tf_op jit(solution)/shard_map/ppermute | solution.py:164
  43.7 26.4 %all-gather.11.cloned.1.call-done = s32[2048,128]{1,0:T(8,128)} async-done(((s32[64,128]{1,0:T(8,128)}), s32[2048,128]{1,0:T(8,128)}) %all-gather.11.cloned.1.call-update) | async-done | bytes 1048592 | tf_op jit(solution)/shard_map/all_gather | solution.py:221
  71.6 11.1 %gate_up.5 = bf16[8,2,32,384]{3,2,1,0:T(8,128)(2,1)} custom-call(s32[8]{0:T(128)} %get-tuple-element.19.refs_0_, s32[32,2,128]{2,1,0:T(2,128)} %constant_dynamic-slice_fusion.refs_1_, bf16[256,4096]{1,0:T(8,128)(2,1)} %copy-done, bf16[256,4096]{1,0:T(8,128)(2,1)} %collective-permute-done.10.refs_3_, ...), custom_call_target="tpu_custom_call" | custom-call | flops 1 | bytes 1 | tf_op jit(solution)/shard_map/gate_up/pallas_call | solution.py:61
  87.3 3.0 %collective-permute-done.14.refs_5_ = bf16[256,4096]{1,0:T(8,128)(2,1)S(1)} collective-permute-done((bf16[256,4096]{1,0:T(8,128)(2,1)}, bf16[256,4096]{1,0:T(8,128)(2,1)S(1)}, u32[]{:S(2)}, u32[]{:S(2)}) %collective-permute-start.14) | collective-permute-done | bytes 2097184 | tf_op jit(solution)/shard_map/ppermute | solution.py:165
  91.6 11.2 %gate_up.6 = bf16[8,2,32,384]{3,2,1,0:T(8,128)(2,1)} custom-call(s32[8]{0:T(128)} %get-tuple-element.18.refs_0_, s32[32,2,128]{2,1,0:T(2,128)} %constant_dynamic-slice_fusion.refs_1_, bf16[256,4096]{1,0:T(8,128)(2,1)} %collective-permute-done.2.refs_2_, bf16[256,4096]{1,0:T(8,128)(2,1)} %copy-done.2, bf16[256,4096]{1,0:T(8,128)(2,1)} %collective-permute-done.13.refs_4_, ...), custom_call_target="tpu_custom_call" | custom-call | flops 1 | bytes 1 | tf_op jit(solution)/shard_map/gate_up/pallas_call | solution.py:61
  103.0 8.0 %collective-permute-done.15.refs_2_ = bf16[256,4096]{1,0:T(8,128)(2,1)} collective-permute-done((bf16[256,4096]{1,0:T(8,128)(2,1)}, bf16[256,4096]{1,0:T(8,128)(2,1)}, u32[]{:S(2)}, u32[]{:S(2)}) %collective-permute-start.15) | collective-permute-done | bytes 2097184 | tf_op jit(solution)/shard_map/ppermute | solution.py:164
  112.2 2.6 collective-permute-start.8
  114.8 2.7 collective-permute-done.16.refs_3_
  119.5 11.3 %gate_up.7 = bf16[8,2,32,384]{3,2,1,0:T(8,128)(2,1)} custom-call(s32[8]{0:T(128)} %get-tuple-element.17.refs_0_, s32[32,2,128]{2,1,0:T(2,128)} %constant_dynamic-slice_fusion.refs_1_, bf16[256,4096]{1,0:T(8,128)(2,1)} %collective-permute-done.15.refs_2_, bf16[256,4096]{1,0:T(8,128)(2,1)} %collective-permute-done.16.refs_3_, bf16[256,4096]{1,0:T(8,128)(2,1)} %copy-done.1, ...), custom_call_target="tpu_custom_call" | custom-call | flops 1 | bytes 1 | tf_op jit(solution)/shard_map/gate_up/pallas_call | solution.py:61
  130.9 8.3 %collective-permute-done.3.refs_2_ = bf16[256,4096]{1,0:T(8,128)(2,1)} collective-permute-done((bf16[256,4096]{1,0:T(8,128)(2,1)}, bf16[256,4096]{1,0:T(8,128)(2,1)}, u32[]{:S(2)}, u32[]{:S(2)}) %collective-permute-start.3) | collective-permute-done | bytes 2097184 | tf_op jit(solution)/shard_map/ppermute | solution.py:164
  139.7 3.9 %collective-permute-done.4.refs_3_ = bf16[256,4096]{1,0:T(8,128)(2,1)S(1)} collective-permute-done((bf16[256,4096]{1,0:T(8,128)(2,1)}, bf16[256,4096]{1,0:T(8,128)(2,1)S(1)}, u32[]{:S(2)}, u32[]{:S(2)}) %collective-permute-start.4) | collective-permute-done | bytes 2097184 | tf_op jit(solution)/shard_map/ppermute | solution.py:165
  143.5 3.0 %collective-permute-done.9.refs_5_ = bf16[256,4096]{1,0:T(8,128)(2,1)S(1)} collective-permute-done((bf16[256,4096]{1,0:T(8,128)(2,1)}, bf16[256,4096]{1,0:T(8,128)(2,1)S(1)}, u32[]{:S(2)}, u32[]{:S(2)}) %collective-permute-start.9) | collective-permute-done | bytes 2097184 | tf_op jit(solution)/shard_map/ppermute | solution.py:165
  147.9 11.3 %gate_up.4 = bf16[8,2,32,384]{3,2,1,0:T(8,128)(2,1)} custom-call(s32[8]{0:T(128)} %get-tuple-element.20.refs_0_, s32[32,2,128]{2,1,0:T(2,128)} %constant_dynamic-slice_fusion.refs_1_, bf16[256,4096]{1,0:T(8,128)(2,1)} %collective-permute-done.3.refs_2_, bf16[256,4096]{1,0:T(8,128)(2,1)} %copy-done.3, bf16[256,4096]{1,0:T(8,128)(2,1)} %collective-permute-done.8.refs_4_, ...), custom_call_target="tpu_custom_call" | custom-call | flops 1 | bytes 1 | tf_op jit(solution)/shard_map/gate_up/pallas_call | solution.py:61
  159.3 5.9 %all-gather.19.cloned.1.call-done = bf16[32,2,32,384]{3,2,1,0:T(8,128)(2,1)} async-done(((bf16[8,2,32,384]{3,2,1,0:T(8,128)(2,1)}), bf16[32,2,32,384]{3,2,1,0:T(8,128)(2,1)}) %all-gather.19.cloned.1.call-update) | async-done | bytes 1572880 | tf_op jit(solution)/shard_map/all_gather | solution.py:237
  165.2 11.1 %down.2.refs_3_ = bf16[32,2,32,1024]{3,2,1,0:T(8,128)(2,1)} custom-call(s32[24]{0:T(128)} %bitcast.41, bf16[4,8,2,32,384]{4,3,2,1,0:T(8,128)(2,1)} %bitcast.37, bf16[4,8,2,32,384]{4,3,2,1,0:T(8,128)(2,1)} %bitcast.38, bf16[4,8,2,32,384]{4,3,2,1,0:T(8,128)(2,1)} %bitcast.39, bf16[4,2,384,1024]{3,2,1,0:T(8,128)(2,1)} %all-to-all-done.refs_4_.refs_2_), custom_call_target="tpu_custom_call" | custom-call | flops 1 | bytes 1 | tf_op jit(solution)/shard_map/down/pallas_call | solution.py:122
  176.3 17.0 %all-gather.13.cloned.1.call-done = bf16[32,2,32,384]{3,2,1,0:T(8,128)(2,1)} async-done(((bf16[8,2,32,384]{3,2,1,0:T(8,128)(2,1)}), bf16[32,2,32,384]{3,2,1,0:T(8,128)(2,1)}) %all-gather.13.cloned.1.call-update) | async-done | bytes 1572880 | tf_op jit(solution)/shard_map/all_gather | solution.py:237
  193.3 6.8 %down.3 = bf16[32,2,32,1024]{3,2,1,0:T(8,128)(2,1)} custom-call(s32[8]{0:T(128)} %get-tuple-element.20.refs_0_, bf16[4,8,2,32,384]{4,3,2,1,0:T(8,128)(2,1)} %bitcast.40, bf16[4,2,384,1024]{3,2,1,0:T(8,128)(2,1)} %all-to-all-done.refs_4_.refs_2_, bf16[32,2,32,1024]{3,2,1,0:T(8,128)(2,1)} %down.2.refs_3_), custom_call_target="tpu_custom_call", output_to_operand_aliasing={{}: (3, {})} | custom-call | flops 1 | bytes 1 | tf_op jit(solution)/shard_map/down/pallas_call | solution.py:122
  200.1 7.4 %all-to-all-start.1 = ((bf16[32,2,32,1024]{3,2,1,0:T(8,128)(2,1)}), bf16[32,2,32,1024]{3,2,1,0:T(8,128)(2,1)}, u32[]{:S(2)}, u32[]{:S(2)}) async-start(bf16[32,2,32,1024]{3,2,1,0:T(8,128)(2,1)} %down.3), calls=%async_computation.1 | async-start | bytes 8388608 | tf_op jit(solution)/shard_map/all_to_all | solution.py:241
  208.4 52.7 %all-to-all-done.1 = bf16[32,2,32,1024]{3,2,1,0:T(8,128)(2,1)} async-done(((bf16[32,2,32,1024]{3,2,1,0:T(8,128)(2,1)}), bf16[32,2,32,1024]{3,2,1,0:T(8,128)(2,1)}, u32[]{:S(2)}, u32[]{:S(2)}) %all-to-all-start.1) | async-done | bytes 4194336 | tf_op jit(solution)/shard_map/all_to_all | solution.py:241
  261.0 3.5 %fusion.1 = f32[256,1024]{1,0:T(8,128)S(1)} fusion(bf16[2048,1024]{1,0:T(8,128)(2,1)} %bitcast.13, bf16[2048,128]{1,0:T(8,128)(2,1)S(1)} %fusion.7, bf16[2048,128]{1,0:T(8,128)(2,1)S(1)} %fusion.6), kind=kOutput, calls=%fused_computation.7 | convolution fusion | flops 1075838976 | bytes 6291456 | tf_op jit(solution)/shard_map/dot_general | solution.py:244
  (86 shorter events, 32.6 us)
Async XLA Ops:
  6.5 18.6 %collective-permute-start = (bf16[128,4096]{1,0:T(8,128)(2,1)}, bf16[128,4096]{1,0:T(8,128)(2,1)S(1)}, u32[]{:S(2)}, u32[]{:S(2)}) collective-permute-start(bf16[128,4096]{1,0:T(8,128)(2,1)} %param.9), channel_id=1, source_target_pairs={{0,32},{4,12},{8,40},{12,20},{16,48},{20,28},{24,56},{28,4},{32,64... | collective-permute-start | bytes 3145736 | tf_op jit(solution)/shard_map/ppermute | solution.py:164
  8.5 16.6 %collective-permute-start.1 = (bf16[128,4096]{1,0:T(8,128)(2,1)}, bf16[128,4096]{1,0:T(8,128)(2,1)}, u32[]{:S(2)}, u32[]{:S(2)}) collective-permute-start(bf16[128,4096]{1,0:T(8,128)(2,1)} %param.9), channel_id=1, source_target_pairs={{0,96},{4,28},{8,104},{12,4},{16,112},{20,12},{24,120},{28,20},{32... | collective-permute-start | bytes 3145736 | tf_op jit(solution)/shard_map/ppermute | solution.py:164
  17.5 93.5 %all-to-all-start = ((bf16[4,2,384,1024]{3,2,1,0:T(8,128)(2,1)}), bf16[4,2,384,1024]{3,2,1,0:T(8,128)(2,1)}, u32[]{:S(2)}, u32[]{:S(2)}) async-start(bf16[4,2,384,1024]{3,2,1,0:T(8,128)(2,1)} %pad_maximum_fusion), calls=%async_computation | async-start | bytes 12582912 | tf_op jit(solution)/shard_map/all_to_all | solution.py:230
  22.9 47.1 %all-gather.11.cloned.1.call-start = ((), (), s32[]{:S(2)}) async-start(), calls=%async_computation.2 | async-start | bytes 1081344 | tf_op jit(solution)/shard_map/all_gather | solution.py:221
  23.8 135.4 %all-gather.15.cloned.1.call-start = ((), (), s32[]{:S(2)}) async-start(), calls=%async_computation.4 | async-start | bytes 1966080 | tf_op jit(solution)/shard_map/all_gather | solution.py:237
  25.2 10.5 %collective-permute-start.5 = (bf16[64,4096]{1,0:T(8,128)(2,1)S(1)}, bf16[64,4096]{1,0:T(8,128)(2,1)S(1)}, u32[]{:S(2)}, u32[]{:S(2)}) collective-permute-start(bf16[64,4096]{1,0:T(8,128)(2,1)S(1)} %slice.46), channel_id=1, source_target_pairs={{0,32},{4,12},{8,40},{12,20},{16,48},{20,28},{24,56},{28,4},{32,64... | collective-permute-start | bytes 1572872 | tf_op jit(solution)/shard_map/ppermute | solution.py:164
  29.1 9.8 %collective-permute-start.6 = (bf16[64,4096]{1,0:T(8,128)(2,1)S(1)}, bf16[64,4096]{1,0:T(8,128)(2,1)S(1)}, u32[]{:S(2)}, u32[]{:S(2)}) collective-permute-start(bf16[64,4096]{1,0:T(8,128)(2,1)S(1)} %slice.47), channel_id=1, source_target_pairs={{0,96},{4,28},{8,104},{12,4},{16,112},{20,12},{24,120},{28,20},{32... | collective-permute-start | bytes 1572872 | tf_op jit(solution)/shard_map/ppermute | solution.py:164
  32.1 39.5 %collective-permute-start.10 = (bf16[256,4096]{1,0:T(8,128)(2,1)S(1)}, bf16[256,4096]{1,0:T(8,128)(2,1)}, u32[]{:S(2)}, u32[]{:S(2)}) collective-permute-start(bf16[256,4096]{1,0:T(8,128)(2,1)S(1)} %constant_dynamic-update-slice_fusion.refs_2_), channel_id=1, source_target_pairs={{0,4},{4,0},{8,12},{12,8},{16,20},{20,16},{24,28},{28,24},{32,36},... | collective-permute-start | bytes 6291464 | tf_op jit(solution)/shard_map/ppermute | solution.py:165
  39.8 31.9 %collective-permute-start.11 = (bf16[256,4096]{1,0:T(8,128)(2,1)}, bf16[256,4096]{1,0:T(8,128)(2,1)}, u32[]{:S(2)}, u32[]{:S(2)}) collective-permute-start(bf16[256,4096]{1,0:T(8,128)(2,1)} %constant_dynamic-update-slice_fusion.2.refs_4_), channel_id=1, source_target_pairs={{0,4},{4,0},{8,12},{12,8},{16,20},{20,16},{24,28},{28,24},{32,36},... | collective-permute-start | bytes 6291464 | tf_op jit(solution)/shard_map/ppermute | solution.py:165
  39.8 43.1 %collective-permute-start.2 = (bf16[256,4096]{1,0:T(8,128)(2,1)S(1)}, bf16[256,4096]{1,0:T(8,128)(2,1)}, u32[]{:S(2)}, u32[]{:S(2)}) collective-permute-start(bf16[256,4096]{1,0:T(8,128)(2,1)S(1)} %constant_dynamic-update-slice_fusion.refs_2_), channel_id=1, source_target_pairs={{0,8},{4,36},{8,16},{12,44},{16,24},{20,52},{24,0},{28,60},{32,40}... | collective-permute-start | bytes 6291464 | tf_op jit(solution)/shard_map/ppermute | solution.py:164
  41.2 41.9 %collective-permute-start.13 = (bf16[256,4096]{1,0:T(8,128)(2,1)S(1)}, bf16[256,4096]{1,0:T(8,128)(2,1)}, u32[]{:S(2)}, u32[]{:S(2)}) collective-permute-start(bf16[256,4096]{1,0:T(8,128)(2,1)S(1)} %constant_dynamic-update-slice_fusion.refs_2_), channel_id=1, source_target_pairs={{0,24},{4,100},{8,0},{12,108},{16,8},{20,116},{24,16},{28,124},{32... | collective-permute-start | bytes 6291464 | tf_op jit(solution)/shard_map/ppermute | solution.py:164
  82.8 76.5 %all-gather.17.cloned.1.call-start = ((), (), s32[]{:S(2)}) async-start(), calls=%async_computation.5 | async-start | bytes 1966080 | tf_op jit(solution)/shard_map/all_gather | solution.py:237
  82.8 4.5 %collective-permute-start.12 = (bf16[256,4096]{1,0:T(8,128)(2,1)}, bf16[256,4096]{1,0:T(8,128)(2,1)S(1)}, u32[]{:S(2)}, u32[]{:S(2)}) collective-permute-start(bf16[256,4096]{1,0:T(8,128)(2,1)} %collective-permute-done.2.refs_2_), channel_id=1, source_target_pairs={{0,4},{4,0},{8,12},{12,8},{16,20},{20,16},{24,28},{28,24},{32,36},... | collective-permute-start | bytes 6291464 | tf_op jit(solution)/shard_map/ppermute | solution.py:165
  83.2 7.1 %collective-permute-start.14 = (bf16[256,4096]{1,0:T(8,128)(2,1)}, bf16[256,4096]{1,0:T(8,128)(2,1)S(1)}, u32[]{:S(2)}, u32[]{:S(2)}) collective-permute-start(bf16[256,4096]{1,0:T(8,128)(2,1)} %collective-permute-done.13.refs_4_), channel_id=1, source_target_pairs={{0,4},{4,0},{8,12},{12,8},{16,20},{20,16},{24,28},{28,24},{32,36},... | collective-permute-start | bytes 6291464 | tf_op jit(solution)/shard_map/ppermute | solution.py:165
  83.4 27.6 %collective-permute-start.15 = (bf16[256,4096]{1,0:T(8,128)(2,1)}, bf16[256,4096]{1,0:T(8,128)(2,1)}, u32[]{:S(2)}, u32[]{:S(2)}) collective-permute-start(bf16[256,4096]{1,0:T(8,128)(2,1)} %constant_dynamic-update-slice_fusion.2.refs_4_), channel_id=1, source_target_pairs={{0,8},{4,36},{8,16},{12,44},{16,24},{20,52},{24,0},{28,60},{32,40}... | collective-permute-start | bytes 6291464 | tf_op jit(solution)/shard_map/ppermute | solution.py:164
  84.5 26.4 %collective-permute-start.7 = (bf16[256,4096]{1,0:T(8,128)(2,1)}, bf16[256,4096]{1,0:T(8,128)(2,1)S(1)}, u32[]{:S(2)}, u32[]{:S(2)}) collective-permute-start(bf16[256,4096]{1,0:T(8,128)(2,1)} %constant_dynamic-update-slice_fusion.2.refs_4_), channel_id=1, source_target_pairs={{0,24},{4,100},{8,0},{12,108},{16,8},{20,116},{24,16},{28,124},{32... | collective-permute-start | bytes 6291464 | tf_op jit(solution)/shard_map/ppermute | solution.py:164
  102.9 62.3 %all-gather.19.cloned.1.call-start = ((), (), s32[]{:S(2)}) async-start(), calls=%async_computation.6 | async-start | bytes 1966080 | tf_op jit(solution)/shard_map/all_gather | solution.py:237
  111.0 6.5 %collective-permute-start.16 = (bf16[256,4096]{1,0:T(8,128)(2,1)}, bf16[256,4096]{1,0:T(8,128)(2,1)}, u32[]{:S(2)}, u32[]{:S(2)}) collective-permute-start(bf16[256,4096]{1,0:T(8,128)(2,1)} %collective-permute-done.15.refs_2_), channel_id=1, source_target_pairs={{0,4},{4,0},{8,12},{12,8},{16,20},{20,16},{24,28},{28,24},{32,36},... | collective-permute-start | bytes 6291464 | tf_op jit(solution)/shard_map/ppermute | solution.py:165
  111.0 7.1 %collective-permute-start.17 = (bf16[256,4096]{1,0:T(8,128)(2,1)S(1)}, bf16[256,4096]{1,0:T(8,128)(2,1)S(1)}, u32[]{:S(2)}, u32[]{:S(2)}) collective-permute-start(bf16[256,4096]{1,0:T(8,128)(2,1)S(1)} %collective-permute-done.7.refs_4_), channel_id=1, source_target_pairs={{0,4},{4,0},{8,12},{12,8},{16,20},{20,16},{24,28},{28,24},{32,36},... | collective-permute-start | bytes 6291464 | tf_op jit(solution)/shard_map/ppermute | solution.py:165
  111.6 27.6 %collective-permute-start.3 = (bf16[256,4096]{1,0:T(8,128)(2,1)}, bf16[256,4096]{1,0:T(8,128)(2,1)}, u32[]{:S(2)}, u32[]{:S(2)}) collective-permute-start(bf16[256,4096]{1,0:T(8,128)(2,1)} %collective-permute-done.2.refs_2_), channel_id=1, source_target_pairs={{0,8},{4,36},{8,16},{12,44},{16,24},{20,52},{24,0},{28,60},{32,40}... | collective-permute-start | bytes 6291464 | tf_op jit(solution)/shard_map/ppermute | solution.py:164
  112.2 26.9 %collective-permute-start.8 = (bf16[256,4096]{1,0:T(8,128)(2,1)S(1)}, bf16[256,4096]{1,0:T(8,128)(2,1)}, u32[]{:S(2)}, u32[]{:S(2)}) collective-permute-start(bf16[256,4096]{1,0:T(8,128)(2,1)S(1)} %collective-permute-done.7.refs_4_), channel_id=1, source_target_pairs={{0,24},{4,100},{8,0},{12,108},{16,8},{20,116},{24,16},{28,124},{32... | collective-permute-start | bytes 6291464 | tf_op jit(solution)/shard_map/ppermute | solution.py:164
  130.8 62.5 %all-gather.13.cloned.1.call-start = ((), (), s32[]{:S(2)}) async-start(), calls=%async_computation.3 | async-start | bytes 1966080 | tf_op jit(solution)/shard_map/all_gather | solution.py:237
  139.2 7.4 %collective-permute-start.9 = (bf16[256,4096]{1,0:T(8,128)(2,1)}, bf16[256,4096]{1,0:T(8,128)(2,1)S(1)}, u32[]{:S(2)}, u32[]{:S(2)}) collective-permute-start(bf16[256,4096]{1,0:T(8,128)(2,1)} %collective-permute-done.8.refs_4_), channel_id=1, source_target_pairs={{0,4},{4,0},{8,12},{12,8},{16,20},{20,16},{24,28},{28,24},{32,36},... | collective-permute-start | bytes 6291464 | tf_op jit(solution)/shard_map/ppermute | solution.py:165
  200.1 60.9 %all-to-all-start.1 = ((bf16[32,2,32,1024]{3,2,1,0:T(8,128)(2,1)}), bf16[32,2,32,1024]{3,2,1,0:T(8,128)(2,1)}, u32[]{:S(2)}, u32[]{:S(2)}) async-start(bf16[32,2,32,1024]{3,2,1,0:T(8,128)(2,1)} %down.3), calls=%async_computation.1 | async-start | bytes 8388608 | tf_op jit(solution)/shard_map/all_to_all | solution.py:241
  (15 other events, 163.2 us)
Sparse Core Ops, SparseCore 0:
  26.0 43.9 all-gather.10
  82.9 25.8 all-gather.14
  110.4 26.5 all-gather.16
  138.6 26.5 all-gather.18
  166.7 26.5 all-gather.12

commit v6 on v5

--- a/solution.py
+++ b/solution.py
@@ -8,16 +8,17 @@
 MOST = 32
 SIDE = 4
 STEPS = 4
+RING = (0, 3, 1, 2)
+MARK = 8
 VMEM_BYTES = 56 * 1024 * 1024
 
 
-def gate_up_body(slots, ids_ref, q_ref, *refs):
-    parts = refs[:4]
-    gate_ref, up_ref, out_ref, rows_ref, acc_ref = refs[4:]
+def gate_up_body(slots, tok, each, at_ref, *refs):
+    parts, marks = refs[:4], refs[4 : 4 + 4 * each]
+    gate_ref, up_ref, out_ref, rows_ref, acc_ref = refs[4 + 4 * each :]
     step = pl.program_id(0)
-    tok = q_ref.shape[-1]
     exp_local = gate_ref.shape[0]
-    each = parts[0].shape[0] // tok
+    block = parts[0].shape[0] // each
     place = lax.broadcasted_iota(jnp.int32, (slots, tok), 0)
 
     @pl.when(step == 0)
@@ -25,15 +26,20 @@
         acc_ref[...] = jnp.zeros_like(acc_ref)
 
     for b in range(4 * each):
-        seats = q_ref[ids_ref[b]]
+        mark = marks[b][...].astype(jnp.int32)
+        seats = mark[0:1]
+        for r in range(1, mark.shape[0]):
+            seats = jnp.where(at_ref[0] == r, mark[r : r + 1], seats)
         pick = jnp.concatenate(
             [
-                jnp.where(place == seats[j][None, :], 1.0, 0.0).astype(jnp.bfloat16)
+                jnp.where(place == seats[:, j * tok : (j + 1) * tok], 1.0, 0.0).astype(
+                    jnp.bfloat16
+                )
                 for j in range(exp_local)
             ],
             axis=0,
         )
-        at = (b % each) * tok
+        at = (b % each) * block
         rows = jnp.dot(
             pick, parts[b // each][at : at + tok, :], preferred_element_type=jnp.float32
         ).astype(jnp.bfloat16)
@@ -51,26 +57,30 @@
             out_ref[:, j] = hidden.reshape(4 * each, slots, hid)
 
 
-def gate_up(ids, q_in, parts, gate_weight, up_weight, slots):
-    _, exp_local, tok = q_in.shape
-    _, width_all, hid = gate_weight.shape
-    count = 4 * parts[0].shape[0] // tok
+def gate_up(spot, parts, gate_weight, up_weight, slots, tok):
+    exp_local, width_all, hid = gate_weight.shape
+    block = tok + MARK
+    each = parts[0].shape[0] // block
+    count = 4 * each
     wide = width_all // STEPS
-    weight_spec = pl.BlockSpec((exp_local, wide, hid), lambda k, ids: (0, k, 0))
-    part_spec = pl.BlockSpec((parts[0].shape[0], wide), lambda k, ids: (0, k))
+    weight_spec = pl.BlockSpec((exp_local, wide, hid), lambda k, at: (0, k, 0))
+    part_spec = pl.BlockSpec((parts[0].shape[0], wide), lambda k, at: (0, k))
+    mark_specs = [
+        pl.BlockSpec(
+            (MARK, exp_local * tok),
+            lambda k, at, b=b: (b * (block // MARK) + tok // MARK, at[1]),
+        )
+        for b in range(each)
+    ]
+    marks = [part for part in parts for _ in range(each)]
     return pl.pallas_call(
-        lambda *refs: gate_up_body(slots, *refs),
+        lambda *refs: gate_up_body(slots, tok, each, *refs),
         out_shape=jax.ShapeDtypeStruct((count, exp_local, slots, hid), jnp.bfloat16),
         grid_spec=pltpu.PrefetchScalarGridSpec(
             num_scalar_prefetch=1,
             grid=(STEPS,),
-            in_specs=[
-                pl.BlockSpec(q_in.shape, lambda k, ids: (0, 0, 0)),
-                *[part_spec] * 4,
-                weight_spec,
-                weight_spec,
-            ],
-            out_specs=pl.BlockSpec((count, exp_local, slots, hid), lambda k, ids: (0, 0, 0, 0)),
+            in_specs=[*[part_spec] * 4, *mark_specs * 4, weight_spec, weight_spec],
+        out_specs=pl.BlockSpec((count, exp_local, slots, hid), lambda k, at: (0, 0, 0, 0)),
             scratch_shapes=[
                 pltpu.VMEM((exp_local, count * slots, wide), jnp.bfloat16),
                 pltpu.VMEM((exp_local, count * slots, 2 * hid), jnp.float32),
@@ -79,48 +89,60 @@
         compiler_params=pltpu.CompilerParams(vmem_limit_bytes=VMEM_BYTES),
         cost_estimate=pl.CostEstimate(flops=1, transcendentals=0, bytes_accessed=1),
         name="gate_up",
-    )(ids, q_in, *parts, gate_weight, up_weight)
-
-
-def down_body(chunks, ids_ref, *refs):
-    hs, w_ref = refs[:chunks], refs[chunks]
+    )(spot, *parts, *marks, gate_weight, up_weight)
+
+
+def down_body(counts, ids_ref, *refs):
+    refs = list(refs)
     out_ref, rows_ref, sem = refs[-3:]
-    n_width, count, exp_local, slots, hid = hs[0].shape
-    cols = w_ref.shape[-1]
-    copies = []
-    for n in range(chunks):
+    mine = ids_ref[rows_ref.shape[0]]
+    sets = []
+    for count in counts:
+        sets.append([refs.pop(0)] if count else [refs.pop(0) for _ in RING])
+    w_ref = refs[0]
+    n_width, exp_local, hid, cols = w_ref.shape
+    copies, base = [], 0
+    for count, hs in zip(counts, sets):
+        blocks, _, slots, _ = hs[0].shape[-4:]
         for j in range(exp_local):
-            rows = [hs[n][y, :, j].reshape(count * slots, hid) for y in range(n_width)]
-            weight = [w_ref[y, j] for y in range(n_width)]
+            if count:
+                rows = [hs[0][y, :, j].reshape(blocks * slots, hid) for y in range(n_width)]
+                weight = [w_ref[y, j] for y in range(n_width)]
+            else:
+                rows = [h[:, j].reshape(blocks * slots, hid) for h in hs]
+                weight = [w_ref[lax.rem(mine + by, n_width), j] for by in RING]
             total = jnp.dot(
                 jnp.concatenate(rows, axis=1),
                 jnp.concatenate(weight, axis=0),
                 preferred_element_type=jnp.float32,
             )
-            rows_ref[n, :, j] = total.astype(jnp.bfloat16).reshape(count, slots, cols)
-        for b in range(count):
-            copy = pltpu.make_async_copy(
-                rows_ref.at[n, b], out_ref.at[ids_ref[n * count + b]], sem.at[n * count + b]
+            rows_ref[base : base + blocks, j] = total.astype(jnp.bfloat16).reshape(
+                blocks, slots, cols
             )
+        for b in range(base, base + blocks):
+            copy = pltpu.make_async_copy(rows_ref.at[b], out_ref.at[ids_ref[b]], sem.at[b])
             copy.start()
             copies.append(copy)
+        base += blocks
     for copy in copies:
         copy.wait()
 
 
 def down(ids, hidden, weights, sources, before=None):
-    chunks = len(hidden)
-    _, count, exp_local, slots, hid = hidden[0].shape
+    counts = [0 if isinstance(h, list) else h.shape[1] for h in hidden]
+    flat = [v for h in hidden for v in (h if isinstance(h, list) else [h])]
+    exp_local, slots = flat[0].shape[-3:-1]
+    blocks = sum(h[0].shape[0] if isinstance(h, list) else h.shape[1] for h in hidden)
     cols = weights.shape[-1]
-    operands = [ids, *hidden, weights]
-    specs = [pl.BlockSpec(memory_space=pltpu.VMEM)] * (chunks + 1)
+    operands = [ids, *flat, weights]
+    specs = [pl.BlockSpec(memory_space=pltpu.VMEM)] * (len(flat) + 1)
     aliases = {}
     if before is not None:
         aliases = {len(operands): 0}
         operands.append(before)
         specs = specs + [pl.BlockSpec(memory_space=pl.ANY)]
     return pl.pallas_call(
-        lambda *refs: down_body(chunks, *refs),
+        lambda *refs: down_body(counts, *refs),
         out_shape=jax.ShapeDtypeStruct((sources, exp_local, slots, cols), jnp.bfloat16),
         grid_spec=pltpu.PrefetchScalarGridSpec(
             num_scalar_prefetch=1,
@@ -128,8 +150,8 @@
             in_specs=specs,
             out_specs=pl.BlockSpec(memory_space=pl.ANY),
             scratch_shapes=[
-                pltpu.VMEM((chunks, count, exp_local, slots, cols), jnp.bfloat16),
-                pltpu.SemaphoreType.DMA((chunks * count,)),
+                pltpu.VMEM((blocks, exp_local, slots, cols), jnp.bfloat16),
+                pltpu.SemaphoreType.DMA((blocks,)),
             ],
         ),
         input_output_aliases=aliases,
@@ -159,10 +181,9 @@
     return [(place_of(z, x, c), place_of(z, x, 1 - c)) for z, x, c in spots]
 
 
-def gather_chunks(tokens, q_in, weights):
-    half = tokens.shape[0] // 2
+def near_chunks(tokens):
+    half = tokens.shape[0] // (2 * MARK) * MARK
     send = lambda v, axis, by: lax.ppermute(v, "expert", move(axis, by))
-    swap = lambda v: lax.ppermute(v, "expert", other_core())
     fore, back = send(tokens, 0, 1), send(tokens, 0, -1)
     fore, back = lax.optimization_barrier((fore, back))
     far = [send(fore[:half], 0, 1), send(back[half:], 0, -1)]
@@ -170,10 +191,7 @@
     near_b = jnp.concatenate([back, *far], axis=0)
     fore_a, back_a = send(near_a, 1, 1), send(near_a, 1, -1)
     fore_b, back_b = send(near_b, 1, 1), send(near_b, 1, -1)
-    back_b, weights = lax.optimization_barrier((back_b, weights))
-    far_a, far_b = send(fore_a, 1, 1), send(back_b, 1, -1)
-    pairs = [(near_a, near_b), (fore_a, back_a), (fore_b, back_b), (far_a, far_b)]
-    return [[a, swap(a), b, swap(b)] for a, b in pairs], q_in, weights
+    return (near_a, near_b), (fore_a, back_a), (fore_b, back_b)
 
 
 def chunk_ids():
@@ -202,6 +220,11 @@
     return ids.astype(jnp.int32).reshape(4, -1)
 
 
+def around(v, by):
+    n = lax.axis_size("width")
+    return lax.ppermute(v, "width", [(i, (i + by) % n) for i in range(n)])
+
+
 def local(tokens, expert_ids, combine_weights, gate_weight, up_weight, down_weight):
     tok_rows = tokens.shape[0]
     exp_local = gate_weight.shape[0]
@@ -218,8 +241,14 @@
     earlier = (order[:, None] < order[None, :]).astype(jnp.bfloat16)
     rank = jnp.dot(member.astype(jnp.bfloat16), earlier, preferred_element_type=jnp.float32)
     place = jnp.where(member, rank.astype(jnp.int32), -1)
-    q_all = lax.all_gather(place, "expert", axis=0, tiled=False)
-    q_in = lax.dynamic_slice_in_dim(q_all, lax.axis_index("expert") * exp_local, exp_local, 1)
+    lines = experts_all * tok_rows // tokens.shape[1]
+    marks = place.astype(jnp.bfloat16).reshape(lines, tokens.shape[1])
+    marks = jnp.pad(marks, ((0, MARK - lines), (0, 0)))
+    marked = jnp.concatenate([tokens, marks], axis=0)
+    across = tokens.shape[1] // (exp_local * tok_rows)
+    me = lax.axis_index("expert")
+    spot = jnp.stack([me // across, me % across]).astype(jnp.int32)
+
     seat = place[:, None, :] == jnp.arange(slots, dtype=jnp.int32)[None, :, None]
     spread = jnp.where(seat, weight_of[:, None, :], 0.0).reshape(experts_all * slots, tok_rows)
     high = spread.astype(jnp.bfloat16)
@@ -230,13 +259,27 @@
     weights = lax.all_to_all(cut, "width", split_axis=0, concat_axis=0, tiled=True)
 
     ids = chunk_ids()
-    hidden = []
-    chunks, q_in, weights = gather_chunks(tokens, q_in, weights)
-    for n, parts in enumerate(chunks):
-        h = gate_up(ids[n], q_in, parts, gate_weight, up_weight, slots)
-        hidden.append(lax.all_gather(h, "width", axis=0, tiled=False))
-    rows = down(ids[:3].reshape(-1), hidden[:3], weights, n_expert)
-    rows = down(ids[3], hidden[3:], weights, n_expert, rows)
+    send = lambda v, by: lax.ppermute(v, "expert", move(1, by))
+    swap = lambda v: lax.ppermute(v, "expert", other_core())
+    crossed = lambda a, b: [a, swap(a), b, swap(b)]
+    compute = lambda parts: gate_up(spot, parts, gate_weight, up_weight, slots, tok_rows)
+    near, (fore_a, back_a), (fore_b, back_b) = near_chunks(marked)
+    first = compute(crossed(*near))
+    parts, first = lax.optimization_barrier((crossed(fore_a, back_a), first))
+    second = compute(parts)
+    fore_b, back_b, weights, second = lax.optimization_barrier((fore_b, back_b, weights, second))
+    far_a, far_b = send(fore_a, 1), send(back_b, -1)
+    third = compute(crossed(fore_b, back_b))
+    far_a, far_b, third = lax.optimization_barrier((far_a, far_b, third))
+    fourth = compute(crossed(far_a, far_b))
+    ring = lambda h: [h, around(h, 1), around(h, -1), around(h, 2)]
+    last = ring(fourth)
+    hidden = [lax.all_gather(h, "width", axis=0, tiled=False) for h in (first, second)]
+    hidden.append(ring(third))
+    mine = lax.axis_index("width").astype(jnp.int32)[None]
+    at = lambda v: jnp.concatenate([v.reshape(-1), mine])
+    rows = down(at(jnp.concatenate([ids[0], ids[2]])), [hidden[0], hidden[2]], weights, n_expert)
+    rows = down(at(jnp.concatenate([ids[1], ids[3]])), [hidden[1], last], weights, n_expert, rows)
 
     returned = lax.all_to_all(rows, "expert", split_axis=0, concat_axis=0, tiled=True)
     returned = returned.reshape(experts_all * slots, cols)

time: 272 us -> 261 us (0.960)
  waiting for transfers between devices: 138 us -> 118 us
  starting transfers between devices: 32 us -> 39.1 us
  other arithmetic: 4.76 us -> 9.7 us
  local copies, waits for them, and re-layouts: 16.5 us -> 11.8 us
    all_gather x5 -> x2, waiting for transfers between devices: 49.4 us -> 13.2 us  [local(): lax.all_gather(h, 'width', axis=0, tiled=False)]
    ppermute x18 -> x24, waiting for transfers between devices: 35.9 us -> 50.6 us  [the longest x8 28.4 us: near_chunks(): send = lambda v, axis, by: lax.ppermute(v, 'expert', move(axis, by))]
    ppermute x18 -> x24, starting transfers between devices: 19 us -> 25.3 us  [the longest x8 14.2 us: near_chunks(): send = lambda v, axis, by: lax.ppermute(v, 'expert', move(axis, by))]
    concatenate x0 -> x4, other arithmetic: none -> 3.61 us  [the longest x1 2.32 us: local(): marked = jnp.concatenate([tokens, marks], axis=0)]
    unnamed x31 -> x36, local copies, waits for them, and re-layouts: 8.58 us -> 5.96 us
  transfers between devices with their start and end apart: 25 -> 28, of which waited for: 14 -> 16; matrix products, arithmetic and copies ran while one was open for 6% -> 5% of each run, Pallas kernels for 21% -> 21%
where the time goes in v6:
time: 261 us; the launch traced here: 260 us
  waiting for transfers between devices  118 us (45%)
  Pallas kernels  63.9 us (24%)
  starting transfers between devices  39.1 us (15%)
  between operations  13.6 us (5%)
  local copies, waits for them, and re-layouts  11.8 us (5%)
  other arithmetic  9.7 us (4%)
  matrix products  3.6 us (1%)
    all_to_all x1, waiting for transfers between devices, local(): lax.all_to_all(rows, 'expert', split_axis=0, concat_axis=0, tiled=True)  52.7 us
    pallas_call x4, Pallas kernels, gate_up(): pl.pallas_call(lambda *refs: gate_up_body(slots, tok, each, *refs), out_s...  45.9 us
    ppermute x8, waiting for transfers between devices, near_chunks(): send = lambda v, axis, by: lax.ppermute(v, 'expert', move(axis, by))  28.4 us
    pallas_call x2, Pallas kernels, down(): pl.pallas_call(lambda *refs: down_body(counts, *refs), out_shape=jax.Shap...  18 us
    ppermute x8, starting transfers between devices, near_chunks(): send = lambda v, axis, by: lax.ppermute(v, 'expert', move(axis, by))  14.2 us
    all_gather x2, waiting for transfers between devices, local(): lax.all_gather(h, 'width', axis=0, tiled=False)  13.2 us
    ppermute x2, waiting for transfers between devices, local(): send = lambda v, by: lax.ppermute(v, 'expert', move(1, by))  9.92 us
    all_to_all x1, starting transfers between devices, local(): lax.all_to_all(rows, 'expert', split_axis=0, concat_axis=0, tiled=True)  8.34 us
  transfers between devices with their start and end apart: 28, of which 16 were waited for; matrix products, arithmetic and copies ran while one was open for 5% of the time, Pallas kernels for 21%

profile of v6, /device:TPU:0, one launch (start us, length us, event | category | flops | bytes accessed | tf_op | source)
XLA Modules:
  0.0 260.1 jit_solution(4227008089891593007)
XLA Ops:
  7.4 2.3 pad_maximum_fusion.2
  13.9 3.6 %slice_bitcast_fusion.3 = (bf16[1,2,384,1024]{3,2,1,0:T(8,128)(2,1)S(1)}, bf16[1,2,384,1024]{3,2,1,0:T(8,128)(2,1)S(1)}, bf16[1,2,384,1024]{3,2,1,0:T(8,128)(2,1)S(1)}, bf16[1,2,384,1024]{3,2,1,0:T(8,128)(2,1)S(1)}) fusion(bf16[2,384,4096]{2,1,0:T(8,128)(2,1)} %param.14), kind=kLoop, calls=%fused_computation.5 | loop fusion | bytes 12582912 | tf_op jit(solution)/shard_map/stack | solution.py:258
  17.5 3.3 %pad_maximum_fusion = bf16[4,2,384,1024]{3,2,1,0:T(8,128)(2,1)} fusion(bf16[1,2,384,1024]{3,2,1,0:T(8,128)(2,1)S(1)} %get-tuple-element.35, bf16[1,2,384,1024]{3,2,1,0:T(8,128)(2,1)S(1)} %get-tuple-element.36, bf16[1,2,384,1024]{3,2,1,0:T(8,128)(2,1)S(1)} %get-tuple-element.34, bf16[1,2,384,1024]{3,2,1,0:T(8,128)(2,1)S(1)} %get-tuple-element.33), kind=kLoop, calls=%fused_computation | loop fusion | flops 9437184 | bytes 12582912 | tf_op jit(solution)/shard_map/stack | solution.py:258
  20.8 5.4 %all-to-all-start = ((bf16[4,2,384,1024]{3,2,1,0:T(8,128)(2,1)}), bf16[4,2,384,1024]{3,2,1,0:T(8,128)(2,1)}, u32[]{:S(2)}, u32[]{:S(2)}) async-start(bf16[4,2,384,1024]{3,2,1,0:T(8,128)(2,1)} %pad_maximum_fusion), calls=%async_computation | async-start | bytes 12582912 | tf_op jit(solution)/shard_map/all_to_all | solution.py:259
  34.1 2.3 collective-permute-start.3
  37.5 11.6 %collective-permute-done.2 = bf16[64,4096]{1,0:T(8,128)(2,1)S(1)} collective-permute-done((bf16[64,4096]{1,0:T(8,128)(2,1)S(1)}, bf16[64,4096]{1,0:T(8,128)(2,1)S(1)}, u32[]{:S(2)}, u32[]{:S(2)}) %collective-permute-start.2) | collective-permute-done | bytes 524320 | tf_op jit(solution)/shard_map/ppermute | solution.py:186
  51.3 11.7 %collective-permute-done.6.refs_1_.refs_5_.refs_6_ = bf16[272,4096]{1,0:T(8,128)(2,1)} collective-permute-done((bf16[272,4096]{1,0:T(8,128)(2,1)S(1)}, bf16[272,4096]{1,0:T(8,128)(2,1)}, u32[]{:S(2)}, u32[]{:S(2)}) %collective-permute-start.6) | collective-permute-done | bytes 2228256 | tf_op jit(solution)/shard_map/ppermute | solution.py:186
  69.4 11.4 %gate_up.4 = bf16[8,2,32,384]{3,2,1,0:T(8,128)(2,1)} custom-call(s32[2]{0:T(128)} %pad_add_fusion.refs_0_, bf16[272,4096]{1,0:T(8,128)(2,1)} %copy-done, bf16[272,4096]{1,0:T(8,128)(2,1)} %copy-done.3, bf16[272,4096]{1,0:T(8,128)(2,1)} %constant_dynamic-update-slice_fusion.refs_3_.refs_9_.refs_10_, ...), custom_call_target="tpu_custom_call" | custom-call | flops 1 | bytes 1 | tf_op jit(solution)/shard_map/gate_up/pallas_call | solution.py:76
  80.8 11.3 %gate_up.5 = bf16[8,2,32,384]{3,2,1,0:T(8,128)(2,1)} custom-call(s32[2]{0:T(128)} %pad_add_fusion.refs_0_, bf16[272,4096]{1,0:T(8,128)(2,1)} %collective-permute-done.6.refs_1_.refs_5_.refs_6_, bf16[272,4096]{1,0:T(8,128)(2,1)} %collective-permute-done.7.refs_2_.refs_7_.refs_8_, bf16[272,4096]{1,0:T(8,128)(2,1)} %copy-done.2, ...), custom_call_target="tpu_custom_call" | custom-call | flops 1 | bytes 1 | tf_op jit(solution)/shard_map/gate_up/pallas_call | solution.py:76
  97.2 2.9 %collective-permute-start.13 = (bf16[272,4096]{1,0:T(8,128)(2,1)}, bf16[272,4096]{1,0:T(8,128)(2,1)}, u32[]{:S(2)}, u32[]{:S(2)}) collective-permute-start(bf16[272,4096]{1,0:T(8,128)(2,1)} %collective-permute-done.5.refs_3_.refs_9_.refs_10_), channel_id=1, source_target_pairs={{0,24},{4,100},{8,0},{12,108},{16,8},{20,116},{24,16},{28,124},{32... | collective-permute-start | bytes 6684680 | tf_op jit(solution)/shard_map/ppermute | solution.py:262
  101.1 3.2 %collective-permute-done.15.refs_4_.refs_11_.refs_12_ = bf16[272,4096]{1,0:T(8,128)(2,1)} collective-permute-done((bf16[272,4096]{1,0:T(8,128)(2,1)}, bf16[272,4096]{1,0:T(8,128)(2,1)}, u32[]{:S(2)}, u32[]{:S(2)}) %collective-permute-start.15) | collective-permute-done | bytes 2228256 | tf_op jit(solution)/shard_map/ppermute | solution.py:263
  104.3 11.6 %gate_up.6.refs_2_ = bf16[8,2,32,384]{3,2,1,0:T(8,128)(2,1)} custom-call(s32[2]{0:T(128)} %pad_add_fusion.refs_0_, bf16[272,4096]{1,0:T(8,128)(2,1)} %collective-permute-done.4.refs_1_.refs_5_.refs_6_, bf16[272,4096]{1,0:T(8,128)(2,1)} %collective-permute-done.14.refs_2_.refs_7_.refs_8_, bf16[272,4096]{1,0:T(8,128)(2,1)} %collective-permute-done.5.refs_3_.refs_9_.refs_10_, ...), custom_call_target="tpu_custom_call" | custom-call | flops 1 | bytes 1 | tf_op jit(solution)/shard_map/gate_up/pallas_call | solution.py:76
  115.8 9.9 %collective-permute-done.12.refs_1_.refs_5_.refs_6_ = bf16[272,4096]{1,0:T(8,128)(2,1)S(1)} collective-permute-done((bf16[272,4096]{1,0:T(8,128)(2,1)}, bf16[272,4096]{1,0:T(8,128)(2,1)S(1)}, u32[]{:S(2)}, u32[]{:S(2)}) %collective-permute-start.12) | collective-permute-done | bytes 2228256 | tf_op jit(solution)/shard_map/ppermute | solution.py:262
  127.1 2.6 collective-permute-start.22
  129.9 2.4 collective-permute-done.16.refs_2_.refs_7_.refs_8_
  133.6 11.6 %gate_up.7.refs_2_ = bf16[8,2,32,384]{3,2,1,0:T(8,128)(2,1)} custom-call(s32[2]{0:T(128)} %pad_add_fusion.refs_0_, bf16[272,4096]{1,0:T(8,128)(2,1)} %copy-done.1, bf16[272,4096]{1,0:T(8,128)(2,1)} %collective-permute-done.16.refs_2_.refs_7_.refs_8_, bf16[272,4096]{1,0:T(8,128)(2,1)} %collective-permute-done.13.refs_3_.refs_9_.refs_10_, ...), custom_call_target="tpu_custom_call" | custom-call | flops 1 | bytes 1 | tf_op jit(solution)/shard_map/gate_up/pallas_call | solution.py:76
  145.8 2.7 %collective-permute-start.19 = (bf16[8,2,32,384]{3,2,1,0:T(8,128)(2,1)}, bf16[8,2,32,384]{3,2,1,0:T(8,128)(2,1)S(1)}, u32[]{:S(2)}, u32[]{:S(2)}) collective-permute-start(bf16[8,2,32,384]{3,2,1,0:T(8,128)(2,1)} %gate_up.7.refs_2_), channel_id=1, source_target_pairs={{0,3},{1,0},{2,1},{3,2},{4,7},{5,4},{6,5},{7,6},{8,11},{9,8},{10,9... | collective-permute-start | bytes 1179656 | tf_op jit(solution)/shard_map/ppermute | solution.py:225
  149.7 4.5 %collective-permute-done.23.refs_5_ = bf16[8,2,32,384]{3,2,1,0:T(8,128)(2,1)S(1)} collective-permute-done((bf16[8,2,32,384]{3,2,1,0:T(8,128)(2,1)}, bf16[8,2,32,384]{3,2,1,0:T(8,128)(2,1)S(1)}, u32[]{:S(2)}, u32[]{:S(2)}) %collective-permute-start.23) | collective-permute-done | bytes 393248 | tf_op jit(solution)/shard_map/ppermute | solution.py:225
  155.0 9.0 %down.2.refs_7_ = bf16[32,2,32,1024]{3,2,1,0:T(8,128)(2,1)} custom-call(s32[17]{0:T(128)} %add_add_fusion.1.refs_0_, bf16[4,8,2,32,384]{4,3,2,1,0:T(8,128)(2,1)} %bitcast.37, bf16[8,2,32,384]{3,2,1,0:T(8,128)(2,1)} %gate_up.6.refs_2_, bf16[8,2,32,384]{3,2,1,0:T(8,128)(2,1)} %copy-done.6, bf16[8,2,32,384]{3,2,1,0:T(8,128)(2,1)} %copy-done.7, ...), custom_call_target="tpu_custom_call" | custom-call | flops 1 | bytes 1 | tf_op jit(solution)/shard_map/down/pallas_call | solution.py:144
  164.0 13.2 %all-gather.5.cloned.1.call-done = bf16[32,2,32,384]{3,2,1,0:T(8,128)(2,1)} async-done(((bf16[8,2,32,384]{3,2,1,0:T(8,128)(2,1)}), bf16[32,2,32,384]{3,2,1,0:T(8,128)(2,1)}) %all-gather.5.cloned.1.call-update) | async-done | bytes 1572880 | tf_op jit(solution)/shard_map/all_gather | solution.py:277
  178.2 8.9 %down.3 = bf16[32,2,32,1024]{3,2,1,0:T(8,128)(2,1)} custom-call(s32[17]{0:T(128)} %add_add_fusion.refs_0_, bf16[4,8,2,32,384]{4,3,2,1,0:T(8,128)(2,1)} %bitcast.36, bf16[8,2,32,384]{3,2,1,0:T(8,128)(2,1)} %gate_up.7.refs_2_, bf16[8,2,32,384]{3,2,1,0:T(8,128)(2,1)} %copy-done.8, bf16[8,2,32,384]{3,2,1,0:T(8,128)(2,1)} %copy-done.10, ...), custom_call_target="tpu_custom_call", output_to_operand_aliasing={{}: (7, {})} | custom-call | flops 1 | bytes 1 | tf_op jit(solution)/shard_map/down/pallas_call | solution.py:144
  187.2 8.3 %all-to-all-start.1 = ((bf16[32,2,32,1024]{3,2,1,0:T(8,128)(2,1)}), bf16[32,2,32,1024]{3,2,1,0:T(8,128)(2,1)}, u32[]{:S(2)}, u32[]{:S(2)}) async-start(bf16[32,2,32,1024]{3,2,1,0:T(8,128)(2,1)} %down.3), calls=%async_computation.1 | async-start | bytes 8388608 | tf_op jit(solution)/shard_map/all_to_all | solution.py:284
  196.4 52.7 %all-to-all-done.1 = bf16[32,2,32,1024]{3,2,1,0:T(8,128)(2,1)} async-done(((bf16[32,2,32,1024]{3,2,1,0:T(8,128)(2,1)}), bf16[32,2,32,1024]{3,2,1,0:T(8,128)(2,1)}, u32[]{:S(2)}, u32[]{:S(2)}) %all-to-all-start.1) | async-done | bytes 4194336 | tf_op jit(solution)/shard_map/all_to_all | solution.py:284
  249.0 3.5 %fusion.1 = f32[256,1024]{1,0:T(8,128)S(1)} fusion(bf16[2048,1024]{1,0:T(8,128)(2,1)} %bitcast.13, bf16[2048,128]{1,0:T(8,128)(2,1)S(1)} %fusion.7, bf16[2048,128]{1,0:T(8,128)(2,1)S(1)} %fusion.6), kind=kOutput, calls=%fused_computation.9 | convolution fusion | flops 1075838976 | bytes 6291456 | tf_op jit(solution)/shard_map/dot_general | solution.py:287
  (99 shorter events, 36.6 us)
Async XLA Ops:
  9.8 17.8 %collective-permute-start = (bf16[136,4096]{1,0:T(8,128)(2,1)}, bf16[136,4096]{1,0:T(8,128)(2,1)S(1)}, u32[]{:S(2)}, u32[]{:S(2)}) collective-permute-start(bf16[136,4096]{1,0:T(8,128)(2,1)} %pad_maximum_fusion.2), channel_id=1, source_target_pairs={{0,32},{4,12},{8,40},{12,20},{16,48},{20,28},{24,56},{28,4},{32,64... | collective-permute-start | bytes 3342344 | tf_op jit(solution)/shard_map/ppermute | solution.py:186
  11.8 15.8 %collective-permute-start.1 = (bf16[136,4096]{1,0:T(8,128)(2,1)}, bf16[136,4096]{1,0:T(8,128)(2,1)S(1)}, u32[]{:S(2)}, u32[]{:S(2)}) collective-permute-start(bf16[136,4096]{1,0:T(8,128)(2,1)} %pad_maximum_fusion.2), channel_id=1, source_target_pairs={{0,96},{4,28},{8,104},{12,4},{16,112},{20,12},{24,120},{28,20},{32... | collective-permute-start | bytes 3342344 | tf_op jit(solution)/shard_map/ppermute | solution.py:186
  20.8 75.6 %all-to-all-start = ((bf16[4,2,384,1024]{3,2,1,0:T(8,128)(2,1)}), bf16[4,2,384,1024]{3,2,1,0:T(8,128)(2,1)}, u32[]{:S(2)}, u32[]{:S(2)}) async-start(bf16[4,2,384,1024]{3,2,1,0:T(8,128)(2,1)} %pad_maximum_fusion), calls=%async_computation | async-start | bytes 12582912 | tf_op jit(solution)/shard_map/all_to_all | solution.py:259
  26.2 123.5 %all-gather.7.cloned.1.call-start = ((), (), s32[]{:S(2)}) async-start(), calls=%async_computation.3 | async-start | bytes 1966080 | tf_op jit(solution)/shard_map/all_gather | solution.py:277
  28.6 34.4 %collective-permute-start.6 = (bf16[272,4096]{1,0:T(8,128)(2,1)S(1)}, bf16[272,4096]{1,0:T(8,128)(2,1)}, u32[]{:S(2)}, u32[]{:S(2)}) collective-permute-start(bf16[272,4096]{1,0:T(8,128)(2,1)S(1)} %pad_maximum_fusion.1.refs_1_.refs_5_.refs_6_), channel_id=1, source_target_pairs={{0,8},{4,36},{8,16},{12,44},{16,24},{20,52},{24,0},{28,60},{32,40}... | collective-permute-start | bytes 6684680 | tf_op jit(solution)/shard_map/ppermute | solution.py:186
  30.1 33.8 %collective-permute-start.8 = (bf16[272,4096]{1,0:T(8,128)(2,1)S(1)}, bf16[272,4096]{1,0:T(8,128)(2,1)S(1)}, u32[]{:S(2)}, u32[]{:S(2)}) collective-permute-start(bf16[272,4096]{1,0:T(8,128)(2,1)S(1)} %pad_maximum_fusion.1.refs_1_.refs_5_.refs_6_), channel_id=1, source_target_pairs={{0,24},{4,100},{8,0},{12,108},{16,8},{20,116},{24,16},{28,124},{32... | collective-permute-start | bytes 6684680 | tf_op jit(solution)/shard_map/ppermute | solution.py:186
  31.9 33.5 %collective-permute-start.10 = (bf16[272,4096]{1,0:T(8,128)(2,1)S(1)}, bf16[272,4096]{1,0:T(8,128)(2,1)S(1)}, u32[]{:S(2)}, u32[]{:S(2)}) collective-permute-start(bf16[272,4096]{1,0:T(8,128)(2,1)S(1)} %pad_maximum_fusion.1.refs_1_.refs_5_.refs_6_), channel_id=1, source_target_pairs={{0,4},{4,0},{8,12},{12,8},{16,20},{20,16},{24,28},{28,24},{32,36},... | collective-permute-start | bytes 6684680 | tf_op jit(solution)/shard_map/ppermute | solution.py:263
  32.9 16.1 %collective-permute-start.2 = (bf16[64,4096]{1,0:T(8,128)(2,1)S(1)}, bf16[64,4096]{1,0:T(8,128)(2,1)S(1)}, u32[]{:S(2)}, u32[]{:S(2)}) collective-permute-start(bf16[64,4096]{1,0:T(8,128)(2,1)S(1)} %slice.42), channel_id=1, source_target_pairs={{0,32},{4,12},{8,40},{12,20},{16,48},{20,28},{24,56},{28,4},{32,64... | collective-permute-start | bytes 1572872 | tf_op jit(solution)/shard_map/ppermute | solution.py:186
  34.1 16.3 %collective-permute-start.3 = (bf16[72,4096]{1,0:T(8,128)(2,1)S(1)}, bf16[72,4096]{1,0:T(8,128)(2,1)S(1)}, u32[]{:S(2)}, u32[]{:S(2)}) collective-permute-start(bf16[72,4096]{1,0:T(8,128)(2,1)S(1)} %slice.43), channel_id=1, source_target_pairs={{0,96},{4,28},{8,104},{12,4},{16,112},{20,12},{24,120},{28,20},{32... | collective-permute-start | bytes 1769480 | tf_op jit(solution)/shard_map/ppermute | solution.py:186
  51.3 18.1 %collective-permute-start.11 = (bf16[272,4096]{1,0:T(8,128)(2,1)}, bf16[272,4096]{1,0:T(8,128)(2,1)}, u32[]{:S(2)}, u32[]{:S(2)}) collective-permute-start(bf16[272,4096]{1,0:T(8,128)(2,1)} %constant_dynamic-update-slice_fusion.refs_3_.refs_9_.refs_10_), channel_id=1, source_target_pairs={{0,4},{4,0},{8,12},{12,8},{16,20},{20,16},{24,28},{28,24},{32,36},... | collective-permute-start | bytes 6684680 | tf_op jit(solution)/shard_map/ppermute | solution.py:263
  63.0 17.8 %collective-permute-start.7 = (bf16[272,4096]{1,0:T(8,128)(2,1)}, bf16[272,4096]{1,0:T(8,128)(2,1)}, u32[]{:S(2)}, u32[]{:S(2)}) collective-permute-start(bf16[272,4096]{1,0:T(8,128)(2,1)} %collective-permute-done.6.refs_1_.refs_5_.refs_6_), channel_id=1, source_target_pairs={{0,4},{4,0},{8,12},{12,8},{16,20},{20,16},{24,28},{28,24},{32,36},... | collective-permute-start | bytes 6684680 | tf_op jit(solution)/shard_map/ppermute | solution.py:263
  63.9 16.9 %collective-permute-start.9 = (bf16[272,4096]{1,0:T(8,128)(2,1)S(1)}, bf16[272,4096]{1,0:T(8,128)(2,1)}, u32[]{:S(2)}, u32[]{:S(2)}) collective-permute-start(bf16[272,4096]{1,0:T(8,128)(2,1)S(1)} %collective-permute-done.8.refs_3_.refs_9_.refs_10_), channel_id=1, source_target_pairs={{0,4},{4,0},{8,12},{12,8},{16,20},{20,16},{24,28},{28,24},{32,36},... | collective-permute-start | bytes 6684680 | tf_op jit(solution)/shard_map/ppermute | solution.py:263
  63.9 29.0 %collective-permute-start.4 = (bf16[272,4096]{1,0:T(8,128)(2,1)}, bf16[272,4096]{1,0:T(8,128)(2,1)}, u32[]{:S(2)}, u32[]{:S(2)}) collective-permute-start(bf16[272,4096]{1,0:T(8,128)(2,1)} %constant_dynamic-update-slice_fusion.refs_3_.refs_9_.refs_10_), channel_id=1, source_target_pairs={{0,8},{4,36},{8,16},{12,44},{16,24},{20,52},{24,0},{28,60},{32,40}... | collective-permute-start | bytes 6684680 | tf_op jit(solution)/shard_map/ppermute | solution.py:186
  66.7 27.8 %collective-permute-start.5 = (bf16[272,4096]{1,0:T(8,128)(2,1)}, bf16[272,4096]{1,0:T(8,128)(2,1)}, u32[]{:S(2)}, u32[]{:S(2)}) collective-permute-start(bf16[272,4096]{1,0:T(8,128)(2,1)} %constant_dynamic-update-slice_fusion.refs_3_.refs_9_.refs_10_), channel_id=1, source_target_pairs={{0,24},{4,100},{8,0},{12,108},{16,8},{20,116},{24,16},{28,124},{32... | collective-permute-start | bytes 6684680 | tf_op jit(solution)/shard_map/ppermute | solution.py:186
  96.9 28.9 %collective-permute-start.12 = (bf16[272,4096]{1,0:T(8,128)(2,1)}, bf16[272,4096]{1,0:T(8,128)(2,1)S(1)}, u32[]{:S(2)}, u32[]{:S(2)}) collective-permute-start(bf16[272,4096]{1,0:T(8,128)(2,1)} %collective-permute-done.6.refs_1_.refs_5_.refs_6_), channel_id=1, source_target_pairs={{0,8},{4,36},{8,16},{12,44},{16,24},{20,52},{24,0},{28,60},{32,40}... | collective-permute-start | bytes 6684680 | tf_op jit(solution)/shard_map/ppermute | solution.py:262
  97.2 28.5 %collective-permute-start.13 = (bf16[272,4096]{1,0:T(8,128)(2,1)}, bf16[272,4096]{1,0:T(8,128)(2,1)}, u32[]{:S(2)}, u32[]{:S(2)}) collective-permute-start(bf16[272,4096]{1,0:T(8,128)(2,1)} %collective-permute-done.5.refs_3_.refs_9_.refs_10_), channel_id=1, source_target_pairs={{0,24},{4,100},{8,0},{12,108},{16,8},{20,116},{24,16},{28,124},{32... | collective-permute-start | bytes 6684680 | tf_op jit(solution)/shard_map/ppermute | solution.py:262
  100.2 77.0 %all-gather.5.cloned.1.call-start = ((), (), s32[]{:S(2)}) async-start(), calls=%async_computation.2 | async-start | bytes 1966080 | tf_op jit(solution)/shard_map/all_gather | solution.py:277
  126.3 22.2 %collective-permute-start.21 = (bf16[8,2,32,384]{3,2,1,0:T(8,128)(2,1)}, bf16[8,2,32,384]{3,2,1,0:T(8,128)(2,1)S(1)}, u32[]{:S(2)}, u32[]{:S(2)}) collective-permute-start(bf16[8,2,32,384]{3,2,1,0:T(8,128)(2,1)} %gate_up.6.refs_2_), channel_id=1, source_target_pairs={{0,1},{1,2},{2,3},{3,0},{4,5},{5,6},{6,7},{7,4},{8,9},{9,10},{10,1... | collective-permute-start | bytes 1179656 | tf_op jit(solution)/shard_map/ppermute | solution.py:225
  127.1 22.6 %collective-permute-start.22 = (bf16[8,2,32,384]{3,2,1,0:T(8,128)(2,1)}, bf16[8,2,32,384]{3,2,1,0:T(8,128)(2,1)S(1)}, u32[]{:S(2)}, u32[]{:S(2)}) collective-permute-start(bf16[8,2,32,384]{3,2,1,0:T(8,128)(2,1)} %gate_up.6.refs_2_), channel_id=1, source_target_pairs={{0,3},{1,0},{2,1},{3,2},{4,7},{5,4},{6,5},{7,6},{8,11},{9,8},{10,9... | collective-permute-start | bytes 1179656 | tf_op jit(solution)/shard_map/ppermute | solution.py:225
  129.7 24.5 %collective-permute-start.23 = (bf16[8,2,32,384]{3,2,1,0:T(8,128)(2,1)}, bf16[8,2,32,384]{3,2,1,0:T(8,128)(2,1)S(1)}, u32[]{:S(2)}, u32[]{:S(2)}) collective-permute-start(bf16[8,2,32,384]{3,2,1,0:T(8,128)(2,1)} %gate_up.6.refs_2_), channel_id=1, source_target_pairs={{0,2},{1,3},{2,0},{3,1},{4,6},{5,7},{6,4},{7,5},{8,10},{9,11},{10,... | collective-permute-start | bytes 1179656 | tf_op jit(solution)/shard_map/ppermute | solution.py:225
  145.3 32.0 %collective-permute-start.18 = (bf16[8,2,32,384]{3,2,1,0:T(8,128)(2,1)}, bf16[8,2,32,384]{3,2,1,0:T(8,128)(2,1)S(1)}, u32[]{:S(2)}, u32[]{:S(2)}) collective-permute-start(bf16[8,2,32,384]{3,2,1,0:T(8,128)(2,1)} %gate_up.7.refs_2_), channel_id=1, source_target_pairs={{0,1},{1,2},{2,3},{3,0},{4,5},{5,6},{6,7},{7,4},{8,9},{9,10},{10,1... | collective-permute-start | bytes 1179656 | tf_op jit(solution)/shard_map/ppermute | solution.py:225
  145.8 31.4 %collective-permute-start.19 = (bf16[8,2,32,384]{3,2,1,0:T(8,128)(2,1)}, bf16[8,2,32,384]{3,2,1,0:T(8,128)(2,1)S(1)}, u32[]{:S(2)}, u32[]{:S(2)}) collective-permute-start(bf16[8,2,32,384]{3,2,1,0:T(8,128)(2,1)} %gate_up.7.refs_2_), channel_id=1, source_target_pairs={{0,3},{1,0},{2,1},{3,2},{4,7},{5,4},{6,5},{7,6},{8,11},{9,8},{10,9... | collective-permute-start | bytes 1179656 | tf_op jit(solution)/shard_map/ppermute | solution.py:225
  148.5 28.7 %collective-permute-start.20 = (bf16[8,2,32,384]{3,2,1,0:T(8,128)(2,1)}, bf16[8,2,32,384]{3,2,1,0:T(8,128)(2,1)S(1)}, u32[]{:S(2)}, u32[]{:S(2)}) collective-permute-start(bf16[8,2,32,384]{3,2,1,0:T(8,128)(2,1)} %gate_up.7.refs_2_), channel_id=1, source_target_pairs={{0,2},{1,3},{2,0},{3,1},{4,6},{5,7},{6,4},{7,5},{8,10},{9,11},{10,... | collective-permute-start | bytes 1179656 | tf_op jit(solution)/shard_map/ppermute | solution.py:225
  187.2 61.8 %all-to-all-start.1 = ((bf16[32,2,32,1024]{3,2,1,0:T(8,128)(2,1)}), bf16[32,2,32,1024]{3,2,1,0:T(8,128)(2,1)}, u32[]{:S(2)}, u32[]{:S(2)}) async-start(bf16[32,2,32,1024]{3,2,1,0:T(8,128)(2,1)} %down.3), calls=%async_computation.1 | async-start | bytes 8388608 | tf_op jit(solution)/shard_map/all_to_all | solution.py:284
  (21 other events, 180.8 us)
Sparse Core Ops, SparseCore 0:
  100.3 24.6 all-gather.6
  126.6 50.5 all-gather.4

commit v7 on v6

--- a/solution.py
+++ b/solution.py
@@ -7,7 +7,7 @@
 
 MOST = 32
 SIDE = 4
-STEPS = 4
+STEPS = 2
 RING = (0, 3, 1, 2)
 MARK = 8
 VMEM_BYTES = 56 * 1024 * 1024

time: 261 us -> 261 us (level)
  no operation moved by 1% of the time
where the time goes in v7:
time: 261 us; the launch traced here: 260 us
  waiting for transfers between devices  118 us (45%)
  Pallas kernels  63.8 us (24%)
  starting transfers between devices  39.3 us (15%)
  between operations  13.6 us (5%)
  local copies, waits for them, and re-layouts  11.8 us (5%)
  other arithmetic  9.7 us (4%)
  matrix products  3.61 us (1%)
    all_to_all x1, waiting for transfers between devices, local(): lax.all_to_all(rows, 'expert', split_axis=0, concat_axis=0, tiled=True)  52.7 us
    pallas_call x4, Pallas kernels, gate_up(): pl.pallas_call(lambda *refs: gate_up_body(slots, tok, each, *refs), out_s...  45.9 us
    ppermute x8, waiting for transfers between devices, near_chunks(): send = lambda v, axis, by: lax.ppermute(v, 'expert', move(axis, by))  28.6 us
    pallas_call x2, Pallas kernels, down(): pl.pallas_call(lambda *refs: down_body(counts, *refs), out_shape=jax.Shap...  18 us
    ppermute x8, starting transfers between devices, near_chunks(): send = lambda v, axis, by: lax.ppermute(v, 'expert', move(axis, by))  14.2 us
    all_gather x2, waiting for transfers between devices, local(): lax.all_gather(h, 'width', axis=0, tiled=False)  13.2 us
    ppermute x2, waiting for transfers between devices, local(): send = lambda v, by: lax.ppermute(v, 'expert', move(1, by))  9.82 us
    all_to_all x1, starting transfers between devices, local(): lax.all_to_all(rows, 'expert', split_axis=0, concat_axis=0, tiled=True)  8.37 us
  transfers between devices with their start and end apart: 28, of which 16 were waited for; matrix products, arithmetic and copies ran while one was open for 5% of the time, Pallas kernels for 21%

profile of v7, /device:TPU:0, one launch (start us, length us, event | category | flops | bytes accessed | tf_op | source)
XLA Modules:
  0.0 260.2 jit_solution(6789611726963893301)
XLA Ops:
  7.4 2.3 pad_maximum_fusion.2
  13.9 3.6 %slice_bitcast_fusion.3 = (bf16[1,2,384,1024]{3,2,1,0:T(8,128)(2,1)S(1)}, bf16[1,2,384,1024]{3,2,1,0:T(8,128)(2,1)S(1)}, bf16[1,2,384,1024]{3,2,1,0:T(8,128)(2,1)S(1)}, bf16[1,2,384,1024]{3,2,1,0:T(8,128)(2,1)S(1)}) fusion(bf16[2,384,4096]{2,1,0:T(8,128)(2,1)} %param.14), kind=kLoop, calls=%fused_computation.5 | loop fusion | bytes 12582912 | tf_op jit(solution)/shard_map/stack | solution.py:258
  17.5 3.3 %pad_maximum_fusion = bf16[4,2,384,1024]{3,2,1,0:T(8,128)(2,1)} fusion(bf16[1,2,384,1024]{3,2,1,0:T(8,128)(2,1)S(1)} %get-tuple-element.35, bf16[1,2,384,1024]{3,2,1,0:T(8,128)(2,1)S(1)} %get-tuple-element.36, bf16[1,2,384,1024]{3,2,1,0:T(8,128)(2,1)S(1)} %get-tuple-element.34, bf16[1,2,384,1024]{3,2,1,0:T(8,128)(2,1)S(1)} %get-tuple-element.33), kind=kLoop, calls=%fused_computation | loop fusion | flops 9437184 | bytes 12582912 | tf_op jit(solution)/shard_map/stack | solution.py:258
  20.8 5.4 %all-to-all-start = ((bf16[4,2,384,1024]{3,2,1,0:T(8,128)(2,1)}), bf16[4,2,384,1024]{3,2,1,0:T(8,128)(2,1)}, u32[]{:S(2)}, u32[]{:S(2)}) async-start(bf16[4,2,384,1024]{3,2,1,0:T(8,128)(2,1)} %pad_maximum_fusion), calls=%async_computation | async-start | bytes 12582912 | tf_op jit(solution)/shard_map/all_to_all | solution.py:259
  34.1 2.3 collective-permute-start.3
  37.5 11.6 %collective-permute-done.2 = bf16[64,4096]{1,0:T(8,128)(2,1)S(1)} collective-permute-done((bf16[64,4096]{1,0:T(8,128)(2,1)S(1)}, bf16[64,4096]{1,0:T(8,128)(2,1)S(1)}, u32[]{:S(2)}, u32[]{:S(2)}) %collective-permute-start.2) | collective-permute-done | bytes 524320 | tf_op jit(solution)/shard_map/ppermute | solution.py:186
  51.3 11.7 %collective-permute-done.6.refs_1_.refs_5_.refs_6_ = bf16[272,4096]{1,0:T(8,128)(2,1)} collective-permute-done((bf16[272,4096]{1,0:T(8,128)(2,1)S(1)}, bf16[272,4096]{1,0:T(8,128)(2,1)}, u32[]{:S(2)}, u32[]{:S(2)}) %collective-permute-start.6) | collective-permute-done | bytes 2228256 | tf_op jit(solution)/shard_map/ppermute | solution.py:186
  69.4 11.3 %gate_up.4 = bf16[8,2,32,384]{3,2,1,0:T(8,128)(2,1)} custom-call(s32[2]{0:T(128)} %pad_add_fusion.refs_0_, bf16[272,4096]{1,0:T(8,128)(2,1)} %copy-done, bf16[272,4096]{1,0:T(8,128)(2,1)} %copy-done.3, bf16[272,4096]{1,0:T(8,128)(2,1)} %constant_dynamic-update-slice_fusion.refs_3_.refs_9_.refs_10_, ...), custom_call_target="tpu_custom_call" | custom-call | flops 1 | bytes 1 | tf_op jit(solution)/shard_map/gate_up/pallas_call | solution.py:76
  80.7 11.3 %gate_up.5 = bf16[8,2,32,384]{3,2,1,0:T(8,128)(2,1)} custom-call(s32[2]{0:T(128)} %pad_add_fusion.refs_0_, bf16[272,4096]{1,0:T(8,128)(2,1)} %collective-permute-done.6.refs_1_.refs_5_.refs_6_, bf16[272,4096]{1,0:T(8,128)(2,1)} %collective-permute-done.7.refs_2_.refs_7_.refs_8_, bf16[272,4096]{1,0:T(8,128)(2,1)} %copy-done.2, ...), custom_call_target="tpu_custom_call" | custom-call | flops 1 | bytes 1 | tf_op jit(solution)/shard_map/gate_up/pallas_call | solution.py:76
  97.2 2.9 %collective-permute-start.13 = (bf16[272,4096]{1,0:T(8,128)(2,1)}, bf16[272,4096]{1,0:T(8,128)(2,1)}, u32[]{:S(2)}, u32[]{:S(2)}) collective-permute-start(bf16[272,4096]{1,0:T(8,128)(2,1)} %collective-permute-done.5.refs_3_.refs_9_.refs_10_), channel_id=1, source_target_pairs={{0,24},{4,100},{8,0},{12,108},{16,8},{20,116},{24,16},{28,124},{32... | collective-permute-start | bytes 6684680 | tf_op jit(solution)/shard_map/ppermute | solution.py:262
  101.1 3.2 %collective-permute-done.15.refs_4_.refs_11_.refs_12_ = bf16[272,4096]{1,0:T(8,128)(2,1)} collective-permute-done((bf16[272,4096]{1,0:T(8,128)(2,1)}, bf16[272,4096]{1,0:T(8,128)(2,1)}, u32[]{:S(2)}, u32[]{:S(2)}) %collective-permute-start.15) | collective-permute-done | bytes 2228256 | tf_op jit(solution)/shard_map/ppermute | solution.py:263
  104.3 11.7 %gate_up.6.refs_2_ = bf16[8,2,32,384]{3,2,1,0:T(8,128)(2,1)} custom-call(s32[2]{0:T(128)} %pad_add_fusion.refs_0_, bf16[272,4096]{1,0:T(8,128)(2,1)} %collective-permute-done.4.refs_1_.refs_5_.refs_6_, bf16[272,4096]{1,0:T(8,128)(2,1)} %collective-permute-done.14.refs_2_.refs_7_.refs_8_, bf16[272,4096]{1,0:T(8,128)(2,1)} %collective-permute-done.5.refs_3_.refs_9_.refs_10_, ...), custom_call_target="tpu_custom_call" | custom-call | flops 1 | bytes 1 | tf_op jit(solution)/shard_map/gate_up/pallas_call | solution.py:76
  115.9 9.8 %collective-permute-done.12.refs_1_.refs_5_.refs_6_ = bf16[272,4096]{1,0:T(8,128)(2,1)S(1)} collective-permute-done((bf16[272,4096]{1,0:T(8,128)(2,1)}, bf16[272,4096]{1,0:T(8,128)(2,1)S(1)}, u32[]{:S(2)}, u32[]{:S(2)}) %collective-permute-start.12) | collective-permute-done | bytes 2228256 | tf_op jit(solution)/shard_map/ppermute | solution.py:262
  127.1 2.6 collective-permute-start.22
  129.9 2.4 collective-permute-done.16.refs_2_.refs_7_.refs_8_
  133.6 11.6 %gate_up.7.refs_2_ = bf16[8,2,32,384]{3,2,1,0:T(8,128)(2,1)} custom-call(s32[2]{0:T(128)} %pad_add_fusion.refs_0_, bf16[272,4096]{1,0:T(8,128)(2,1)} %copy-done.1, bf16[272,4096]{1,0:T(8,128)(2,1)} %collective-permute-done.16.refs_2_.refs_7_.refs_8_, bf16[272,4096]{1,0:T(8,128)(2,1)} %collective-permute-done.13.refs_3_.refs_9_.refs_10_, ...), custom_call_target="tpu_custom_call" | custom-call | flops 1 | bytes 1 | tf_op jit(solution)/shard_map/gate_up/pallas_call | solution.py:76
  146.0 2.5 collective-permute-start.19
  149.9 4.3 %collective-permute-done.23.refs_5_ = bf16[8,2,32,384]{3,2,1,0:T(8,128)(2,1)S(1)} collective-permute-done((bf16[8,2,32,384]{3,2,1,0:T(8,128)(2,1)}, bf16[8,2,32,384]{3,2,1,0:T(8,128)(2,1)S(1)}, u32[]{:S(2)}, u32[]{:S(2)}) %collective-permute-start.23) | collective-permute-done | bytes 393248 | tf_op jit(solution)/shard_map/ppermute | solution.py:225
  155.0 9.0 %down.2.refs_7_ = bf16[32,2,32,1024]{3,2,1,0:T(8,128)(2,1)} custom-call(s32[17]{0:T(128)} %add_add_fusion.1.refs_0_, bf16[4,8,2,32,384]{4,3,2,1,0:T(8,128)(2,1)} %bitcast.37, bf16[8,2,32,384]{3,2,1,0:T(8,128)(2,1)} %gate_up.6.refs_2_, bf16[8,2,32,384]{3,2,1,0:T(8,128)(2,1)} %copy-done.6, bf16[8,2,32,384]{3,2,1,0:T(8,128)(2,1)} %copy-done.7, ...), custom_call_target="tpu_custom_call" | custom-call | flops 1 | bytes 1 | tf_op jit(solution)/shard_map/down/pallas_call | solution.py:144
  164.0 13.2 %all-gather.5.cloned.1.call-done = bf16[32,2,32,384]{3,2,1,0:T(8,128)(2,1)} async-done(((bf16[8,2,32,384]{3,2,1,0:T(8,128)(2,1)}), bf16[32,2,32,384]{3,2,1,0:T(8,128)(2,1)}) %all-gather.5.cloned.1.call-update) | async-done | bytes 1572880 | tf_op jit(solution)/shard_map/all_gather | solution.py:277
  178.2 8.9 %down.3 = bf16[32,2,32,1024]{3,2,1,0:T(8,128)(2,1)} custom-call(s32[17]{0:T(128)} %add_add_fusion.refs_0_, bf16[4,8,2,32,384]{4,3,2,1,0:T(8,128)(2,1)} %bitcast.36, bf16[8,2,32,384]{3,2,1,0:T(8,128)(2,1)} %gate_up.7.refs_2_, bf16[8,2,32,384]{3,2,1,0:T(8,128)(2,1)} %copy-done.8, bf16[8,2,32,384]{3,2,1,0:T(8,128)(2,1)} %copy-done.10, ...), custom_call_target="tpu_custom_call", output_to_operand_aliasing={{}: (7, {})} | custom-call | flops 1 | bytes 1 | tf_op jit(solution)/shard_map/down/pallas_call | solution.py:144
  187.2 8.4 %all-to-all-start.1 = ((bf16[32,2,32,1024]{3,2,1,0:T(8,128)(2,1)}), bf16[32,2,32,1024]{3,2,1,0:T(8,128)(2,1)}, u32[]{:S(2)}, u32[]{:S(2)}) async-start(bf16[32,2,32,1024]{3,2,1,0:T(8,128)(2,1)} %down.3), calls=%async_computation.1 | async-start | bytes 8388608 | tf_op jit(solution)/shard_map/all_to_all | solution.py:284
  196.4 52.7 %all-to-all-done.1 = bf16[32,2,32,1024]{3,2,1,0:T(8,128)(2,1)} async-done(((bf16[32,2,32,1024]{3,2,1,0:T(8,128)(2,1)}), bf16[32,2,32,1024]{3,2,1,0:T(8,128)(2,1)}, u32[]{:S(2)}, u32[]{:S(2)}) %all-to-all-start.1) | async-done | bytes 4194336 | tf_op jit(solution)/shard_map/all_to_all | solution.py:284
  249.1 3.5 %fusion.1 = f32[256,1024]{1,0:T(8,128)S(1)} fusion(bf16[2048,1024]{1,0:T(8,128)(2,1)} %bitcast.13, bf16[2048,128]{1,0:T(8,128)(2,1)S(1)} %fusion.7, bf16[2048,128]{1,0:T(8,128)(2,1)S(1)} %fusion.6), kind=kOutput, calls=%fused_computation.9 | convolution fusion | flops 1075838976 | bytes 6291456 | tf_op jit(solution)/shard_map/dot_general | solution.py:287
  (99 shorter events, 37.0 us)
Async XLA Ops:
  9.8 17.8 %collective-permute-start = (bf16[136,4096]{1,0:T(8,128)(2,1)}, bf16[136,4096]{1,0:T(8,128)(2,1)S(1)}, u32[]{:S(2)}, u32[]{:S(2)}) collective-permute-start(bf16[136,4096]{1,0:T(8,128)(2,1)} %pad_maximum_fusion.2), channel_id=1, source_target_pairs={{0,32},{4,12},{8,40},{12,20},{16,48},{20,28},{24,56},{28,4},{32,64... | collective-permute-start | bytes 3342344 | tf_op jit(solution)/shard_map/ppermute | solution.py:186
  11.8 15.8 %collective-permute-start.1 = (bf16[136,4096]{1,0:T(8,128)(2,1)}, bf16[136,4096]{1,0:T(8,128)(2,1)S(1)}, u32[]{:S(2)}, u32[]{:S(2)}) collective-permute-start(bf16[136,4096]{1,0:T(8,128)(2,1)} %pad_maximum_fusion.2), channel_id=1, source_target_pairs={{0,96},{4,28},{8,104},{12,4},{16,112},{20,12},{24,120},{28,20},{32... | collective-permute-start | bytes 3342344 | tf_op jit(solution)/shard_map/ppermute | solution.py:186
  20.8 75.6 %all-to-all-start = ((bf16[4,2,384,1024]{3,2,1,0:T(8,128)(2,1)}), bf16[4,2,384,1024]{3,2,1,0:T(8,128)(2,1)}, u32[]{:S(2)}, u32[]{:S(2)}) async-start(bf16[4,2,384,1024]{3,2,1,0:T(8,128)(2,1)} %pad_maximum_fusion), calls=%async_computation | async-start | bytes 12582912 | tf_op jit(solution)/shard_map/all_to_all | solution.py:259
  26.2 123.7 %all-gather.7.cloned.1.call-start = ((), (), s32[]{:S(2)}) async-start(), calls=%async_computation.3 | async-start | bytes 1966080 | tf_op jit(solution)/shard_map/all_gather | solution.py:277
  28.6 34.4 %collective-permute-start.6 = (bf16[272,4096]{1,0:T(8,128)(2,1)S(1)}, bf16[272,4096]{1,0:T(8,128)(2,1)}, u32[]{:S(2)}, u32[]{:S(2)}) collective-permute-start(bf16[272,4096]{1,0:T(8,128)(2,1)S(1)} %pad_maximum_fusion.1.refs_1_.refs_5_.refs_6_), channel_id=1, source_target_pairs={{0,8},{4,36},{8,16},{12,44},{16,24},{20,52},{24,0},{28,60},{32,40}... | collective-permute-start | bytes 6684680 | tf_op jit(solution)/shard_map/ppermute | solution.py:186
  30.1 33.8 %collective-permute-start.8 = (bf16[272,4096]{1,0:T(8,128)(2,1)S(1)}, bf16[272,4096]{1,0:T(8,128)(2,1)S(1)}, u32[]{:S(2)}, u32[]{:S(2)}) collective-permute-start(bf16[272,4096]{1,0:T(8,128)(2,1)S(1)} %pad_maximum_fusion.1.refs_1_.refs_5_.refs_6_), channel_id=1, source_target_pairs={{0,24},{4,100},{8,0},{12,108},{16,8},{20,116},{24,16},{28,124},{32... | collective-permute-start | bytes 6684680 | tf_op jit(solution)/shard_map/ppermute | solution.py:186
  31.9 33.5 %collective-permute-start.10 = (bf16[272,4096]{1,0:T(8,128)(2,1)S(1)}, bf16[272,4096]{1,0:T(8,128)(2,1)S(1)}, u32[]{:S(2)}, u32[]{:S(2)}) collective-permute-start(bf16[272,4096]{1,0:T(8,128)(2,1)S(1)} %pad_maximum_fusion.1.refs_1_.refs_5_.refs_6_), channel_id=1, source_target_pairs={{0,4},{4,0},{8,12},{12,8},{16,20},{20,16},{24,28},{28,24},{32,36},... | collective-permute-start | bytes 6684680 | tf_op jit(solution)/shard_map/ppermute | solution.py:263
  32.9 16.1 %collective-permute-start.2 = (bf16[64,4096]{1,0:T(8,128)(2,1)S(1)}, bf16[64,4096]{1,0:T(8,128)(2,1)S(1)}, u32[]{:S(2)}, u32[]{:S(2)}) collective-permute-start(bf16[64,4096]{1,0:T(8,128)(2,1)S(1)} %slice.42), channel_id=1, source_target_pairs={{0,32},{4,12},{8,40},{12,20},{16,48},{20,28},{24,56},{28,4},{32,64... | collective-permute-start | bytes 1572872 | tf_op jit(solution)/shard_map/ppermute | solution.py:186
  34.1 16.3 %collective-permute-start.3 = (bf16[72,4096]{1,0:T(8,128)(2,1)S(1)}, bf16[72,4096]{1,0:T(8,128)(2,1)S(1)}, u32[]{:S(2)}, u32[]{:S(2)}) collective-permute-start(bf16[72,4096]{1,0:T(8,128)(2,1)S(1)} %slice.43), channel_id=1, source_target_pairs={{0,96},{4,28},{8,104},{12,4},{16,112},{20,12},{24,120},{28,20},{32... | collective-permute-start | bytes 1769480 | tf_op jit(solution)/shard_map/ppermute | solution.py:186
  51.3 18.1 %collective-permute-start.11 = (bf16[272,4096]{1,0:T(8,128)(2,1)}, bf16[272,4096]{1,0:T(8,128)(2,1)}, u32[]{:S(2)}, u32[]{:S(2)}) collective-permute-start(bf16[272,4096]{1,0:T(8,128)(2,1)} %constant_dynamic-update-slice_fusion.refs_3_.refs_9_.refs_10_), channel_id=1, source_target_pairs={{0,4},{4,0},{8,12},{12,8},{16,20},{20,16},{24,28},{28,24},{32,36},... | collective-permute-start | bytes 6684680 | tf_op jit(solution)/shard_map/ppermute | solution.py:263
  63.0 17.6 %collective-permute-start.7 = (bf16[272,4096]{1,0:T(8,128)(2,1)}, bf16[272,4096]{1,0:T(8,128)(2,1)}, u32[]{:S(2)}, u32[]{:S(2)}) collective-permute-start(bf16[272,4096]{1,0:T(8,128)(2,1)} %collective-permute-done.6.refs_1_.refs_5_.refs_6_), channel_id=1, source_target_pairs={{0,4},{4,0},{8,12},{12,8},{16,20},{20,16},{24,28},{28,24},{32,36},... | collective-permute-start | bytes 6684680 | tf_op jit(solution)/shard_map/ppermute | solution.py:263
  63.9 16.8 %collective-permute-start.9 = (bf16[272,4096]{1,0:T(8,128)(2,1)S(1)}, bf16[272,4096]{1,0:T(8,128)(2,1)}, u32[]{:S(2)}, u32[]{:S(2)}) collective-permute-start(bf16[272,4096]{1,0:T(8,128)(2,1)S(1)} %collective-permute-done.8.refs_3_.refs_9_.refs_10_), channel_id=1, source_target_pairs={{0,4},{4,0},{8,12},{12,8},{16,20},{20,16},{24,28},{28,24},{32,36},... | collective-permute-start | bytes 6684680 | tf_op jit(solution)/shard_map/ppermute | solution.py:263
  63.9 29.0 %collective-permute-start.4 = (bf16[272,4096]{1,0:T(8,128)(2,1)}, bf16[272,4096]{1,0:T(8,128)(2,1)}, u32[]{:S(2)}, u32[]{:S(2)}) collective-permute-start(bf16[272,4096]{1,0:T(8,128)(2,1)} %constant_dynamic-update-slice_fusion.refs_3_.refs_9_.refs_10_), channel_id=1, source_target_pairs={{0,8},{4,36},{8,16},{12,44},{16,24},{20,52},{24,0},{28,60},{32,40}... | collective-permute-start | bytes 6684680 | tf_op jit(solution)/shard_map/ppermute | solution.py:186
  66.7 27.8 %collective-permute-start.5 = (bf16[272,4096]{1,0:T(8,128)(2,1)}, bf16[272,4096]{1,0:T(8,128)(2,1)}, u32[]{:S(2)}, u32[]{:S(2)}) collective-permute-start(bf16[272,4096]{1,0:T(8,128)(2,1)} %constant_dynamic-update-slice_fusion.refs_3_.refs_9_.refs_10_), channel_id=1, source_target_pairs={{0,24},{4,100},{8,0},{12,108},{16,8},{20,116},{24,16},{28,124},{32... | collective-permute-start | bytes 6684680 | tf_op jit(solution)/shard_map/ppermute | solution.py:186
  96.9 28.9 %collective-permute-start.12 = (bf16[272,4096]{1,0:T(8,128)(2,1)}, bf16[272,4096]{1,0:T(8,128)(2,1)S(1)}, u32[]{:S(2)}, u32[]{:S(2)}) collective-permute-start(bf16[272,4096]{1,0:T(8,128)(2,1)} %collective-permute-done.6.refs_1_.refs_5_.refs_6_), channel_id=1, source_target_pairs={{0,8},{4,36},{8,16},{12,44},{16,24},{20,52},{24,0},{28,60},{32,40}... | collective-permute-start | bytes 6684680 | tf_op jit(solution)/shard_map/ppermute | solution.py:262
  97.2 28.5 %collective-permute-start.13 = (bf16[272,4096]{1,0:T(8,128)(2,1)}, bf16[272,4096]{1,0:T(8,128)(2,1)}, u32[]{:S(2)}, u32[]{:S(2)}) collective-permute-start(bf16[272,4096]{1,0:T(8,128)(2,1)} %collective-permute-done.5.refs_3_.refs_9_.refs_10_), channel_id=1, source_target_pairs={{0,24},{4,100},{8,0},{12,108},{16,8},{20,116},{24,16},{28,124},{32... | collective-permute-start | bytes 6684680 | tf_op jit(solution)/shard_map/ppermute | solution.py:262
  100.2 77.0 %all-gather.5.cloned.1.call-start = ((), (), s32[]{:S(2)}) async-start(), calls=%async_computation.2 | async-start | bytes 1966080 | tf_op jit(solution)/shard_map/all_gather | solution.py:277
  126.3 22.2 %collective-permute-start.21 = (bf16[8,2,32,384]{3,2,1,0:T(8,128)(2,1)}, bf16[8,2,32,384]{3,2,1,0:T(8,128)(2,1)S(1)}, u32[]{:S(2)}, u32[]{:S(2)}) collective-permute-start(bf16[8,2,32,384]{3,2,1,0:T(8,128)(2,1)} %gate_up.6.refs_2_), channel_id=1, source_target_pairs={{0,1},{1,2},{2,3},{3,0},{4,5},{5,6},{6,7},{7,4},{8,9},{9,10},{10,1... | collective-permute-start | bytes 1179656 | tf_op jit(solution)/shard_map/ppermute | solution.py:225
  127.1 22.8 %collective-permute-start.22 = (bf16[8,2,32,384]{3,2,1,0:T(8,128)(2,1)}, bf16[8,2,32,384]{3,2,1,0:T(8,128)(2,1)S(1)}, u32[]{:S(2)}, u32[]{:S(2)}) collective-permute-start(bf16[8,2,32,384]{3,2,1,0:T(8,128)(2,1)} %gate_up.6.refs_2_), channel_id=1, source_target_pairs={{0,3},{1,0},{2,1},{3,2},{4,7},{5,4},{6,5},{7,6},{8,11},{9,8},{10,9... | collective-permute-start | bytes 1179656 | tf_op jit(solution)/shard_map/ppermute | solution.py:225
  129.7 24.5 %collective-permute-start.23 = (bf16[8,2,32,384]{3,2,1,0:T(8,128)(2,1)}, bf16[8,2,32,384]{3,2,1,0:T(8,128)(2,1)S(1)}, u32[]{:S(2)}, u32[]{:S(2)}) collective-permute-start(bf16[8,2,32,384]{3,2,1,0:T(8,128)(2,1)} %gate_up.6.refs_2_), channel_id=1, source_target_pairs={{0,2},{1,3},{2,0},{3,1},{4,6},{5,7},{6,4},{7,5},{8,10},{9,11},{10,... | collective-permute-start | bytes 1179656 | tf_op jit(solution)/shard_map/ppermute | solution.py:225
  145.3 31.9 %collective-permute-start.18 = (bf16[8,2,32,384]{3,2,1,0:T(8,128)(2,1)}, bf16[8,2,32,384]{3,2,1,0:T(8,128)(2,1)S(1)}, u32[]{:S(2)}, u32[]{:S(2)}) collective-permute-start(bf16[8,2,32,384]{3,2,1,0:T(8,128)(2,1)} %gate_up.7.refs_2_), channel_id=1, source_target_pairs={{0,1},{1,2},{2,3},{3,0},{4,5},{5,6},{6,7},{7,4},{8,9},{9,10},{10,1... | collective-permute-start | bytes 1179656 | tf_op jit(solution)/shard_map/ppermute | solution.py:225
  146.0 31.3 %collective-permute-start.19 = (bf16[8,2,32,384]{3,2,1,0:T(8,128)(2,1)}, bf16[8,2,32,384]{3,2,1,0:T(8,128)(2,1)S(1)}, u32[]{:S(2)}, u32[]{:S(2)}) collective-permute-start(bf16[8,2,32,384]{3,2,1,0:T(8,128)(2,1)} %gate_up.7.refs_2_), channel_id=1, source_target_pairs={{0,3},{1,0},{2,1},{3,2},{4,7},{5,4},{6,5},{7,6},{8,11},{9,8},{10,9... | collective-permute-start | bytes 1179656 | tf_op jit(solution)/shard_map/ppermute | solution.py:225
  148.5 28.7 %collective-permute-start.20 = (bf16[8,2,32,384]{3,2,1,0:T(8,128)(2,1)}, bf16[8,2,32,384]{3,2,1,0:T(8,128)(2,1)S(1)}, u32[]{:S(2)}, u32[]{:S(2)}) collective-permute-start(bf16[8,2,32,384]{3,2,1,0:T(8,128)(2,1)} %gate_up.7.refs_2_), channel_id=1, source_target_pairs={{0,2},{1,3},{2,0},{3,1},{4,6},{5,7},{6,4},{7,5},{8,10},{9,11},{10,... | collective-permute-start | bytes 1179656 | tf_op jit(solution)/shard_map/ppermute | solution.py:225
  187.2 61.9 %all-to-all-start.1 = ((bf16[32,2,32,1024]{3,2,1,0:T(8,128)(2,1)}), bf16[32,2,32,1024]{3,2,1,0:T(8,128)(2,1)}, u32[]{:S(2)}, u32[]{:S(2)}) async-start(bf16[32,2,32,1024]{3,2,1,0:T(8,128)(2,1)} %down.3), calls=%async_computation.1 | async-start | bytes 8388608 | tf_op jit(solution)/shard_map/all_to_all | solution.py:284
  (21 other events, 180.6 us)
Sparse Core Ops, SparseCore 0:
  100.3 24.6 all-gather.6
  126.6 50.5 all-gather.4
